TPU v7x, 128 devices: a whole 4x4x4 slice. The times are simulated.
128 devices in a mesh: section: 2 (over x_lo), seq: 8 (over y, core), tp: 8 (over z, x_hi).
Axes of the slice: x: 4 (x_hi: 2, x_lo: 2; x = x_hi * 2 + x_lo), y: 4, z: 4, core: 2. Of those that a mesh axis runs over, the one named last changes fastest.
Arguments:
- hidden_image: bfloat16 [2, 1024, 1536], P(None, 'seq'), may hold values from -6 to 6
- hidden_text: bfloat16 [2, 256, 1536], P(None, 'seq'), may hold values from -6 to 6
- latent: float32 [2, 1024, 64], P(None, 'seq'), may hold values from -6 to 6
- timestep: int32 [2], replicated, may hold values from 14 to 27
- text_length: int32 [2], replicated, may hold values from 64 to 154, as said below
- text_keep: int32 [2, 256], replicated, may hold values 0 or 1
- patch_order: int32 [4], replicated, may hold values from 0 to 3, each once
- stale_image_kv: bfloat16 [2, 2, 1024, 2, 1536], P('section', None, 'seq', None, 'tp'), may hold values from -160 to 160
- stale_text_kv: bfloat16 [2, 2, 256, 2, 1536], P('section', None, 'seq', None, 'tp'), may hold values from -6 to 6
- mod_image: float32 [2, 2, 6, 1536], P('section'), may hold values from -3 to 3
- mod_text: float32 [2, 2, 6, 1536], P('section'), may hold values from -3 to 3
- mod_final: float32 [2, 2, 1536], replicated, may hold values from -3 to 3
- qkv_image: bfloat16 [2, 1536, 3, 1536], P('section', None, None, 'tp'), may hold values from -0.15625 to 0.15625
- out_image: bfloat16 [2, 1536, 1536], P('section', 'tp'), may hold values from -0.15625 to 0.15625
- up_image: bfloat16 [2, 1536, 6144], P('section', None, 'tp'), may hold values from -0.15625 to 0.15625
- down_image: bfloat16 [2, 6144, 1536], P('section', 'tp'), may hold values from -0.078125 to 0.078125
- qkv_text: bfloat16 [2, 1536, 3, 1536], P('section', None, None, 'tp'), may hold values from -0.15625 to 0.15625
- out_text: bfloat16 [2, 1536, 1536], P('section', 'tp'), may hold values from -0.15625 to 0.15625
- up_text: bfloat16 [2, 1536, 6144], P('section', None, 'tp'), may hold values from -0.15625 to 0.15625
- down_text: bfloat16 [2, 6144, 1536], P('section', 'tp'), may hold values from -0.078125 to 0.078125
- final_weight: bfloat16 [1536, 64], replicated, may hold values from -0.3125 to 0.3125
Outputs:
- latent_out: float32 [2, 2, 1024, 64], P('section', None, 'seq')
- image_kv_next: bfloat16 [2, 2, 1024, 2, 1536], P('section', None, 'seq', None, 'tp')
- text_kv_next: bfloat16 [2, 2, 256, 2, 1536], P('section', None, 'seq', None, 'tp')
- text_hidden: bfloat16 [2, 2, 256, 1536], P('section', None, 'seq')
Inputs may be any that keep to these rules, and one draw needn't show every extreme that they name: `text_length`: some request has exactly 154 text tokens.
All inputs are finite; a program needn't handle non-finite values.
Results may differ from a plain program's by a relative error of at most 0.023.
Values may be sent and summed in bfloat16 or wider, within the bound.
No kernel may reach another device: no remote copies, remote signals or barrier semaphores. Data moves between devices by JAX's collectives and lax.ppermute only.
A program may use at most 128 MiB of HBM per device.

v0:
```python
import jax
import jax.numpy as jnp
from jax import lax
from jax.experimental import pallas as pl
from jax.experimental.pallas import tpu as pltpu
from jax.sharding import PartitionSpec as P

HD = 64
STEPS = 28
EPSILON = 1e-06
NEGATIVE = -1e30
TIME_SHIFT = 3.0

F32 = jnp.float32
BF16 = jnp.bfloat16

REQ, SLOTS, PT, TQ = 2, 4, 32, 8
ROWS = PT + TQ
CHUNKS = REQ * SLOTS
Z, X = 4, 2
Y, C = 4, 2
LANES = 128
RING = (1, 3, 2)
PIECES = ((0, 0), (0, 1), (1, 0), (1, 1), (3, 0), (3, 1), (2, 0), (2, 1))

VMEM = pl.BlockSpec(memory_space=pltpu.VMEM)
SMEM = pl.BlockSpec(memory_space=pltpu.SMEM)


def call(body, name, in_specs, out_shapes, scratch=()):
    return pl.pallas_call(
        body,
        name=name,
        in_specs=list(in_specs),
        out_specs=[VMEM] * len(out_shapes),
        out_shape=[jax.ShapeDtypeStruct(*each) for each in out_shapes],
        scratch_shapes=list(scratch),
        compiler_params=pltpu.CompilerParams(vmem_limit_bytes=40 * 1024 * 1024),
    )


def along_z(value, step):
    pairs = [(z * X + x, (z + step) % Z * X + x) for z in range(Z) for x in range(X)]
    return lax.ppermute(value, "tp", pairs)


def across_x(value):
    return lax.ppermute(value, "tp", [(i, i ^ 1) for i in range(Z * X)])


def along_y(value, step):
    pairs = [(y * C + c, (y + step) % Y * C + c) for y in range(Y) for c in range(C)]
    return lax.ppermute(value, "seq", pairs)


def across_core(value):
    return lax.ppermute(value, "seq", [(i, i ^ 1) for i in range(Y * C)])


def to_next_section(value, flip):
    size = Z * X
    return lax.ppermute(value, ("section", "tp"), [(i, size + (i ^ flip)) for i in range(size)])


def gathered_seq(value):
    far = {(0, 0): value, (0, 1): across_core(value)}
    for step in RING:
        far[step, 0] = along_y(value, step)
    for step in RING:
        far[step, 1] = across_core(far[step, 0])
    return [far[piece] for piece in PIECES]


def spread_z(pair):
    received = {step: along_z(pair, step) for step in RING}
    return [pair] + [received[step] for step in (1, 2, 3)]


def normed(rows, shift, scale):
    mean_value = jnp.mean(rows, axis=-1, keepdims=True)
    centred = rows - mean_value
    variance = jnp.mean(centred * centred, axis=-1, keepdims=True)
    return centred * lax.rsqrt(variance + EPSILON) * (1.0 + scale) + shift


def mm(left, right):
    return jnp.dot(left, right, preferred_element_type=F32)


def mm_t(left, right):
    return lax.dot_general(left, right, (((1,), (1,)), ((), ())), preferred_element_type=F32)


def project_all(image_rows, text_rows, w_image, w_text, q_image, q_text, kv, kv_text):
    width = q_image.shape[1]
    image = image_rows[...]
    text = text_rows[...].astype(BF16)
    q_image[...] = mm_t(image, w_image[0:width, :]).astype(BF16)
    q_text[...] = mm_t(text, w_text[0:width, :]).astype(BF16).astype(F32)
    keys_values = mm_t(w_image[width:, :], image).astype(BF16)
    text_kv = mm_t(text, w_text[width:, :]).astype(BF16)
    kv_text[...] = text_kv
    span, count = SLOTS * PT, SLOTS * TQ
    for r in range(REQ):
        kv[r, 0 : 2 * width, :] = keys_values[:, r * span : (r + 1) * span]
        for i in range(2 * width // LANES):
            at = 2 * width + i * count
            kv[r, at : at + count, :] = text_kv[
                r * count : (r + 1) * count, i * LANES : (i + 1) * LANES
            ]


def project_first(place, image, text, mod_image, mod_text, *refs):
    weights, outs, own, (image_rows, text_rows) = refs[:2], refs[2:6], refs[6], refs[7:]
    tp = place[2]
    own[0:PT, :] = image[tp]
    own[PT:ROWS, :] = text[tp]
    for r in range(REQ):
        span, count = SLOTS * PT, SLOTS * TQ
        rows = image[r * SLOTS : (r + 1) * SLOTS].astype(F32).reshape(span, image.shape[2])
        image_rows[r * span : (r + 1) * span, :] = normed(
            rows, mod_image[0, r : r + 1], mod_image[1, r : r + 1]
        ).astype(BF16)
        rows = text[r * SLOTS : (r + 1) * SLOTS].astype(F32).reshape(count, text.shape[2])
        text_rows[r * count : (r + 1) * count, :] = normed(
            rows, mod_text[0, r : r + 1], mod_text[1, r : r + 1]
        )
    project_all(image_rows, text_rows, *weights, *outs)


def chunk_at(place, step, flip):
    return (place[0] + Z - step) % Z * X + (place[1] + flip) % X


def project_next(place, p0, p1, p2, p3, mod_image, mod_text, *refs):
    weights, outs, (image_rows, text_rows) = refs[:2], refs[2:6], refs[6:]
    for step, piece in enumerate((p0, p1, p2, p3)):
        for flip in range(X):
            chunk = chunk_at(place, step, flip)
            r = chunk // SLOTS
            image_rows[pl.ds(pl.multiple_of(chunk * PT, PT), PT), :] = normed(
                piece[flip, 0:PT, :].astype(F32),
                mod_image[0, pl.ds(r, 1), :],
                mod_image[1, pl.ds(r, 1), :],
            ).astype(BF16)
            text_rows[pl.ds(pl.multiple_of(chunk * TQ, TQ), TQ), :] = normed(
                piece[flip, PT:ROWS, :].astype(F32),
                mod_text[0, pl.ds(r, 1), :],
                mod_text[1, pl.ds(r, 1), :],
            )
    project_all(image_rows, text_rows, *weights, *outs)


def slot_of(patch, order):
    return sum(jnp.where(patch == order[k], k, 0) for k in range(SLOTS))


def attend(order, bias, q_image, q_text, *refs):
    fresh, stale = refs[0:8], refs[8:16]
    out_image, out_text, out, o_image, o_text = refs[16:]
    width = q_image.shape[1]
    heads = width // HD
    span, count = SLOTS * PT, SLOTS * TQ
    rows = span + count
    image_keys = len(fresh) * span
    key_count = image_keys + len(fresh) * count
    head_of_row = lax.broadcasted_iota(jnp.int32, (rows, width), 1) // HD
    row = lax.broadcasted_iota(jnp.int32, (rows, 1), 0)
    row_slot = jnp.where(row < span, slot_of(row // PT, order), (row - span) // TQ)
    key = lax.broadcasted_iota(jnp.int32, (1, key_count), 1)
    key_slot = jnp.where(
        key < image_keys, slot_of(key % span // PT, order), (key - image_keys) % count // TQ
    )
    is_fresh = key_slot <= row_slot

    def text_of(pieces, r):
        return jnp.concatenate(
            [
                jnp.concatenate(
                    [
                        piece[r, 2 * width + i * count : 2 * width + (i + 1) * count, :]
                        for i in range(2 * width // LANES)
                    ],
                    axis=1,
                )
                for piece in pieces
            ],
            axis=0,
        )

    def scores_of(queries, pieces, text, r):
        keys = jnp.concatenate([piece[r, 0:width, :] for piece in pieces], axis=1)
        return jnp.concatenate([mm(queries, keys), mm_t(queries, text[:, 0:width])], axis=1)

    def summed_of(weights, pieces, text, r):
        values = jnp.concatenate([piece[r, width : 2 * width, :] for piece in pieces], axis=1)
        return mm_t(weights[:, 0:image_keys], values) + mm(
            weights[:, image_keys:], text[:, width:]
        )

    for r in range(REQ):
        q = jnp.concatenate(
            [
                q_image[r * span : (r + 1) * span, :].astype(F32),
                q_text[r * count : (r + 1) * count, :],
            ],
            axis=0,
        )
        fresh_text, stale_text = text_of(fresh, r), text_of(stale, r)
        merged = jnp.zeros((rows, width), F32)
        for h in range(heads):
            queries = jnp.where(head_of_row == h, q, 0.0).astype(BF16)
            scores = jnp.where(
                is_fresh,
                scores_of(queries, fresh, fresh_text, r),
                scores_of(queries, stale, stale_text, r),
            ) * HD ** (-0.5)
            scores = scores + bias[r : r + 1, :]
            top = jnp.max(scores, axis=-1, keepdims=True)
            weights = jnp.exp(scores - top)
            total = jnp.sum(weights, axis=-1, keepdims=True)
            summed = summed_of(
                jnp.where(is_fresh, weights, 0.0).astype(BF16), fresh, fresh_text, r
            ) + summed_of(jnp.where(is_fresh, 0.0, weights).astype(BF16), stale, stale_text, r)
            merged = jnp.where(head_of_row == h, summed / total, merged)
        o_image[r * span : (r + 1) * span, :] = merged[0:span].astype(BF16)
        o_text[r * count : (r + 1) * count, :] = merged[span:].astype(BF16)
    d_model = out.shape[2]
    image = mm(o_image[...], out_image[...])
    text = mm(o_text[...], out_text[...])
    out[:, 0:PT, :] = image.reshape(CHUNKS, PT, d_model).astype(BF16)
    out[:, PT:ROWS, :] = text.reshape(CHUNKS, TQ, d_model).astype(BF16)


def pack_stale(image, text, out):
    width = image.shape[1]
    count = SLOTS * TQ
    for r in range(REQ):
        out[r, 0:width, :] = image[r]
        for i in range(width // LANES):
            out[r, width + i * count : width + (i + 1) * count, :] = text[
                r, :, i * LANES : (i + 1) * LANES
            ]


def own_mod(mod, i, place):
    return mod[i, pl.ds(place[2] // SLOTS, 1), :]


def summed_chunks(received):
    total = received[0].astype(F32)
    for i in range(1, CHUNKS):
        total = total + received[i].astype(F32)
    return total


def after_attention(place, rows, received, mod_image, mod_text, h1, b):
    summed = summed_chunks(received)
    for low, high, mod in ((0, PT, mod_image), (PT, ROWS, mod_text)):
        first = rows[low:high, :].astype(F32) + own_mod(mod, 2, place) * summed[low:high]
        h1[low:high, :] = first
        b[low:high, :] = normed(
            first, own_mod(mod, 3, place), own_mod(mod, 4, place)
        ).astype(BF16)


def feed_forward(place, p0, p1, p2, p3, up_image, down_image, up_text, down_text, *refs):
    out, image_rows, text_rows = refs
    d_model = out.shape[2]
    for d, piece in enumerate((p0, p1, p2, p3)):
        for flip in range(X):
            at = d * X + flip
            image_rows[at * PT : (at + 1) * PT, :] = piece[flip, 0:PT, :]
            text_rows[at * TQ : (at + 1) * TQ, :] = piece[flip, PT:ROWS, :].astype(F32)
    hidden = jax.nn.gelu(mm(image_rows[...], up_image[...]), approximate=True).astype(BF16)
    image = mm(hidden, down_image[...])
    hidden = jax.nn.gelu(
        mm(text_rows[...].astype(BF16), up_text[...]), approximate=True
    ).astype(BF16)
    text = mm(hidden, down_text[...])
    for d in range(Z):
        for flip in range(X):
            at = d * X + flip
            chunk = chunk_at(place, d, flip)
            out[chunk, 0:PT, :] = image[at * PT : (at + 1) * PT].astype(BF16)
            out[chunk, PT:ROWS, :] = text[at * TQ : (at + 1) * TQ].astype(BF16)


def layer_rows(place, h1, received, mod_image, mod_text):
    summed = summed_chunks(received)
    image = (h1[0:PT, :] + own_mod(mod_image, 5, place) * summed[0:PT]).astype(BF16)
    text = (h1[PT:ROWS, :] + own_mod(mod_text, 5, place) * summed[PT:ROWS]).astype(BF16)
    return image, text


def after_mlp(place, h1, received, mod_image, mod_text, y):
    image, text = layer_rows(place, h1, received, mod_image, mod_text)
    y[0:PT, :] = image
    y[PT:ROWS, :] = text


def last_rows(place, h1, received, mod_image, mod_text, mod_final, weight, first, out):
    image, text = layer_rows(place, h1, received, mod_image, mod_text)
    r = place[2] // SLOTS
    rows = normed(
        image.astype(F32), mod_final[pl.ds(r, 1), 0, :], mod_final[pl.ds(r, 1), 1, :]
    ).astype(BF16)
    velocity = mm_t(weight[...], rows)
    width = text.shape[-1]
    text = jnp.where(place[3] == 0, first[PT:ROWS, :].astype(F32), text.astype(F32))
    out[:, 0:width] = text.astype(BF16)
    out[:, width:] = jnp.concatenate(
        [velocity[i * TQ : (i + 1) * TQ] for i in range(velocity.shape[0] // TQ)], axis=1
    ).astype(BF16)


def outputs(place, factor, received, latent, latent_out, text_out):
    width = text_out.shape[-1]
    count = place[3] * CHUNKS
    for chunk in range(CHUNKS):
        text_out[chunk] = received[count + chunk, :, 0:width]
    for r in range(REQ):
        rows = [
            received[CHUNKS + r * SLOTS + p, :, width:].astype(F32) for p in range(SLOTS)
        ]
        for i in range(latent.shape[1] // TQ):
            velocity = jnp.concatenate([each[:, i * PT : (i + 1) * PT] for each in rows], axis=1)
            at = slice(i * TQ, (i + 1) * TQ)
            latent_out[r, at, :] = latent[r, at, :] + factor[r] * velocity


def sigma_of(index_value):
    progress = 1.0 - index_value / STEPS
    return TIME_SHIFT * progress / (1.0 + (TIME_SHIFT - 1.0) * progress)


def on_device(
    hidden_image,
    hidden_text,
    latent,
    timestep,
    text_length,
    text_keep,
    patch_order,
    stale_image_kv,
    stale_text_kv,
    mod_image,
    mod_text,
    mod_final,
    qkv_image,
    out_image,
    up_image,
    down_image,
    qkv_text,
    out_text,
    up_text,
    down_text,
    final_weight,
):
    d_model = hidden_image.shape[2]
    width = qkv_image.shape[3]
    channels = latent.shape[2]
    section = lax.axis_index("section")
    tp = lax.axis_index("tp")
    seq = lax.axis_index("seq")
    place = jnp.stack([tp // X, tp % X, tp, section]).astype(jnp.int32)
    span, count = SLOTS * PT, SLOTS * TQ
    packed_rows = 2 * width + count * 2 * width // LANES
    packed = ((REQ, packed_rows, LANES), BF16)

    stale_image = jnp.transpose(stale_image_kv[0], (0, 2, 3, 1)).reshape(REQ, 2 * width, span)
    stale_text = stale_text_kv[0].reshape(REQ, count, 2 * width)
    (stale,) = call(pack_stale, "pack_stale", [VMEM] * 2, [packed])(stale_image, stale_text)
    stale_pieces = gathered_seq(stale)

    positions = jnp.arange(text_keep.shape[1], dtype=jnp.int32)
    valid = (positions[None, :] < text_length[:, None]) & (text_keep == 1)
    text_bias = jnp.where(valid, 0.0, NEGATIVE).astype(F32).reshape(REQ, Y * C, count)
    piece_seq = [(seq // C + Y - step) % Y * C + (seq + flip) % C for step, flip in PIECES]
    text_bias = jnp.concatenate(
        [lax.dynamic_index_in_dim(text_bias, each, 1, keepdims=False) for each in piece_seq], axis=1
    )
    bias = jnp.concatenate([jnp.zeros((REQ, Y * C * span), F32), text_bias], axis=1)

    def flat_qkv(weight):
        return jnp.transpose(weight[0], (1, 2, 0)).reshape(3 * width, d_model)

    weights = flat_qkv(qkv_image), flat_qkv(qkv_text)
    mods = jnp.transpose(mod_image[0], (1, 0, 2)), jnp.transpose(mod_text[0], (1, 0, 2))

    qkv_shapes = [
        ((CHUNKS * PT, width), BF16),
        ((CHUNKS * TQ, width), F32),
        packed,
        ((CHUNKS * TQ, 2 * width), BF16),
    ]
    rows_scratch = [
        pltpu.VMEM((CHUNKS * PT, d_model), BF16),
        pltpu.VMEM((CHUNKS * TQ, d_model), F32),
    ]
    chunks = ((CHUNKS, ROWS, d_model), BF16)
    row_f32, row_bf16 = ((ROWS, d_model), F32), ((ROWS, d_model), BF16)

    def exchanged(value):
        return lax.all_to_all(value, "tp", 0, 0, tiled=True)

    def rest_of_layer(q_image, q_text, kv, rows):
        (partial,) = call(
            attend,
            "attend",
            [SMEM] + [VMEM] * 21,
            [chunks],
            [pltpu.VMEM((CHUNKS * PT, width), BF16), pltpu.VMEM((CHUNKS * TQ, width), BF16)],
        )(
            patch_order,
            bias,
            q_image,
            q_text,
            *gathered_seq(kv),
            *stale_pieces,
            out_image[0],
            out_text[0],
        )
        h1, b = call(
            after_attention, "after_attention", [SMEM] + [VMEM] * 4, [row_f32, row_bf16]
        )(place, rows, exchanged(partial), *mods)
        pieces = spread_z(jnp.stack([b, across_x(b)]))
        (partial,) = call(
            feed_forward, "feed_forward", [SMEM] + [VMEM] * 8, [chunks], rows_scratch
        )(place, *pieces, up_image[0], down_image[0], up_text[0], down_text[0])
        return h1, exchanged(partial)

    q_image, q_text, kv_first, kv_text_first, own_rows = call(
        project_first, "project_first", [SMEM] + [VMEM] * 6, qkv_shapes + [row_bf16], rows_scratch
    )(
        place,
        hidden_image.reshape(CHUNKS, PT, d_model),
        hidden_text.reshape(CHUNKS, TQ, d_model),
        *mods,
        *weights,
    )
    h1, received = rest_of_layer(q_image, q_text, kv_first, own_rows)
    (y_first,) = call(after_mlp, "after_mlp", [SMEM] + [VMEM] * 4, [row_bf16])(
        place, h1, received, *mods
    )
    arrived = to_next_section(y_first, 0)
    pieces = spread_z(jnp.stack([arrived, to_next_section(y_first, 1)]))
    q_image, q_text, kv_next, kv_text_next = call(
        project_next, "project_next", [SMEM] + [VMEM] * 8, qkv_shapes, rows_scratch
    )(place, *pieces, *mods, *weights)
    h1, received = rest_of_layer(q_image, q_text, kv_next, arrived)
    tail = ((TQ, d_model + PT * channels // TQ), BF16)
    (tail_rows,) = call(last_rows, "last_rows", [SMEM] + [VMEM] * 7, [tail])(
        place, h1, received, *mods, mod_final, jnp.transpose(final_weight), y_first
    )
    shared = lax.all_to_all(
        jnp.broadcast_to(tail_rows[None], (2 * CHUNKS,) + tail_rows.shape),
        ("section", "tp"),
        0,
        0,
        tiled=True,
    )
    index_value = timestep.astype(F32)
    sigma_now = sigma_of(index_value)
    sigma_next = sigma_of(index_value + 1.0)
    factor = jnp.where(section == 0, sigma_next - sigma_now, -sigma_now)
    latent_part, text_hidden = call(
        outputs,
        "outputs",
        [SMEM] * 2 + [VMEM] * 2,
        [((REQ, channels, span), F32), ((CHUNKS, TQ, d_model), BF16)],
    )(place, factor, shared, jnp.transpose(latent, (0, 2, 1)))
    image_kv = jnp.where(section == 0, kv_first[:, : 2 * width], kv_next[:, : 2 * width])
    text_kv = jnp.where(section == 0, kv_text_first, kv_text_next)
    return (
        jnp.transpose(latent_part, (0, 2, 1))[None],
        jnp.transpose(image_kv.reshape(REQ, 2, width, span), (0, 3, 1, 2))[None],
        text_kv.reshape(1, REQ, count, 2, width),
        text_hidden.reshape(1, REQ, count, d_model),
    )


def solution(mesh):
    in_specs = (
        P(None, "seq", None),
        P(None, "seq", None),
        P(None, "seq", None),
        P(),
        P(),
        P(),
        P(),
        P("section", None, "seq", None, "tp"),
        P("section", None, "seq", None, "tp"),
        P("section", None, None, None),
        P("section", None, None, None),
        P(),
        P("section", None, None, "tp"),
        P("section", "tp", None),
        P("section", None, "tp"),
        P("section", "tp", None),
        P("section", None, None, "tp"),
        P("section", "tp", None),
        P("section", None, "tp"),
        P("section", "tp", None),
        P(),
    )
    out_specs = (
        P("section", None, "seq", None),
        P("section", None, "seq", None, "tp"),
        P("section", None, "seq", None, "tp"),
        P("section", None, "seq", None),
    )
    return jax.shard_map(
        on_device, mesh=mesh, in_specs=in_specs, out_specs=out_specs, check_vma=False
    )
```

profile of v0, /device:TPU:0, one launch (start us, length us, event | category | flops | bytes accessed | tf_op | source)
XLA Modules:
  0.0 238.6 jit_solution(13114733667390111448)
XLA Ops:
  2.5 3.4 %collective-permute-start.12 = (bf16[2,480,128]{2,1,0:T(8,128)(2,1)S(1)}, bf16[2,480,128]{2,1,0:T(8,128)(2,1)S(1)}, u32[]{:S(2)}, u32[]{:S(2)}) collective-permute-start(bf16[2,480,128]{2,1,0:T(8,128)(2,1)S(1)} %pack_stale.1.refs_8_), channel_id=1, source_target_pairs={{0,32},{8,40},{16,48},{24,56},{32,0},{40,8},{48,16},{56,24},{1,33}... | collective-permute-start | bytes 737288 | tf_op jit(solution)/shard_map/ppermute | solution.py:53
  19.0 2.6 %collective-permute-start.3 = (bf16[2,480,128]{2,1,0:T(8,128)(2,1)S(1)}, bf16[2,480,128]{2,1,0:T(8,128)(2,1)}, u32[]{:S(2)}, u32[]{:S(2)}) collective-permute-start(bf16[2,480,128]{2,1,0:T(8,128)(2,1)S(1)} %get-tuple-element.22.refs_0_), channel_id=1, source_target_pairs={{0,48},{8,56},{16,0},{24,8},{32,16},{40,24},{48,32},{56,40},{1,49}... | collective-permute-start | bytes 737288 | tf_op jit(solution)/shard_map/ppermute | solution.py:53
  22.2 6.4 %collective-permute-done.5.refs_6_ = bf16[2,480,128]{2,1,0:T(8,128)(2,1)} collective-permute-done((bf16[2,480,128]{2,1,0:T(8,128)(2,1)S(1)}, bf16[2,480,128]{2,1,0:T(8,128)(2,1)}, u32[]{:S(2)}, u32[]{:S(2)}) %collective-permute-start.5) | collective-permute-done | bytes 245792 | tf_op jit(solution)/shard_map/ppermute | solution.py:53
  28.6 4.5 %collective-permute-done.3.refs_4_ = bf16[2,480,128]{2,1,0:T(8,128)(2,1)} collective-permute-done((bf16[2,480,128]{2,1,0:T(8,128)(2,1)S(1)}, bf16[2,480,128]{2,1,0:T(8,128)(2,1)}, u32[]{:S(2)}, u32[]{:S(2)}) %collective-permute-start.3) | collective-permute-done | bytes 245792 | tf_op jit(solution)/shard_map/ppermute | solution.py:53
  37.9 6.9 %attend.2 = bf16[8,40,1536]{2,1,0:T(8,128)(2,1)S(1)} custom-call(s32[4]{0:T(128)S(1)} %copy-done.33, f32[2,1280]{1,0:T(2,128)S(1)} %concatenate.3.bias, bf16[256,192]{1,0:T(8,128)(2,1)S(1)} %copy-done.26, f32[64,192]{1,0:T(8,128)S(1)} %get-tuple-element.21.q_text, bf16[2,480,128]{2,1,0:T(8,128)(2,1)S(1)} %copy-done.15, ...), custom_call_target="tpu_custom_call" | custom-call | tf_op jit(solution)/shard_map/attend/pallas_call | solution.py:408
  44.8 24.6 %all_to_all.25.received = bf16[8,40,1536]{2,1,0:T(8,128)(2,1)S(1)} all-to-all(bf16[8,40,1536]{2,1,0:T(8,128)(2,1)S(1)} %attend.2), channel_id=1, replica_groups=mesh['section'=2,'seq'=8,'tp'=8] {'tp'}, dimensions={0} | all-to-all | bytes 1966080 | tf_op jit(solution)/shard_map/all_to_all | solution.py:405
  71.2 5.6 %collective-permute-done.14 = bf16[40,1536]{1,0:T(8,128)(2,1)S(1)} collective-permute-done((bf16[40,1536]{1,0:T(8,128)(2,1)S(1)}, bf16[40,1536]{1,0:T(8,128)(2,1)S(1)}, u32[]{:S(2)}, u32[]{:S(2)}) %collective-permute-start.14) | collective-permute-done | bytes 122912 | tf_op jit(solution)/shard_map/ppermute | solution.py:48
  79.6 5.7 %collective-permute-done.17.p3 = bf16[2,40,1536]{2,1,0:T(8,128)(2,1)S(1)} collective-permute-done((bf16[2,40,1536]{2,1,0:T(8,128)(2,1)S(1)}, bf16[2,40,1536]{2,1,0:T(8,128)(2,1)S(1)}, u32[]{:S(2)}, u32[]{:S(2)}) %collective-permute-start.17) | collective-permute-done | bytes 245792 | tf_op jit(solution)/shard_map/ppermute | solution.py:44
  87.5 2.5 %collective-permute-done.15.p1 = bf16[2,40,1536]{2,1,0:T(8,128)(2,1)S(1)} collective-permute-done((bf16[2,40,1536]{2,1,0:T(8,128)(2,1)S(1)}, bf16[2,40,1536]{2,1,0:T(8,128)(2,1)S(1)}, u32[]{:S(2)}, u32[]{:S(2)}) %collective-permute-start.15) | collective-permute-done | bytes 245792 | tf_op jit(solution)/shard_map/ppermute | solution.py:44
  90.1 3.2 %feed_forward.2 = bf16[8,40,1536]{2,1,0:T(8,128)(2,1)S(1)} custom-call(s32[4]{0:T(128)S(1)} %pad_add_fusion.place, bf16[2,40,1536]{2,1,0:T(8,128)(2,1)S(1)} %pad_maximum_fusion.p0, bf16[2,40,1536]{2,1,0:T(8,128)(2,1)S(1)} %collective-permute-done.15.p1, bf16[2,40,1536]{2,1,0:T(8,128)(2,1)S(1)} %collective-permute-done.16.p2, ...), custom_call_target="tpu_custom_call" | custom-call | tf_op jit(solution)/shard_map/feed_forward/pallas_call | solution.py:428
  93.3 20.0 %all_to_all.26.received = bf16[8,40,1536]{2,1,0:T(8,128)(2,1)S(1)} all-to-all(bf16[8,40,1536]{2,1,0:T(8,128)(2,1)S(1)} %feed_forward.2), channel_id=1, replica_groups=mesh['section'=2,'seq'=8,'tp'=8] {'tp'}, dimensions={0} | all-to-all | bytes 1966080 | tf_op jit(solution)/shard_map/all_to_all | solution.py:405
  122.9 5.2 %collective-permute-done.22.p3 = bf16[2,40,1536]{2,1,0:T(8,128)(2,1)S(1)} collective-permute-done((bf16[2,40,1536]{2,1,0:T(8,128)(2,1)S(1)}, bf16[2,40,1536]{2,1,0:T(8,128)(2,1)S(1)}, u32[]{:S(2)}, u32[]{:S(2)}) %collective-permute-start.22) | collective-permute-done | bytes 245792 | tf_op jit(solution)/shard_map/ppermute | solution.py:44
  128.1 2.7 %collective-permute-done.21.p2 = bf16[2,40,1536]{2,1,0:T(8,128)(2,1)S(1)} collective-permute-done((bf16[2,40,1536]{2,1,0:T(8,128)(2,1)S(1)}, bf16[2,40,1536]{2,1,0:T(8,128)(2,1)S(1)}, u32[]{:S(2)}, u32[]{:S(2)}) %collective-permute-start.21) | collective-permute-done | bytes 245792 | tf_op jit(solution)/shard_map/ppermute | solution.py:44
  130.8 2.6 %collective-permute-done.20.p1 = bf16[2,40,1536]{2,1,0:T(8,128)(2,1)S(1)} collective-permute-done((bf16[2,40,1536]{2,1,0:T(8,128)(2,1)S(1)}, bf16[2,40,1536]{2,1,0:T(8,128)(2,1)S(1)}, u32[]{:S(2)}, u32[]{:S(2)}) %collective-permute-start.20) | collective-permute-done | bytes 245792 | tf_op jit(solution)/shard_map/ppermute | solution.py:44
  139.6 6.7 %collective-permute-done.28.refs_6_ = bf16[2,480,128]{2,1,0:T(8,128)(2,1)S(1)} collective-permute-done((bf16[2,480,128]{2,1,0:T(8,128)(2,1)S(1)}, bf16[2,480,128]{2,1,0:T(8,128)(2,1)S(1)}, u32[]{:S(2)}, u32[]{:S(2)}) %collective-permute-start.28) | collective-permute-done | bytes 245792 | tf_op jit(solution)/shard_map/ppermute | solution.py:53
  150.7 5.8 %attend.3 = bf16[8,40,1536]{2,1,0:T(8,128)(2,1)S(1)} custom-call(s32[4]{0:T(128)S(1)} %copy-done.33, f32[2,1280]{1,0:T(2,128)S(1)} %concatenate.3.bias, bf16[256,192]{1,0:T(8,128)(2,1)S(1)} %get-tuple-element.25.q_image, f32[64,192]{1,0:T(8,128)S(1)} %get-tuple-element.26.q_text, bf16[2,480,128]{2,1,0:T(8,128)(2,1)S(1)} %get-tuple-element.27.refs_0_, ...), custom_call_target="tpu_custom_call" | custom-call | tf_op jit(solution)/shard_map/attend/pallas_call | solution.py:408
  156.4 20.2 %all_to_all.27.received = bf16[8,40,1536]{2,1,0:T(8,128)(2,1)S(1)} all-to-all(bf16[8,40,1536]{2,1,0:T(8,128)(2,1)S(1)} %attend.3), channel_id=1, replica_groups=mesh['section'=2,'seq'=8,'tp'=8] {'tp'}, dimensions={0} | all-to-all | bytes 1966080 | tf_op jit(solution)/shard_map/all_to_all | solution.py:405
  178.5 5.6 %collective-permute-done.30 = bf16[40,1536]{1,0:T(8,128)(2,1)S(1)} collective-permute-done((bf16[40,1536]{1,0:T(8,128)(2,1)S(1)}, bf16[40,1536]{1,0:T(8,128)(2,1)S(1)}, u32[]{:S(2)}, u32[]{:S(2)}) %collective-permute-start.30) | collective-permute-done | bytes 122912 | tf_op jit(solution)/shard_map/ppermute | solution.py:48
  186.8 5.7 %collective-permute-done.33.p3 = bf16[2,40,1536]{2,1,0:T(8,128)(2,1)S(1)} collective-permute-done((bf16[2,40,1536]{2,1,0:T(8,128)(2,1)S(1)}, bf16[2,40,1536]{2,1,0:T(8,128)(2,1)S(1)}, u32[]{:S(2)}, u32[]{:S(2)}) %collective-permute-start.33) | collective-permute-done | bytes 245792 | tf_op jit(solution)/shard_map/ppermute | solution.py:44
  197.2 4.1 %feed_forward.3 = bf16[8,40,1536]{2,1,0:T(8,128)(2,1)} custom-call(s32[4]{0:T(128)S(1)} %pad_add_fusion.place, bf16[2,40,1536]{2,1,0:T(8,128)(2,1)S(1)} %pad_maximum_fusion.2.p0, bf16[2,40,1536]{2,1,0:T(8,128)(2,1)S(1)} %collective-permute-done.31.p1, bf16[2,40,1536]{2,1,0:T(8,128)(2,1)S(1)} %collective-permute-done.32.p2, ...), custom_call_target="tpu_custom_call" | custom-call | tf_op jit(solution)/shard_map/feed_forward/pallas_call | solution.py:428
  201.4 3.9 %all-to-all-start.3 = ((bf16[8,40,1536]{2,1,0:T(8,128)(2,1)}), bf16[8,40,1536]{2,1,0:T(8,128)(2,1)S(1)}, u32[]{:S(2)}, u32[]{:S(2)}) async-start(bf16[8,40,1536]{2,1,0:T(8,128)(2,1)} %feed_forward.3), calls=%async_computation.3 | async-start | bytes 1966080 | tf_op jit(solution)/shard_map/all_to_all | solution.py:405
  205.3 16.0 %all-to-all-done.3.received = bf16[8,40,1536]{2,1,0:T(8,128)(2,1)S(1)} async-done(((bf16[8,40,1536]{2,1,0:T(8,128)(2,1)}), bf16[8,40,1536]{2,1,0:T(8,128)(2,1)S(1)}, u32[]{:S(2)}, u32[]{:S(2)}) %all-to-all-start.3) | async-done | bytes 983072 | tf_op jit(solution)/shard_map/all_to_all | solution.py:405
  223.3 3.9 %all-to-all-start.4 = ((bf16[16,8,1792]{2,1,0:T(8,128)(2,1)}), bf16[16,8,1792]{2,1,0:T(8,128)(2,1)S(1)}, u32[]{:S(2)}, u32[]{:S(2)}) async-start(bf16[16,8,1792]{2,1,0:T(8,128)(2,1)} %broadcast_in_dim.28), calls=%async_computation.4 | async-start | bytes 917504 | tf_op jit(solution)/shard_map/all_to_all | solution.py:456
  228.7 8.7 %all-to-all-done.4.received = bf16[16,8,1792]{2,1,0:T(8,128)(2,1)S(1)} async-done(((bf16[16,8,1792]{2,1,0:T(8,128)(2,1)}), bf16[16,8,1792]{2,1,0:T(8,128)(2,1)S(1)}, u32[]{:S(2)}, u32[]{:S(2)}) %all-to-all-start.4) | async-done | bytes 458784 | tf_op jit(solution)/shard_map/all_to_all | solution.py:456
  (152 shorter events, 61.3 us)
Async XLA Ops:
  2.5 16.4 %collective-permute-start.12 = (bf16[2,480,128]{2,1,0:T(8,128)(2,1)S(1)}, bf16[2,480,128]{2,1,0:T(8,128)(2,1)S(1)}, u32[]{:S(2)}, u32[]{:S(2)}) collective-permute-start(bf16[2,480,128]{2,1,0:T(8,128)(2,1)S(1)} %pack_stale.1.refs_8_), channel_id=1, source_target_pairs={{0,32},{8,40},{16,48},{24,56},{32,0},{40,8},{48,16},{56,24},{1,33}... | collective-permute-start | bytes 737288 | tf_op jit(solution)/shard_map/ppermute | solution.py:53
  5.9 15.7 %collective-permute-start.10 = (bf16[2,480,128]{2,1,0:T(8,128)(2,1)S(1)}, bf16[2,480,128]{2,1,0:T(8,128)(2,1)S(1)}, u32[]{:S(2)}, u32[]{:S(2)}) collective-permute-start(bf16[2,480,128]{2,1,0:T(8,128)(2,1)S(1)} %pack_stale.1.refs_8_), channel_id=1, source_target_pairs={{0,48},{8,56},{16,0},{24,8},{32,16},{40,24},{48,32},{56,40},{1,49}... | collective-permute-start | bytes 737288 | tf_op jit(solution)/shard_map/ppermute | solution.py:53
  6.9 14.6 %collective-permute-start.8 = (bf16[2,480,128]{2,1,0:T(8,128)(2,1)S(1)}, bf16[2,480,128]{2,1,0:T(8,128)(2,1)S(1)}, u32[]{:S(2)}, u32[]{:S(2)}) collective-permute-start(bf16[2,480,128]{2,1,0:T(8,128)(2,1)S(1)} %pack_stale.1.refs_8_), channel_id=1, source_target_pairs={{0,16},{8,24},{16,32},{24,40},{32,48},{40,56},{48,0},{56,8},{1,17}... | collective-permute-start | bytes 737288 | tf_op jit(solution)/shard_map/ppermute | solution.py:53
  7.9 13.8 %collective-permute-start.7 = (bf16[2,480,128]{2,1,0:T(8,128)(2,1)S(1)}, bf16[2,480,128]{2,1,0:T(8,128)(2,1)S(1)}, u32[]{:S(2)}, u32[]{:S(2)}) collective-permute-start(bf16[2,480,128]{2,1,0:T(8,128)(2,1)S(1)} %pack_stale.1.refs_8_), channel_id=1, source_target_pairs={{0,8},{8,0},{16,24},{24,16},{32,40},{40,32},{48,56},{56,48},{1,9},... | collective-permute-start | bytes 737288 | tf_op jit(solution)/shard_map/ppermute | solution.py:57
  18.2 10.4 %collective-permute-start.5 = (bf16[2,480,128]{2,1,0:T(8,128)(2,1)S(1)}, bf16[2,480,128]{2,1,0:T(8,128)(2,1)}, u32[]{:S(2)}, u32[]{:S(2)}) collective-permute-start(bf16[2,480,128]{2,1,0:T(8,128)(2,1)S(1)} %get-tuple-element.22.refs_0_), channel_id=1, source_target_pairs={{0,32},{8,40},{16,48},{24,56},{32,0},{40,8},{48,16},{56,24},{1,33}... | collective-permute-start | bytes 737288 | tf_op jit(solution)/shard_map/ppermute | solution.py:53
  19.0 14.2 %collective-permute-start.3 = (bf16[2,480,128]{2,1,0:T(8,128)(2,1)S(1)}, bf16[2,480,128]{2,1,0:T(8,128)(2,1)}, u32[]{:S(2)}, u32[]{:S(2)}) collective-permute-start(bf16[2,480,128]{2,1,0:T(8,128)(2,1)S(1)} %get-tuple-element.22.refs_0_), channel_id=1, source_target_pairs={{0,48},{8,56},{16,0},{24,8},{32,16},{40,24},{48,32},{56,40},{1,49}... | collective-permute-start | bytes 737288 | tf_op jit(solution)/shard_map/ppermute | solution.py:53
  21.6 11.9 %collective-permute-start.1 = (bf16[2,480,128]{2,1,0:T(8,128)(2,1)S(1)}, bf16[2,480,128]{2,1,0:T(8,128)(2,1)}, u32[]{:S(2)}, u32[]{:S(2)}) collective-permute-start(bf16[2,480,128]{2,1,0:T(8,128)(2,1)S(1)} %get-tuple-element.22.refs_0_), channel_id=1, source_target_pairs={{0,16},{8,24},{16,32},{24,40},{32,48},{40,56},{48,0},{56,8},{1,17}... | collective-permute-start | bytes 737288 | tf_op jit(solution)/shard_map/ppermute | solution.py:53
  21.6 12.0 %collective-permute-start = (bf16[2,480,128]{2,1,0:T(8,128)(2,1)S(1)}, bf16[2,480,128]{2,1,0:T(8,128)(2,1)}, u32[]{:S(2)}, u32[]{:S(2)}) collective-permute-start(bf16[2,480,128]{2,1,0:T(8,128)(2,1)S(1)} %get-tuple-element.22.refs_0_), channel_id=1, source_target_pairs={{0,8},{8,0},{16,24},{24,16},{32,40},{40,32},{48,56},{56,48},{1,9},... | collective-permute-start | bytes 737288 | tf_op jit(solution)/shard_map/ppermute | solution.py:57
  21.7 12.3 %collective-permute-start.13 = (bf16[2,480,128]{2,1,0:T(8,128)(2,1)S(1)}, bf16[2,480,128]{2,1,0:T(8,128)(2,1)S(1)}, u32[]{:S(2)}, u32[]{:S(2)}) collective-permute-start(bf16[2,480,128]{2,1,0:T(8,128)(2,1)S(1)} %collective-permute-done.12.refs_14_), channel_id=1, source_target_pairs={{0,8},{8,0},{16,24},{24,16},{32,40},{40,32},{48,56},{56,48},{1,9},... | collective-permute-start | bytes 737288 | tf_op jit(solution)/shard_map/ppermute | solution.py:57
  76.8 8.6 %collective-permute-start.17 = (bf16[2,40,1536]{2,1,0:T(8,128)(2,1)S(1)}, bf16[2,40,1536]{2,1,0:T(8,128)(2,1)S(1)}, u32[]{:S(2)}, u32[]{:S(2)}) collective-permute-start(bf16[2,40,1536]{2,1,0:T(8,128)(2,1)S(1)} %pad_maximum_fusion.p0), channel_id=1, source_target_pairs={{0,6},{1,7},{2,0},{3,1},{4,2},{5,3},{6,4},{7,5},{8,14},{9,15},{10,... | collective-permute-start | bytes 737288 | tf_op jit(solution)/shard_map/ppermute | solution.py:44
  77.9 9.6 %collective-permute-start.16 = (bf16[2,40,1536]{2,1,0:T(8,128)(2,1)S(1)}, bf16[2,40,1536]{2,1,0:T(8,128)(2,1)S(1)}, u32[]{:S(2)}, u32[]{:S(2)}) collective-permute-start(bf16[2,40,1536]{2,1,0:T(8,128)(2,1)S(1)} %pad_maximum_fusion.p0), channel_id=1, source_target_pairs={{0,4},{1,5},{2,6},{3,7},{4,0},{5,1},{6,2},{7,3},{8,12},{9,13},{10,... | collective-permute-start | bytes 737288 | tf_op jit(solution)/shard_map/ppermute | solution.py:44
  79.4 10.7 %collective-permute-start.15 = (bf16[2,40,1536]{2,1,0:T(8,128)(2,1)S(1)}, bf16[2,40,1536]{2,1,0:T(8,128)(2,1)S(1)}, u32[]{:S(2)}, u32[]{:S(2)}) collective-permute-start(bf16[2,40,1536]{2,1,0:T(8,128)(2,1)S(1)} %pad_maximum_fusion.p0), channel_id=1, source_target_pairs={{0,2},{1,3},{2,4},{3,5},{4,6},{5,7},{6,0},{7,1},{8,10},{9,11},{10,... | collective-permute-start | bytes 737288 | tf_op jit(solution)/shard_map/ppermute | solution.py:44
  120.2 7.9 %collective-permute-start.22 = (bf16[2,40,1536]{2,1,0:T(8,128)(2,1)S(1)}, bf16[2,40,1536]{2,1,0:T(8,128)(2,1)S(1)}, u32[]{:S(2)}, u32[]{:S(2)}) collective-permute-start(bf16[2,40,1536]{2,1,0:T(8,128)(2,1)S(1)} %pad_maximum_fusion.1.p0), channel_id=1, source_target_pairs={{0,6},{1,7},{2,0},{3,1},{4,2},{5,3},{6,4},{7,5},{8,14},{9,15},{10,... | collective-permute-start | bytes 737288 | tf_op jit(solution)/shard_map/ppermute | solution.py:44
  121.4 9.3 %collective-permute-start.21 = (bf16[2,40,1536]{2,1,0:T(8,128)(2,1)S(1)}, bf16[2,40,1536]{2,1,0:T(8,128)(2,1)S(1)}, u32[]{:S(2)}, u32[]{:S(2)}) collective-permute-start(bf16[2,40,1536]{2,1,0:T(8,128)(2,1)S(1)} %pad_maximum_fusion.1.p0), channel_id=1, source_target_pairs={{0,4},{1,5},{2,6},{3,7},{4,0},{5,1},{6,2},{7,3},{8,12},{9,13},{10,... | collective-permute-start | bytes 737288 | tf_op jit(solution)/shard_map/ppermute | solution.py:44
  122.9 10.4 %collective-permute-start.20 = (bf16[2,40,1536]{2,1,0:T(8,128)(2,1)S(1)}, bf16[2,40,1536]{2,1,0:T(8,128)(2,1)S(1)}, u32[]{:S(2)}, u32[]{:S(2)}) collective-permute-start(bf16[2,40,1536]{2,1,0:T(8,128)(2,1)S(1)} %pad_maximum_fusion.1.p0), channel_id=1, source_target_pairs={{0,2},{1,3},{2,4},{3,5},{4,6},{5,7},{6,0},{7,1},{8,10},{9,11},{10,... | collective-permute-start | bytes 737288 | tf_op jit(solution)/shard_map/ppermute | solution.py:44
  135.8 10.5 %collective-permute-start.28 = (bf16[2,480,128]{2,1,0:T(8,128)(2,1)S(1)}, bf16[2,480,128]{2,1,0:T(8,128)(2,1)S(1)}, u32[]{:S(2)}, u32[]{:S(2)}) collective-permute-start(bf16[2,480,128]{2,1,0:T(8,128)(2,1)S(1)} %get-tuple-element.27.refs_0_), channel_id=1, source_target_pairs={{0,32},{8,40},{16,48},{24,56},{32,0},{40,8},{48,16},{56,24},{1,33}... | collective-permute-start | bytes 737288 | tf_op jit(solution)/shard_map/ppermute | solution.py:53
  137.5 11.3 %collective-permute-start.26 = (bf16[2,480,128]{2,1,0:T(8,128)(2,1)S(1)}, bf16[2,480,128]{2,1,0:T(8,128)(2,1)S(1)}, u32[]{:S(2)}, u32[]{:S(2)}) collective-permute-start(bf16[2,480,128]{2,1,0:T(8,128)(2,1)S(1)} %get-tuple-element.27.refs_0_), channel_id=1, source_target_pairs={{0,48},{8,56},{16,0},{24,8},{32,16},{40,24},{48,32},{56,40},{1,49}... | collective-permute-start | bytes 737288 | tf_op jit(solution)/shard_map/ppermute | solution.py:53
  139.5 9.4 %collective-permute-start.24 = (bf16[2,480,128]{2,1,0:T(8,128)(2,1)S(1)}, bf16[2,480,128]{2,1,0:T(8,128)(2,1)S(1)}, u32[]{:S(2)}, u32[]{:S(2)}) collective-permute-start(bf16[2,480,128]{2,1,0:T(8,128)(2,1)S(1)} %get-tuple-element.27.refs_0_), channel_id=1, source_target_pairs={{0,16},{8,24},{16,32},{24,40},{32,48},{40,56},{48,0},{56,8},{1,17}... | collective-permute-start | bytes 737288 | tf_op jit(solution)/shard_map/ppermute | solution.py:53
  139.6 9.8 %collective-permute-start.23 = (bf16[2,480,128]{2,1,0:T(8,128)(2,1)S(1)}, bf16[2,480,128]{2,1,0:T(8,128)(2,1)S(1)}, u32[]{:S(2)}, u32[]{:S(2)}) collective-permute-start(bf16[2,480,128]{2,1,0:T(8,128)(2,1)S(1)} %get-tuple-element.27.refs_0_), channel_id=1, source_target_pairs={{0,8},{8,0},{16,24},{24,16},{32,40},{40,32},{48,56},{56,48},{1,9},... | collective-permute-start | bytes 737288 | tf_op jit(solution)/shard_map/ppermute | solution.py:57
  184.1 8.4 %collective-permute-start.33 = (bf16[2,40,1536]{2,1,0:T(8,128)(2,1)S(1)}, bf16[2,40,1536]{2,1,0:T(8,128)(2,1)S(1)}, u32[]{:S(2)}, u32[]{:S(2)}) collective-permute-start(bf16[2,40,1536]{2,1,0:T(8,128)(2,1)S(1)} %pad_maximum_fusion.2.p0), channel_id=1, source_target_pairs={{0,6},{1,7},{2,0},{3,1},{4,2},{5,3},{6,4},{7,5},{8,14},{9,15},{10,... | collective-permute-start | bytes 737288 | tf_op jit(solution)/shard_map/ppermute | solution.py:44
  185.1 9.6 %collective-permute-start.32 = (bf16[2,40,1536]{2,1,0:T(8,128)(2,1)S(1)}, bf16[2,40,1536]{2,1,0:T(8,128)(2,1)S(1)}, u32[]{:S(2)}, u32[]{:S(2)}) collective-permute-start(bf16[2,40,1536]{2,1,0:T(8,128)(2,1)S(1)} %pad_maximum_fusion.2.p0), channel_id=1, source_target_pairs={{0,4},{1,5},{2,6},{3,7},{4,0},{5,1},{6,2},{7,3},{8,12},{9,13},{10,... | collective-permute-start | bytes 737288 | tf_op jit(solution)/shard_map/ppermute | solution.py:44
  186.5 10.7 %collective-permute-start.31 = (bf16[2,40,1536]{2,1,0:T(8,128)(2,1)S(1)}, bf16[2,40,1536]{2,1,0:T(8,128)(2,1)S(1)}, u32[]{:S(2)}, u32[]{:S(2)}) collective-permute-start(bf16[2,40,1536]{2,1,0:T(8,128)(2,1)S(1)} %pad_maximum_fusion.2.p0), channel_id=1, source_target_pairs={{0,2},{1,3},{2,4},{3,5},{4,6},{5,7},{6,0},{7,1},{8,10},{9,11},{10,... | collective-permute-start | bytes 737288 | tf_op jit(solution)/shard_map/ppermute | solution.py:44
  201.4 20.0 %all-to-all-start.3 = ((bf16[8,40,1536]{2,1,0:T(8,128)(2,1)}), bf16[8,40,1536]{2,1,0:T(8,128)(2,1)S(1)}, u32[]{:S(2)}, u32[]{:S(2)}) async-start(bf16[8,40,1536]{2,1,0:T(8,128)(2,1)} %feed_forward.3), calls=%async_computation.3 | async-start | bytes 1966080 | tf_op jit(solution)/shard_map/all_to_all | solution.py:405
  223.3 14.0 %all-to-all-start.4 = ((bf16[16,8,1792]{2,1,0:T(8,128)(2,1)}), bf16[16,8,1792]{2,1,0:T(8,128)(2,1)S(1)}, u32[]{:S(2)}, u32[]{:S(2)}) async-start(bf16[16,8,1792]{2,1,0:T(8,128)(2,1)} %broadcast_in_dim.28), calls=%async_computation.4 | async-start | bytes 917504 | tf_op jit(solution)/shard_map/all_to_all | solution.py:456
  (49 other events, 855.7 us)
where the time goes:
time: 239 us
  waiting for transfers between devices  91.9 us (38%)
  blocking collectives  64.7 us (27%)
  starting transfers between devices  35.7 us (15%)
  Pallas kernels  29.3 us (12%)
  local copies, waits for them, and re-layouts  14.9 us (6%)
    all_to_all x3, blocking collectives, exchanged(): return lax.all_to_all(value, 'tp', 0, 0, tiled=True)  64.7 us
    ppermute x9, waiting for transfers between devices, along_z(): return lax.ppermute(value, 'tp', pairs)  31.3 us
    ppermute x9, waiting for transfers between devices, along_y(): return lax.ppermute(value, 'seq', pairs)  20.7 us
    all_to_all x1, waiting for transfers between devices, exchanged(): return lax.all_to_all(value, 'tp', 0, 0, tiled=True)  16 us
    pallas_call x2, Pallas kernels, rest_of_layer(): call(attend, 'attend', [SMEM] + [VMEM] * 21, [chunks], [pltpu.VMEM((CHUNK...  12.6 us
    ppermute x9, starting transfers between devices, along_y(): return lax.ppermute(value, 'seq', pairs)  12.5 us
    ppermute x2, waiting for transfers between devices, across_x(): return lax.ppermute(value, 'tp', [(i, i ^ 1) for i in range(Z * X)])  11.1 us
    unnamed x74, local copies, waits for them, and re-layouts  11 us
  transfers between devices with their start and end apart: 36, of which 24 were waited for; matrix products, arithmetic and copies ran while one was open for 1% of the time, Pallas kernels for 1%

commit v1 on v0

--- a/solution.py
+++ b/solution.py
@@ -133,11 +133,14 @@
 
 
 def project_next(place, p0, p1, p2, p3, mod_image, mod_text, *refs):
-    weights, outs, (image_rows, text_rows) = refs[:2], refs[2:6], refs[6:]
+    weights, outs, (image_rows, text_rows) = refs[:2], refs[2:6], refs[8:]
+    image_out, text_out = refs[6:8]
     for step, piece in enumerate((p0, p1, p2, p3)):
         for flip in range(X):
             chunk = chunk_at(place, step, flip)
             r = chunk // SLOTS
+            image_out[chunk] = piece[flip, 0:PT, :]
+            text_out[chunk] = piece[flip, PT:ROWS, :]
             image_rows[pl.ds(pl.multiple_of(chunk * PT, PT), PT), :] = normed(
                 piece[flip, 0:PT, :].astype(F32),
                 mod_image[0, pl.ds(r, 1), :],
@@ -155,9 +158,7 @@
     return sum(jnp.where(patch == order[k], k, 0) for k in range(SLOTS))
 
 
-def attend(order, bias, q_image, q_text, *refs):
-    fresh, stale = refs[0:8], refs[8:16]
-    out_image, out_text, out, o_image, o_text = refs[16:]
+def attended(order, bias, q_image, q_text, fresh, stale):
     width = q_image.shape[1]
     heads = width // HD
     span, count = SLOTS * PT, SLOTS * TQ
@@ -223,13 +224,32 @@
                 jnp.where(is_fresh, weights, 0.0).astype(BF16), fresh, fresh_text, r
             ) + summed_of(jnp.where(is_fresh, 0.0, weights).astype(BF16), stale, stale_text, r)
             merged = jnp.where(head_of_row == h, summed / total, merged)
-        o_image[r * span : (r + 1) * span, :] = merged[0:span].astype(BF16)
-        o_text[r * count : (r + 1) * count, :] = merged[span:].astype(BF16)
+        yield r, merged[0:span].astype(BF16), merged[span:].astype(BF16)
+
+
+def attend_project(order, bias, q_image, q_text, *refs):
+    fresh, stale = refs[0:8], refs[8:16]
+    out_image, out_text, out, o_image, o_text = refs[16:]
+    span, count = SLOTS * PT, SLOTS * TQ
+    for r, image, text in attended(order, bias, q_image, q_text, fresh, stale):
+        o_image[r * span : (r + 1) * span, :] = image
+        o_text[r * count : (r + 1) * count, :] = text
     d_model = out.shape[2]
     image = mm(o_image[...], out_image[...])
     text = mm(o_text[...], out_text[...])
     out[:, 0:PT, :] = image.reshape(CHUNKS, PT, d_model).astype(BF16)
     out[:, PT:ROWS, :] = text.reshape(CHUNKS, TQ, d_model).astype(BF16)
+
+
+def attend_heads(order, bias, q_image, q_text, *refs):
+    fresh, stale, out = refs[0:8], refs[8:16], refs[16]
+    rows = SLOTS * ROWS
+    for r, image, text in attended(order, bias, q_image, q_text, fresh, stale):
+        heads = jnp.concatenate([image, text], axis=0)
+        out[r * rows : (r + 1) * rows, :] = heads[:, 0:LANES]
+        half = heads.shape[1] - LANES
+        at = REQ * rows
+        out[at : at + rows, r * half : (r + 1) * half] = heads[:, LANES:]
 
 
 def pack_stale(image, text, out):
@@ -284,6 +304,58 @@
             chunk = chunk_at(place, d, flip)
             out[chunk, 0:PT, :] = image[at * PT : (at + 1) * PT].astype(BF16)
             out[chunk, PT:ROWS, :] = text[at * TQ : (at + 1) * TQ].astype(BF16)
+
+
+def heads_mlp(place, o0, o1, o2, o3, image, text, w_own, w_other, *refs):
+    up_image, down_image, up_text, down_text, mod_image, mod_text = refs[:6]
+    out, own, o_image, o_text, image_h1, text_h1, image_rows, text_rows = refs[6:]
+    d_model = out.shape[2]
+    span, count, rows = SLOTS * PT, SLOTS * TQ, SLOTS * ROWS
+    for step, piece in enumerate((o0, o1, o2, o3)):
+        from_z = (place[0] + Z - step) % Z
+        low, high = place[1], 1 - place[1]
+        for r in range(REQ):
+            half = LANES // REQ
+            parts = []
+            for source in (low, high):
+                parts.append(piece[source, r * rows : (r + 1) * rows, :])
+                parts.append(
+                    piece[source, REQ * rows : REQ * rows + rows, r * half : (r + 1) * half]
+                )
+            heads = jnp.concatenate(parts, axis=1)
+            lanes = pl.ds(pl.multiple_of(from_z * heads.shape[1], LANES), heads.shape[1])
+            o_image[r * span : (r + 1) * span, lanes] = heads[0:span]
+            o_text[r * count : (r + 1) * count, lanes] = heads[span:]
+
+    def projected(w_image, w_text):
+        image_h1[...] = mm(o_image[...], w_image[...])
+        text_h1[...] = mm(o_text[...], w_text[...])
+
+    @pl.when(place[4] == 0)
+    def _():
+        projected(w_own, w_other)
+
+    @pl.when(place[4] != 0)
+    def _():
+        projected(w_other, w_own)
+
+    for rows_in, h1, b, mod, size in (
+        (image, image_h1, image_rows, mod_image, PT),
+        (text, text_h1, text_rows, mod_text, TQ),
+    ):
+        for r in range(REQ):
+            at = slice(r * SLOTS * size, (r + 1) * SLOTS * size)
+            x = rows_in[r * SLOTS : (r + 1) * SLOTS].astype(F32).reshape(SLOTS * size, d_model)
+            first = x + mod[2, r : r + 1] * h1[at, :]
+            h1[at, :] = first
+            b[at, :] = normed(first, mod[3, r : r + 1], mod[4, r : r + 1]).astype(BF16)
+    tp = place[2]
+    own[0:PT, :] = image_h1[pl.ds(pl.multiple_of(tp * PT, PT), PT), :]
+    own[PT:ROWS, :] = text_h1[pl.ds(pl.multiple_of(tp * TQ, TQ), TQ), :]
+    hidden = jax.nn.gelu(mm(image_rows[...], up_image[...]), approximate=True).astype(BF16)
+    out[:, 0:PT, :] = mm(hidden, down_image[...]).reshape(CHUNKS, PT, d_model).astype(BF16)
+    hidden = jax.nn.gelu(mm(text_rows[...], up_text[...]), approximate=True).astype(BF16)
+    out[:, PT:ROWS, :] = mm(hidden, down_text[...]).reshape(CHUNKS, TQ, d_model).astype(BF16)
 
 
 def layer_rows(place, h1, received, mod_image, mod_text):
@@ -363,7 +435,7 @@
     section = lax.axis_index("section")
     tp = lax.axis_index("tp")
     seq = lax.axis_index("seq")
-    place = jnp.stack([tp // X, tp % X, tp, section]).astype(jnp.int32)
+    place = jnp.stack([tp // X, tp % X, tp, section, seq % C]).astype(jnp.int32)
     span, count = SLOTS * PT, SLOTS * TQ
     packed_rows = 2 * width + count * 2 * width // LANES
     packed = ((REQ, packed_rows, LANES), BF16)
@@ -404,10 +476,16 @@
     def exchanged(value):
         return lax.all_to_all(value, "tp", 0, 0, tiled=True)
 
-    def rest_of_layer(q_image, q_text, kv, rows):
+    w_own = lax.all_gather(
+        jnp.where(seq % C == 0, out_image[0], out_text[0]), "tp", axis=0, tiled=True
+    )
+    w_other = across_core(w_own)
+    mlp = up_image[0], down_image[0], up_text[0], down_text[0]
+
+    def rest_by_sums(q_image, q_text, kv, rows):
         (partial,) = call(
-            attend,
-            "attend",
+            attend_project,
+            "attend_project",
             [SMEM] + [VMEM] * 21,
             [chunks],
             [pltpu.VMEM((CHUNKS * PT, width), BF16), pltpu.VMEM((CHUNKS * TQ, width), BF16)],
@@ -427,7 +505,29 @@
         pieces = spread_z(jnp.stack([b, across_x(b)]))
         (partial,) = call(
             feed_forward, "feed_forward", [SMEM] + [VMEM] * 8, [chunks], rows_scratch
-        )(place, *pieces, up_image[0], down_image[0], up_text[0], down_text[0])
+        )(place, *pieces, *mlp)
+        return h1, exchanged(partial)
+
+    def rest_by_heads(q_image, q_text, kv, image_all, text_all):
+        heads = ((REQ * SLOTS * ROWS * width // LANES, LANES), BF16)
+        (o,) = call(attend_heads, "attend_heads", [SMEM] + [VMEM] * 19, [heads])(
+            patch_order, bias, q_image, q_text, *gathered_seq(kv), *stale_pieces
+        )
+        pieces = spread_z(jnp.stack([o, across_x(o)]))
+        partial, h1 = call(
+            heads_mlp,
+            "heads_mlp",
+            [SMEM] + [VMEM] * 14,
+            [chunks, row_f32],
+            [
+                pltpu.VMEM((CHUNKS * PT, d_model), BF16),
+                pltpu.VMEM((CHUNKS * TQ, d_model), BF16),
+                pltpu.VMEM((CHUNKS * PT, d_model), F32),
+                pltpu.VMEM((CHUNKS * TQ, d_model), F32),
+                pltpu.VMEM((CHUNKS * PT, d_model), BF16),
+                pltpu.VMEM((CHUNKS * TQ, d_model), BF16),
+            ],
+        )(place, *pieces, image_all, text_all, w_own, w_other, *mlp, *mods)
         return h1, exchanged(partial)
 
     q_image, q_text, kv_first, kv_text_first, own_rows = call(
@@ -439,16 +539,20 @@
         *mods,
         *weights,
     )
-    h1, received = rest_of_layer(q_image, q_text, kv_first, own_rows)
+    h1, received = rest_by_sums(q_image, q_text, kv_first, own_rows)
     (y_first,) = call(after_mlp, "after_mlp", [SMEM] + [VMEM] * 4, [row_bf16])(
         place, h1, received, *mods
     )
     arrived = to_next_section(y_first, 0)
     pieces = spread_z(jnp.stack([arrived, to_next_section(y_first, 1)]))
-    q_image, q_text, kv_next, kv_text_next = call(
-        project_next, "project_next", [SMEM] + [VMEM] * 8, qkv_shapes, rows_scratch
+    q_image, q_text, kv_next, kv_text_next, image_all, text_all = call(
+        project_next,
+        "project_next",
+        [SMEM] + [VMEM] * 8,
+        qkv_shapes + [((CHUNKS, PT, d_model), BF16), ((CHUNKS, TQ, d_model), BF16)],
+        rows_scratch,
     )(place, *pieces, *mods, *weights)
-    h1, received = rest_of_layer(q_image, q_text, kv_next, arrived)
+    h1, received = rest_by_heads(q_image, q_text, kv_next, image_all, text_all)
     tail = ((TQ, d_model + PT * channels // TQ), BF16)
     (tail_rows,) = call(last_rows, "last_rows", [SMEM] + [VMEM] * 7, [tail])(
         place, h1, received, *mods, mod_final, jnp.transpose(final_weight), y_first

time: 239 us -> 301 us (1.26)
  waiting for transfers between devices: 91.9 us -> 151 us
  blocking collectives: 64.7 us -> 39.5 us
  between operations: 1.03 us -> 14.4 us
  Pallas kernels: 29.3 us -> 35.8 us
  starting transfers between devices: 35.7 us -> 39.2 us
  other arithmetic: 0.95 us -> 4.08 us
    all_gather x0 -> x1, waiting for transfers between devices: none -> 61.9 us  [on_device(): lax.all_gather(jnp.where(seq % C == 0, out_image[0], out_text[0]), 'tp',...]
    all_to_all x3 -> x2, blocking collectives: 64.7 us -> 39.5 us  [exchanged(): return lax.all_to_all(value, 'tp', 0, 0, tiled=True)]
    pallas_call x7 -> x6, Pallas kernels: 24.1 us -> 29.9 us  [the longest x1 10.3 us: rest_by_heads(): call(heads_mlp, 'heads_mlp', [SMEM] + [VMEM] * 14, [chunks, row_f32], [pl...]
    ppermute x9, waiting for transfers between devices: 20.7 us -> 16.2 us  [along_y(): return lax.ppermute(value, 'seq', pairs)]
    unnamed x74 -> x82, local copies, waits for them, and re-layouts: 11 us -> 13.9 us
  transfers between devices with their start and end apart: 36 -> 38, of which waited for: 24 -> 24; matrix products, arithmetic and copies ran while one was open for 1% -> 1% of each run, Pallas kernels for 1% -> 8%
where the time goes in v1:
time: 301 us
  waiting for transfers between devices  151 us (50%)
  blocking collectives  39.5 us (13%)
  starting transfers between devices  39.2 us (13%)
  Pallas kernels  35.8 us (12%)
  local copies, waits for them, and re-layouts  16.5 us (5%)
  between operations  14.4 us (5%)
  other arithmetic  4.08 us (1%)
    all_gather x1, waiting for transfers between devices, on_device(): lax.all_gather(jnp.where(seq % C == 0, out_image[0], out_text[0]), 'tp',...  61.9 us
    all_to_all x2, blocking collectives, exchanged(): return lax.all_to_all(value, 'tp', 0, 0, tiled=True)  39.5 us
    ppermute x9, waiting for transfers between devices, along_z(): return lax.ppermute(value, 'tp', pairs)  31.8 us
    all_to_all x1, waiting for transfers between devices, exchanged(): return lax.all_to_all(value, 'tp', 0, 0, tiled=True)  16.9 us
    ppermute x9, waiting for transfers between devices, along_y(): return lax.ppermute(value, 'seq', pairs)  16.2 us
    ppermute x9, starting transfers between devices, along_y(): return lax.ppermute(value, 'seq', pairs)  14.1 us
    unnamed x82, local copies, waits for them, and re-layouts  13.9 us
    ppermute x2, waiting for transfers between devices, across_x(): return lax.ppermute(value, 'tp', [(i, i ^ 1) for i in range(Z * X)])  11.1 us
  transfers between devices with their start and end apart: 38, of which 24 were waited for; matrix products, arithmetic and copies ran while one was open for 1% of the time, Pallas kernels for 8%

profile of v1, /device:TPU:0, one launch (start us, length us, event | category | flops | bytes accessed | tf_op | source)
XLA Modules:
  0.0 300.5 jit_solution(16670337346457356230)
XLA Ops:
  9.7 3.4 %collective-permute-start.12 = (bf16[2,480,128]{2,1,0:T(8,128)(2,1)S(1)}, bf16[2,480,128]{2,1,0:T(8,128)(2,1)S(1)}, u32[]{:S(2)}, u32[]{:S(2)}) collective-permute-start(bf16[2,480,128]{2,1,0:T(8,128)(2,1)S(1)} %pack_stale.1.refs_8_), channel_id=1, source_target_pairs={{0,32},{8,40},{16,48},{24,56},{32,0},{40,8},{48,16},{56,24},{1,33}... | collective-permute-start | bytes 737288 | tf_op jit(solution)/shard_map/ppermute | solution.py:53
  18.8 2.8 project_first.1
  24.2 2.6 collective-permute-start.3
  26.9 61.9 %all-gather.2.cloned.1.call-done.w_own = bf16[1536,1536]{1,0:T(8,128)(2,1)} async-done(((bf16[192,1536]{1,0:T(8,128)(2,1)}), bf16[1536,1536]{1,0:T(8,128)(2,1)}) %all-gather.2.cloned.1.call-update) | async-done | bytes 4718608 | tf_op jit(solution)/shard_map/all_gather | solution.py:479
  91.7 7.0 %collective-permute-done.1.refs_2_ = bf16[2,480,128]{2,1,0:T(8,128)(2,1)} collective-permute-done((bf16[2,480,128]{2,1,0:T(8,128)(2,1)}, bf16[2,480,128]{2,1,0:T(8,128)(2,1)}, u32[]{:S(2)}, u32[]{:S(2)}) %collective-permute-start.1) | collective-permute-done | bytes 245792 | tf_op jit(solution)/shard_map/ppermute | solution.py:53
  109.3 7.2 %attend_project.1 = bf16[8,40,1536]{2,1,0:T(8,128)(2,1)S(1)} custom-call(s32[4]{0:T(128)S(1)} %copy-done.35, f32[2,1280]{1,0:T(2,128)S(1)} %copy-done.25, bf16[256,192]{1,0:T(8,128)(2,1)S(1)} %copy-done.24, f32[64,192]{1,0:T(8,128)S(1)} %copy-done.28, bf16[2,480,128]{2,1,0:T(8,128)(2,1)} %get-tuple-element.24.refs_0_, ...), custom_call_target="tpu_custom_call" | custom-call | tf_op jit(solution)/shard_map/attend_project/pallas_call | solution.py:486
  116.5 19.7 %all_to_all.20.received = bf16[8,40,1536]{2,1,0:T(8,128)(2,1)S(1)} all-to-all(bf16[8,40,1536]{2,1,0:T(8,128)(2,1)S(1)} %attend_project.1), channel_id=1, replica_groups=mesh['section'=2,'seq'=8,'tp'=8] {'tp'}, dimensions={0} | all-to-all | bytes 1966080 | tf_op jit(solution)/shard_map/all_to_all | solution.py:477
  137.9 5.6 %collective-permute-done.14 = bf16[40,1536]{1,0:T(8,128)(2,1)S(1)} collective-permute-done((bf16[40,1536]{1,0:T(8,128)(2,1)S(1)}, bf16[40,1536]{1,0:T(8,128)(2,1)S(1)}, u32[]{:S(2)}, u32[]{:S(2)}) %collective-permute-start.14) | collective-permute-done | bytes 122912 | tf_op jit(solution)/shard_map/ppermute | solution.py:48
  146.2 5.7 %collective-permute-done.17.p3 = bf16[2,40,1536]{2,1,0:T(8,128)(2,1)S(1)} collective-permute-done((bf16[2,40,1536]{2,1,0:T(8,128)(2,1)S(1)}, bf16[2,40,1536]{2,1,0:T(8,128)(2,1)S(1)}, u32[]{:S(2)}, u32[]{:S(2)}) %collective-permute-start.17) | collective-permute-done | bytes 245792 | tf_op jit(solution)/shard_map/ppermute | solution.py:44
  156.8 3.2 %feed_forward.1 = bf16[8,40,1536]{2,1,0:T(8,128)(2,1)S(1)} custom-call(s32[5]{0:T(128)S(1)} %stack.50.place, bf16[2,40,1536]{2,1,0:T(8,128)(2,1)S(1)} %pad_maximum_fusion.p0, bf16[2,40,1536]{2,1,0:T(8,128)(2,1)S(1)} %collective-permute-done.15.p1, bf16[2,40,1536]{2,1,0:T(8,128)(2,1)S(1)} %collective-permute-done.16.p2, ...), custom_call_target="tpu_custom_call" | custom-call | tf_op jit(solution)/shard_map/feed_forward/pallas_call | solution.py:506
  160.0 19.8 %all_to_all.21.received = bf16[8,40,1536]{2,1,0:T(8,128)(2,1)S(1)} all-to-all(bf16[8,40,1536]{2,1,0:T(8,128)(2,1)S(1)} %feed_forward.1), channel_id=1, replica_groups=mesh['section'=2,'seq'=8,'tp'=8] {'tp'}, dimensions={0} | all-to-all | bytes 1966080 | tf_op jit(solution)/shard_map/all_to_all | solution.py:477
  180.5 3.0 %collective-permute-start.19 = (bf16[40,1536]{1,0:T(8,128)(2,1)S(1)}, bf16[40,1536]{1,0:T(8,128)(2,1)S(1)}, u32[]{:S(2)}, u32[]{:S(2)}) collective-permute-start(bf16[40,1536]{1,0:T(8,128)(2,1)S(1)} %after_mlp.1.first), channel_id=1, source_target_pairs={{0,65},{1,64},{2,67},{3,66},{4,69},{5,68},{6,71},{7,70},{8,73},{9,... | collective-permute-start | bytes 368648 | tf_op jit(solution)/shard_map/ppermute | solution.py:62
  190.0 5.2 %collective-permute-done.22.p3 = bf16[2,40,1536]{2,1,0:T(8,128)(2,1)S(1)} collective-permute-done((bf16[2,40,1536]{2,1,0:T(8,128)(2,1)S(1)}, bf16[2,40,1536]{2,1,0:T(8,128)(2,1)S(1)}, u32[]{:S(2)}, u32[]{:S(2)}) %collective-permute-start.22) | collective-permute-done | bytes 245792 | tf_op jit(solution)/shard_map/ppermute | solution.py:44
  195.2 2.7 collective-permute-done.21.p2
  206.9 6.6 %collective-permute-done.28.refs_6_ = bf16[2,480,128]{2,1,0:T(8,128)(2,1)S(1)} collective-permute-done((bf16[2,480,128]{2,1,0:T(8,128)(2,1)S(1)}, bf16[2,480,128]{2,1,0:T(8,128)(2,1)S(1)}, u32[]{:S(2)}, u32[]{:S(2)}) %collective-permute-start.28) | collective-permute-done | bytes 245792 | tf_op jit(solution)/shard_map/ppermute | solution.py:53
  217.6 5.8 %attend_heads.1 = bf16[480,128]{1,0:T(8,128)(2,1)S(1)} custom-call(s32[4]{0:T(128)S(1)} %copy-done.36, f32[2,1280]{1,0:T(2,128)S(1)} %copy-done.26, bf16[256,192]{1,0:T(8,128)(2,1)S(1)} %get-tuple-element.27.q_image, f32[64,192]{1,0:T(8,128)S(1)} %get-tuple-element.28.q_text, bf16[2,480,128]{2,1,0:T(8,128)(2,1)S(1)} %get-tuple-element.29.refs_0_, ...), custom_call_target="tpu_custom_call" | custom-call | tf_op jit(solution)/shard_map/attend_heads/pallas_call | solution.py:513
  224.8 5.5 %collective-permute-done.30 = bf16[480,128]{1,0:T(8,128)(2,1)S(1)} collective-permute-done((bf16[480,128]{1,0:T(8,128)(2,1)S(1)}, bf16[480,128]{1,0:T(8,128)(2,1)S(1)}, u32[]{:S(2)}, u32[]{:S(2)}) %collective-permute-start.30) | collective-permute-done | bytes 122912 | tf_op jit(solution)/shard_map/ppermute | solution.py:48
  233.7 5.7 %collective-permute-done.33.o3 = bf16[2,480,128]{2,1,0:T(8,128)(2,1)S(1)} collective-permute-done((bf16[2,480,128]{2,1,0:T(8,128)(2,1)S(1)}, bf16[2,480,128]{2,1,0:T(8,128)(2,1)S(1)}, u32[]{:S(2)}, u32[]{:S(2)}) %collective-permute-start.33) | collective-permute-done | bytes 245792 | tf_op jit(solution)/shard_map/ppermute | solution.py:44
  241.0 3.5 %collective-permute-done.31.o1 = bf16[2,480,128]{2,1,0:T(8,128)(2,1)S(1)} collective-permute-done((bf16[2,480,128]{2,1,0:T(8,128)(2,1)S(1)}, bf16[2,480,128]{2,1,0:T(8,128)(2,1)S(1)}, u32[]{:S(2)}, u32[]{:S(2)}) %collective-permute-start.31) | collective-permute-done | bytes 245792 | tf_op jit(solution)/shard_map/ppermute | solution.py:44
  244.5 10.3 %heads_mlp.1 = (bf16[8,40,1536]{2,1,0:T(8,128)(2,1)}, f32[40,1536]{1,0:T(8,128)S(1)}) custom-call(s32[5]{0:T(128)S(1)} %stack.50.place, bf16[2,480,128]{2,1,0:T(8,128)(2,1)S(1)} %pad_maximum_fusion.2.o0, bf16[2,480,128]{2,1,0:T(8,128)(2,1)S(1)} %collective-permute-done.31.o1, bf16[2,480,128]{2,1,0:T(8,128)(2,1)S(1)} %collective-permute-done.32.o2, ...), custom_call_target="tpu_custom_call" | custom-call | tf_op jit(solution)/shard_map/heads_mlp/pallas_call | solution.py:517
  254.8 3.7 %all-to-all-start.2 = ((bf16[8,40,1536]{2,1,0:T(8,128)(2,1)}), bf16[8,40,1536]{2,1,0:T(8,128)(2,1)S(1)}, u32[]{:S(2)}, u32[]{:S(2)}) async-start(bf16[8,40,1536]{2,1,0:T(8,128)(2,1)} %get-tuple-element.33), calls=%async_computation.2 | async-start | bytes 1966080 | tf_op jit(solution)/shard_map/all_to_all | solution.py:477
  258.5 16.9 %all-to-all-done.2.received = bf16[8,40,1536]{2,1,0:T(8,128)(2,1)S(1)} async-done(((bf16[8,40,1536]{2,1,0:T(8,128)(2,1)}), bf16[8,40,1536]{2,1,0:T(8,128)(2,1)S(1)}, u32[]{:S(2)}, u32[]{:S(2)}) %all-to-all-start.2) | async-done | bytes 983072 | tf_op jit(solution)/shard_map/all_to_all | solution.py:477
  277.4 4.4 %all-to-all-start.3 = ((bf16[16,8,1792]{2,1,0:T(8,128)(2,1)}), bf16[16,8,1792]{2,1,0:T(8,128)(2,1)S(1)}, u32[]{:S(2)}, u32[]{:S(2)}) async-start(bf16[16,8,1792]{2,1,0:T(8,128)(2,1)} %broadcast_in_dim.28), calls=%async_computation.3 | async-start | bytes 917504 | tf_op jit(solution)/shard_map/all_to_all | solution.py:560
  284.2 8.2 %all-to-all-done.3.received = bf16[16,8,1792]{2,1,0:T(8,128)(2,1)S(1)} async-done(((bf16[16,8,1792]{2,1,0:T(8,128)(2,1)}), bf16[16,8,1792]{2,1,0:T(8,128)(2,1)S(1)}, u32[]{:S(2)}, u32[]{:S(2)}) %all-to-all-start.3) | async-done | bytes 458784 | tf_op jit(solution)/shard_map/all_to_all | solution.py:560
  (164 shorter events, 65.9 us)
Async XLA Ops:
  7.2 81.6 %all-gather.2.cloned.1.call-start = ((), (), s32[]{:S(2)}) async-start(), calls=%async_computation.4 | async-start | bytes 5308416 | tf_op jit(solution)/shard_map/all_gather | solution.py:479
  9.7 14.5 %collective-permute-start.12 = (bf16[2,480,128]{2,1,0:T(8,128)(2,1)S(1)}, bf16[2,480,128]{2,1,0:T(8,128)(2,1)S(1)}, u32[]{:S(2)}, u32[]{:S(2)}) collective-permute-start(bf16[2,480,128]{2,1,0:T(8,128)(2,1)S(1)} %pack_stale.1.refs_8_), channel_id=1, source_target_pairs={{0,32},{8,40},{16,48},{24,56},{32,0},{40,8},{48,16},{56,24},{1,33}... | collective-permute-start | bytes 737288 | tf_op jit(solution)/shard_map/ppermute | solution.py:53
  13.1 13.8 %collective-permute-start.10 = (bf16[2,480,128]{2,1,0:T(8,128)(2,1)S(1)}, bf16[2,480,128]{2,1,0:T(8,128)(2,1)S(1)}, u32[]{:S(2)}, u32[]{:S(2)}) collective-permute-start(bf16[2,480,128]{2,1,0:T(8,128)(2,1)S(1)} %pack_stale.1.refs_8_), channel_id=1, source_target_pairs={{0,48},{8,56},{16,0},{24,8},{32,16},{40,24},{48,32},{56,40},{1,49}... | collective-permute-start | bytes 737288 | tf_op jit(solution)/shard_map/ppermute | solution.py:53
  14.2 74.7 %collective-permute-start.8 = (bf16[2,480,128]{2,1,0:T(8,128)(2,1)S(1)}, bf16[2,480,128]{2,1,0:T(8,128)(2,1)}, u32[]{:S(2)}, u32[]{:S(2)}) collective-permute-start(bf16[2,480,128]{2,1,0:T(8,128)(2,1)S(1)} %pack_stale.1.refs_8_), channel_id=1, source_target_pairs={{0,16},{8,24},{16,32},{24,40},{32,48},{40,56},{48,0},{56,8},{1,17}... | collective-permute-start | bytes 737288 | tf_op jit(solution)/shard_map/ppermute | solution.py:53
  15.1 75.2 %collective-permute-start.7 = (bf16[2,480,128]{2,1,0:T(8,128)(2,1)S(1)}, bf16[2,480,128]{2,1,0:T(8,128)(2,1)}, u32[]{:S(2)}, u32[]{:S(2)}) collective-permute-start(bf16[2,480,128]{2,1,0:T(8,128)(2,1)S(1)} %pack_stale.1.refs_8_), channel_id=1, source_target_pairs={{0,8},{8,0},{16,24},{24,16},{32,40},{40,32},{48,56},{56,48},{1,9},... | collective-permute-start | bytes 737288 | tf_op jit(solution)/shard_map/ppermute | solution.py:57
  23.5 67.0 %collective-permute-start.5 = (bf16[2,480,128]{2,1,0:T(8,128)(2,1)}, bf16[2,480,128]{2,1,0:T(8,128)(2,1)}, u32[]{:S(2)}, u32[]{:S(2)}) collective-permute-start(bf16[2,480,128]{2,1,0:T(8,128)(2,1)} %get-tuple-element.24.refs_0_), channel_id=1, source_target_pairs={{0,32},{8,40},{16,48},{24,56},{32,0},{40,8},{48,16},{56,24},{1,33}... | collective-permute-start | bytes 737288 | tf_op jit(solution)/shard_map/ppermute | solution.py:53
  24.2 66.6 %collective-permute-start.3 = (bf16[2,480,128]{2,1,0:T(8,128)(2,1)}, bf16[2,480,128]{2,1,0:T(8,128)(2,1)}, u32[]{:S(2)}, u32[]{:S(2)}) collective-permute-start(bf16[2,480,128]{2,1,0:T(8,128)(2,1)} %get-tuple-element.24.refs_0_), channel_id=1, source_target_pairs={{0,48},{8,56},{16,0},{24,8},{32,16},{40,24},{48,32},{56,40},{1,49}... | collective-permute-start | bytes 737288 | tf_op jit(solution)/shard_map/ppermute | solution.py:53
  88.8 155.7 %collective-permute-start.34 = (bf16[1536,1536]{1,0:T(8,128)(2,1)}, bf16[1536,1536]{1,0:T(8,128)(2,1)}, u32[]{:S(2)}, u32[]{:S(2)}) collective-permute-start(bf16[1536,1536]{1,0:T(8,128)(2,1)} %all-gather.2.cloned.1.call-done.w_own), channel_id=1, source_target_pairs={{0,8},{8,0},{16,24},{24,16},{32,40},{40,32},{48,56},{56,48},{1,9},... | collective-permute-start | bytes 14155784 | tf_op jit(solution)/shard_map/ppermute | solution.py:57
  88.8 9.9 %collective-permute-start.1 = (bf16[2,480,128]{2,1,0:T(8,128)(2,1)}, bf16[2,480,128]{2,1,0:T(8,128)(2,1)}, u32[]{:S(2)}, u32[]{:S(2)}) collective-permute-start(bf16[2,480,128]{2,1,0:T(8,128)(2,1)} %get-tuple-element.24.refs_0_), channel_id=1, source_target_pairs={{0,16},{8,24},{16,32},{24,40},{32,48},{40,56},{48,0},{56,8},{1,17}... | collective-permute-start | bytes 737288 | tf_op jit(solution)/shard_map/ppermute | solution.py:53
  90.5 8.7 %collective-permute-start.13 = (bf16[2,480,128]{2,1,0:T(8,128)(2,1)S(1)}, bf16[2,480,128]{2,1,0:T(8,128)(2,1)}, u32[]{:S(2)}, u32[]{:S(2)}) collective-permute-start(bf16[2,480,128]{2,1,0:T(8,128)(2,1)S(1)} %collective-permute-done.12.refs_14_), channel_id=1, source_target_pairs={{0,8},{8,0},{16,24},{24,16},{32,40},{40,32},{48,56},{56,48},{1,9},... | collective-permute-start | bytes 737288 | tf_op jit(solution)/shard_map/ppermute | solution.py:57
  90.8 8.5 %collective-permute-start.11 = (bf16[2,480,128]{2,1,0:T(8,128)(2,1)S(1)}, bf16[2,480,128]{2,1,0:T(8,128)(2,1)}, u32[]{:S(2)}, u32[]{:S(2)}) collective-permute-start(bf16[2,480,128]{2,1,0:T(8,128)(2,1)S(1)} %collective-permute-done.10.refs_12_), channel_id=1, source_target_pairs={{0,8},{8,0},{16,24},{24,16},{32,40},{40,32},{48,56},{56,48},{1,9},... | collective-permute-start | bytes 737288 | tf_op jit(solution)/shard_map/ppermute | solution.py:57
  144.5 9.8 %collective-permute-start.16 = (bf16[2,40,1536]{2,1,0:T(8,128)(2,1)S(1)}, bf16[2,40,1536]{2,1,0:T(8,128)(2,1)S(1)}, u32[]{:S(2)}, u32[]{:S(2)}) collective-permute-start(bf16[2,40,1536]{2,1,0:T(8,128)(2,1)S(1)} %pad_maximum_fusion.p0), channel_id=1, source_target_pairs={{0,4},{1,5},{2,6},{3,7},{4,0},{5,1},{6,2},{7,3},{8,12},{9,13},{10,... | collective-permute-start | bytes 737288 | tf_op jit(solution)/shard_map/ppermute | solution.py:44
  146.0 10.8 %collective-permute-start.15 = (bf16[2,40,1536]{2,1,0:T(8,128)(2,1)S(1)}, bf16[2,40,1536]{2,1,0:T(8,128)(2,1)S(1)}, u32[]{:S(2)}, u32[]{:S(2)}) collective-permute-start(bf16[2,40,1536]{2,1,0:T(8,128)(2,1)S(1)} %pad_maximum_fusion.p0), channel_id=1, source_target_pairs={{0,2},{1,3},{2,4},{3,5},{4,6},{5,7},{6,0},{7,1},{8,10},{9,11},{10,... | collective-permute-start | bytes 737288 | tf_op jit(solution)/shard_map/ppermute | solution.py:44
  188.5 9.3 %collective-permute-start.21 = (bf16[2,40,1536]{2,1,0:T(8,128)(2,1)S(1)}, bf16[2,40,1536]{2,1,0:T(8,128)(2,1)S(1)}, u32[]{:S(2)}, u32[]{:S(2)}) collective-permute-start(bf16[2,40,1536]{2,1,0:T(8,128)(2,1)S(1)} %pad_maximum_fusion.1.p0), channel_id=1, source_target_pairs={{0,4},{1,5},{2,6},{3,7},{4,0},{5,1},{6,2},{7,3},{8,12},{9,13},{10,... | collective-permute-start | bytes 737288 | tf_op jit(solution)/shard_map/ppermute | solution.py:44
  190.0 10.4 %collective-permute-start.20 = (bf16[2,40,1536]{2,1,0:T(8,128)(2,1)S(1)}, bf16[2,40,1536]{2,1,0:T(8,128)(2,1)S(1)}, u32[]{:S(2)}, u32[]{:S(2)}) collective-permute-start(bf16[2,40,1536]{2,1,0:T(8,128)(2,1)S(1)} %pad_maximum_fusion.1.p0), channel_id=1, source_target_pairs={{0,2},{1,3},{2,4},{3,5},{4,6},{5,7},{6,0},{7,1},{8,10},{9,11},{10,... | collective-permute-start | bytes 737288 | tf_op jit(solution)/shard_map/ppermute | solution.py:44
  203.0 10.4 %collective-permute-start.28 = (bf16[2,480,128]{2,1,0:T(8,128)(2,1)S(1)}, bf16[2,480,128]{2,1,0:T(8,128)(2,1)S(1)}, u32[]{:S(2)}, u32[]{:S(2)}) collective-permute-start(bf16[2,480,128]{2,1,0:T(8,128)(2,1)S(1)} %get-tuple-element.29.refs_0_), channel_id=1, source_target_pairs={{0,32},{8,40},{16,48},{24,56},{32,0},{40,8},{48,16},{56,24},{1,33}... | collective-permute-start | bytes 737288 | tf_op jit(solution)/shard_map/ppermute | solution.py:53
  204.8 10.1 %collective-permute-start.26 = (bf16[2,480,128]{2,1,0:T(8,128)(2,1)S(1)}, bf16[2,480,128]{2,1,0:T(8,128)(2,1)S(1)}, u32[]{:S(2)}, u32[]{:S(2)}) collective-permute-start(bf16[2,480,128]{2,1,0:T(8,128)(2,1)S(1)} %get-tuple-element.29.refs_0_), channel_id=1, source_target_pairs={{0,48},{8,56},{16,0},{24,8},{32,16},{40,24},{48,32},{56,40},{1,49}... | collective-permute-start | bytes 737288 | tf_op jit(solution)/shard_map/ppermute | solution.py:53
  206.0 10.1 %collective-permute-start.24 = (bf16[2,480,128]{2,1,0:T(8,128)(2,1)S(1)}, bf16[2,480,128]{2,1,0:T(8,128)(2,1)S(1)}, u32[]{:S(2)}, u32[]{:S(2)}) collective-permute-start(bf16[2,480,128]{2,1,0:T(8,128)(2,1)S(1)} %get-tuple-element.29.refs_0_), channel_id=1, source_target_pairs={{0,16},{8,24},{16,32},{24,40},{32,48},{40,56},{48,0},{56,8},{1,17}... | collective-permute-start | bytes 737288 | tf_op jit(solution)/shard_map/ppermute | solution.py:53
  206.9 9.2 %collective-permute-start.23 = (bf16[2,480,128]{2,1,0:T(8,128)(2,1)S(1)}, bf16[2,480,128]{2,1,0:T(8,128)(2,1)S(1)}, u32[]{:S(2)}, u32[]{:S(2)}) collective-permute-start(bf16[2,480,128]{2,1,0:T(8,128)(2,1)S(1)} %get-tuple-element.29.refs_0_), channel_id=1, source_target_pairs={{0,8},{8,0},{16,24},{24,16},{32,40},{40,32},{48,56},{56,48},{1,9},... | collective-permute-start | bytes 737288 | tf_op jit(solution)/shard_map/ppermute | solution.py:57
  230.4 9.0 %collective-permute-start.33 = (bf16[2,480,128]{2,1,0:T(8,128)(2,1)S(1)}, bf16[2,480,128]{2,1,0:T(8,128)(2,1)S(1)}, u32[]{:S(2)}, u32[]{:S(2)}) collective-permute-start(bf16[2,480,128]{2,1,0:T(8,128)(2,1)S(1)} %pad_maximum_fusion.2.o0), channel_id=1, source_target_pairs={{0,6},{1,7},{2,0},{3,1},{4,2},{5,3},{6,4},{7,5},{8,14},{9,15},{10,... | collective-permute-start | bytes 737288 | tf_op jit(solution)/shard_map/ppermute | solution.py:44
  230.5 10.5 %collective-permute-start.32 = (bf16[2,480,128]{2,1,0:T(8,128)(2,1)S(1)}, bf16[2,480,128]{2,1,0:T(8,128)(2,1)S(1)}, u32[]{:S(2)}, u32[]{:S(2)}) collective-permute-start(bf16[2,480,128]{2,1,0:T(8,128)(2,1)S(1)} %pad_maximum_fusion.2.o0), channel_id=1, source_target_pairs={{0,4},{1,5},{2,6},{3,7},{4,0},{5,1},{6,2},{7,3},{8,12},{9,13},{10,... | collective-permute-start | bytes 737288 | tf_op jit(solution)/shard_map/ppermute | solution.py:44
  232.3 12.2 %collective-permute-start.31 = (bf16[2,480,128]{2,1,0:T(8,128)(2,1)S(1)}, bf16[2,480,128]{2,1,0:T(8,128)(2,1)S(1)}, u32[]{:S(2)}, u32[]{:S(2)}) collective-permute-start(bf16[2,480,128]{2,1,0:T(8,128)(2,1)S(1)} %pad_maximum_fusion.2.o0), channel_id=1, source_target_pairs={{0,2},{1,3},{2,4},{3,5},{4,6},{5,7},{6,0},{7,1},{8,10},{9,11},{10,... | collective-permute-start | bytes 737288 | tf_op jit(solution)/shard_map/ppermute | solution.py:44
  254.8 20.6 %all-to-all-start.2 = ((bf16[8,40,1536]{2,1,0:T(8,128)(2,1)}), bf16[8,40,1536]{2,1,0:T(8,128)(2,1)S(1)}, u32[]{:S(2)}, u32[]{:S(2)}) async-start(bf16[8,40,1536]{2,1,0:T(8,128)(2,1)} %get-tuple-element.33), calls=%async_computation.2 | async-start | bytes 1966080 | tf_op jit(solution)/shard_map/all_to_all | solution.py:477
  277.4 15.0 %all-to-all-start.3 = ((bf16[16,8,1792]{2,1,0:T(8,128)(2,1)}), bf16[16,8,1792]{2,1,0:T(8,128)(2,1)S(1)}, u32[]{:S(2)}, u32[]{:S(2)}) async-start(bf16[16,8,1792]{2,1,0:T(8,128)(2,1)} %broadcast_in_dim.28), calls=%async_computation.3 | async-start | bytes 917504 | tf_op jit(solution)/shard_map/all_to_all | solution.py:560
  (55 other events, 963.6 us)
Sparse Core Ops, SparseCore 0:
  10.3 78.4 all-gather.1

commit v2 on v0

--- a/solution.py
+++ b/solution.py
@@ -20,14 +20,14 @@
 Z, X = 4, 2
 Y, C = 4, 2
 LANES = 128
-RING = (1, 3, 2)
+RING = (2, 1, 3)
 PIECES = ((0, 0), (0, 1), (1, 0), (1, 1), (3, 0), (3, 1), (2, 0), (2, 1))
 
 VMEM = pl.BlockSpec(memory_space=pltpu.VMEM)
 SMEM = pl.BlockSpec(memory_space=pltpu.SMEM)
 
 
-def call(body, name, in_specs, out_shapes, scratch=()):
+def call(body, name, in_specs, out_shapes, scratch=(), mib=40):
     return pl.pallas_call(
         body,
         name=name,
@@ -35,7 +35,7 @@
         out_specs=[VMEM] * len(out_shapes),
         out_shape=[jax.ShapeDtypeStruct(*each) for each in out_shapes],
         scratch_shapes=list(scratch),
-        compiler_params=pltpu.CompilerParams(vmem_limit_bytes=40 * 1024 * 1024),
+        compiler_params=pltpu.CompilerParams(vmem_limit_bytes=mib * 1024 * 1024),
     )
 
 
@@ -155,17 +155,18 @@
     return sum(jnp.where(patch == order[k], k, 0) for k in range(SLOTS))
 
 
-def attend(order, bias, q_image, q_text, *refs):
+def attend(place, order, bias, q_image, q_text, *refs):
     fresh, stale = refs[0:8], refs[8:16]
-    out_image, out_text, out, o_image, o_text = refs[16:]
+    out_image, out_text = refs[16:18]
+    outs, (o_image, o_text, image, text) = refs[18:26], refs[26:]
     width = q_image.shape[1]
     heads = width // HD
     span, count = SLOTS * PT, SLOTS * TQ
     rows = span + count
     image_keys = len(fresh) * span
     key_count = image_keys + len(fresh) * count
-    head_of_row = lax.broadcasted_iota(jnp.int32, (rows, width), 1) // HD
-    row = lax.broadcasted_iota(jnp.int32, (rows, 1), 0)
+    lane_head = lax.broadcasted_iota(jnp.int32, (rows, width), 1) // HD
+    row = lax.broadcasted_iota(jnp.int32, (heads * rows, 1), 0) % rows
     row_slot = jnp.where(row < span, slot_of(row // PT, order), (row - span) // TQ)
     key = lax.broadcasted_iota(jnp.int32, (1, key_count), 1)
     key_slot = jnp.where(
@@ -206,30 +207,38 @@
             ],
             axis=0,
         )
+        queries = jnp.concatenate(
+            [jnp.where(lane_head == h, q, 0.0) for h in range(heads)], axis=0
+        ).astype(BF16)
         fresh_text, stale_text = text_of(fresh, r), text_of(stale, r)
-        merged = jnp.zeros((rows, width), F32)
-        for h in range(heads):
-            queries = jnp.where(head_of_row == h, q, 0.0).astype(BF16)
-            scores = jnp.where(
-                is_fresh,
-                scores_of(queries, fresh, fresh_text, r),
-                scores_of(queries, stale, stale_text, r),
-            ) * HD ** (-0.5)
-            scores = scores + bias[r : r + 1, :]
-            top = jnp.max(scores, axis=-1, keepdims=True)
-            weights = jnp.exp(scores - top)
-            total = jnp.sum(weights, axis=-1, keepdims=True)
-            summed = summed_of(
-                jnp.where(is_fresh, weights, 0.0).astype(BF16), fresh, fresh_text, r
-            ) + summed_of(jnp.where(is_fresh, 0.0, weights).astype(BF16), stale, stale_text, r)
-            merged = jnp.where(head_of_row == h, summed / total, merged)
+        scores = jnp.where(
+            is_fresh,
+            scores_of(queries, fresh, fresh_text, r),
+            scores_of(queries, stale, stale_text, r),
+        ) * HD ** (-0.5)
+        scores = scores + bias[r : r + 1, :]
+        top = jnp.max(scores, axis=-1, keepdims=True)
+        weights = jnp.exp(scores - top)
+        total = jnp.sum(weights, axis=-1, keepdims=True)
+        summed = summed_of(
+            jnp.where(is_fresh, weights, 0.0).astype(BF16), fresh, fresh_text, r
+        ) + summed_of(jnp.where(is_fresh, 0.0, weights).astype(BF16), stale, stale_text, r)
+        summed = summed / total
+        merged = summed[0:rows]
+        for h in range(1, heads):
+            merged = jnp.where(lane_head == h, summed[h * rows : (h + 1) * rows], merged)
         o_image[r * span : (r + 1) * span, :] = merged[0:span].astype(BF16)
         o_text[r * count : (r + 1) * count, :] = merged[span:].astype(BF16)
-    d_model = out.shape[2]
-    image = mm(o_image[...], out_image[...])
-    text = mm(o_text[...], out_text[...])
-    out[:, 0:PT, :] = image.reshape(CHUNKS, PT, d_model).astype(BF16)
-    out[:, PT:ROWS, :] = text.reshape(CHUNKS, TQ, d_model).astype(BF16)
+    image[...] = mm(o_image[...], out_image[...])
+    text[...] = mm(o_text[...], out_text[...])
+    for i, out in enumerate(outs):
+        chunk = (place[0] + i // X) % Z * X + (place[1] + i % X) % X
+        out[0:PT, :] = image[pl.ds(pl.multiple_of(chunk * PT, PT), PT), :].astype(BF16)
+        out[PT:ROWS, :] = text[pl.ds(pl.multiple_of(chunk * TQ, TQ), TQ), :].astype(BF16)
+
+
+def add_far(p0, p1, p2, p3, out):
+    out[...] = summed_parts((p0, p1, p2, p3)).astype(BF16)
 
 
 def pack_stale(image, text, out):
@@ -247,15 +256,15 @@
     return mod[i, pl.ds(place[2] // SLOTS, 1), :]
 
 
-def summed_chunks(received):
-    total = received[0].astype(F32)
-    for i in range(1, CHUNKS):
-        total = total + received[i].astype(F32)
+def summed_parts(parts):
+    total = parts[0][...].astype(F32)
+    for part in parts[1:]:
+        total = total + part[...].astype(F32)
     return total
 
 
-def after_attention(place, rows, received, mod_image, mod_text, h1, b):
-    summed = summed_chunks(received)
+def after_attention(place, rows, p0, p1, p2, p3, p4, mod_image, mod_text, h1, b):
+    summed = summed_parts((p0, p1, p2, p3, p4))
     for low, high, mod in ((0, PT, mod_image), (PT, ROWS, mod_text)):
         first = rows[low:high, :].astype(F32) + own_mod(mod, 2, place) * summed[low:high]
         h1[low:high, :] = first
@@ -265,8 +274,7 @@
 
 
 def feed_forward(place, p0, p1, p2, p3, up_image, down_image, up_text, down_text, *refs):
-    out, image_rows, text_rows = refs
-    d_model = out.shape[2]
+    outs, (image_rows, text_rows) = refs[:8], refs[8:]
     for d, piece in enumerate((p0, p1, p2, p3)):
         for flip in range(X):
             at = d * X + flip
@@ -281,26 +289,27 @@
     for d in range(Z):
         for flip in range(X):
             at = d * X + flip
-            chunk = chunk_at(place, d, flip)
-            out[chunk, 0:PT, :] = image[at * PT : (at + 1) * PT].astype(BF16)
-            out[chunk, PT:ROWS, :] = text[at * TQ : (at + 1) * TQ].astype(BF16)
-
-
-def layer_rows(place, h1, received, mod_image, mod_text):
-    summed = summed_chunks(received)
+            out = outs[(Z - d) % Z * X + flip]
+            out[0:PT, :] = image[at * PT : (at + 1) * PT].astype(BF16)
+            out[PT:ROWS, :] = text[at * TQ : (at + 1) * TQ].astype(BF16)
+
+
+def layer_rows(place, h1, parts, mod_image, mod_text):
+    summed = summed_parts(parts)
     image = (h1[0:PT, :] + own_mod(mod_image, 5, place) * summed[0:PT]).astype(BF16)
     text = (h1[PT:ROWS, :] + own_mod(mod_text, 5, place) * summed[PT:ROWS]).astype(BF16)
     return image, text
 
 
-def after_mlp(place, h1, received, mod_image, mod_text, y):
-    image, text = layer_rows(place, h1, received, mod_image, mod_text)
+def after_mlp(place, h1, p0, p1, p2, p3, p4, mod_image, mod_text, y):
+    image, text = layer_rows(place, h1, (p0, p1, p2, p3, p4), mod_image, mod_text)
     y[0:PT, :] = image
     y[PT:ROWS, :] = text
 
 
-def last_rows(place, h1, received, mod_image, mod_text, mod_final, weight, first, out):
-    image, text = layer_rows(place, h1, received, mod_image, mod_text)
+def last_rows(place, h1, p0, p1, p2, p3, p4, mod_image, mod_text, mod_final, *refs):
+    weight, first, out = refs
+    image, text = layer_rows(place, h1, (p0, p1, p2, p3, p4), mod_image, mod_text)
     r = place[2] // SLOTS
     rows = normed(
         image.astype(F32), mod_final[pl.ds(r, 1), 0, :], mod_final[pl.ds(r, 1), 1, :]
@@ -398,20 +407,28 @@
         pltpu.VMEM((CHUNKS * PT, d_model), BF16),
         pltpu.VMEM((CHUNKS * TQ, d_model), F32),
     ]
-    chunks = ((CHUNKS, ROWS, d_model), BF16)
     row_f32, row_bf16 = ((ROWS, d_model), F32), ((ROWS, d_model), BF16)
 
-    def exchanged(value):
-        return lax.all_to_all(value, "tp", 0, 0, tiled=True)
+    def exchanged(parts):
+        far = [along_z(parts[step * X + 1], step) for step in RING]
+        near = [along_z(parts[step * X], step) for step in RING]
+        (half,) = call(add_far, "add_far", [VMEM] * 4, [row_bf16])(parts[1], *far)
+        return [parts[0], *near, across_x(half)]
 
     def rest_of_layer(q_image, q_text, kv, rows):
-        (partial,) = call(
+        partial = call(
             attend,
             "attend",
-            [SMEM] + [VMEM] * 21,
-            [chunks],
-            [pltpu.VMEM((CHUNKS * PT, width), BF16), pltpu.VMEM((CHUNKS * TQ, width), BF16)],
+            [SMEM] * 2 + [VMEM] * 21,
+            [row_bf16] * 8,
+            [
+                pltpu.VMEM((CHUNKS * PT, width), BF16),
+                pltpu.VMEM((CHUNKS * TQ, width), BF16),
+                pltpu.VMEM((CHUNKS * PT, d_model), F32),
+                pltpu.VMEM((CHUNKS * TQ, d_model), F32),
+            ],
         )(
+            place,
             patch_order,
             bias,
             q_image,
@@ -422,16 +439,21 @@
             out_text[0],
         )
         h1, b = call(
-            after_attention, "after_attention", [SMEM] + [VMEM] * 4, [row_f32, row_bf16]
-        )(place, rows, exchanged(partial), *mods)
+            after_attention, "after_attention", [SMEM] + [VMEM] * 8, [row_f32, row_bf16]
+        )(place, rows, *exchanged(partial), *mods)
         pieces = spread_z(jnp.stack([b, across_x(b)]))
-        (partial,) = call(
-            feed_forward, "feed_forward", [SMEM] + [VMEM] * 8, [chunks], rows_scratch
+        partial = call(
+            feed_forward, "feed_forward", [SMEM] + [VMEM] * 8, [row_bf16] * 8, rows_scratch
         )(place, *pieces, up_image[0], down_image[0], up_text[0], down_text[0])
         return h1, exchanged(partial)
 
     q_image, q_text, kv_first, kv_text_first, own_rows = call(
-        project_first, "project_first", [SMEM] + [VMEM] * 6, qkv_shapes + [row_bf16], rows_scratch
+        project_first,
+        "project_first",
+        [SMEM] + [VMEM] * 6,
+        qkv_shapes + [row_bf16],
+        rows_scratch,
+        60,
     )(
         place,
         hidden_image.reshape(CHUNKS, PT, d_model),
@@ -440,8 +462,8 @@
         *weights,
     )
     h1, received = rest_of_layer(q_image, q_text, kv_first, own_rows)
-    (y_first,) = call(after_mlp, "after_mlp", [SMEM] + [VMEM] * 4, [row_bf16])(
-        place, h1, received, *mods
+    (y_first,) = call(after_mlp, "after_mlp", [SMEM] + [VMEM] * 8, [row_bf16])(
+        place, h1, *received, *mods
     )
     arrived = to_next_section(y_first, 0)
     pieces = spread_z(jnp.stack([arrived, to_next_section(y_first, 1)]))
@@ -450,8 +472,8 @@
     )(place, *pieces, *mods, *weights)
     h1, received = rest_of_layer(q_image, q_text, kv_next, arrived)
     tail = ((TQ, d_model + PT * channels // TQ), BF16)
-    (tail_rows,) = call(last_rows, "last_rows", [SMEM] + [VMEM] * 7, [tail])(
-        place, h1, received, *mods, mod_final, jnp.transpose(final_weight), y_first
+    (tail_rows,) = call(last_rows, "last_rows", [SMEM] + [VMEM] * 11, [tail])(
+        place, h1, *received, *mods, mod_final, jnp.transpose(final_weight), y_first
     )
     shared = lax.all_to_all(
         jnp.broadcast_to(tail_rows[None], (2 * CHUNKS,) + tail_rows.shape),

time: 239 us -> 237 us (level); the launches traced: 239 us -> 233 us
  blocking collectives: 64.7 us -> 0 us
  starting transfers between devices: 35.7 us -> 96.4 us
  Pallas kernels: 29.3 us -> 33.2 us
  local copies, waits for them, and re-layouts: 14.9 us -> 11 us
  waiting for transfers between devices: 91.9 us -> 89.5 us
    all_to_all x3 -> x0, blocking collectives: 64.7 us -> none  [exchanged(): return lax.all_to_all(value, 'tp', 0, 0, tiled=True)]
    ppermute x9 -> x33, starting transfers between devices: 8.18 us -> 45.6 us  [along_z(): return lax.ppermute(value, 'tp', pairs)]
    all_to_all x1 -> x0, waiting for transfers between devices: 16 us -> none  [exchanged(): return lax.all_to_all(value, 'tp', 0, 0, tiled=True)]
    ppermute x2 -> x6, starting transfers between devices: 1.82 us -> 13.4 us  [across_x(): return lax.ppermute(value, 'tp', [(i, i ^ 1) for i in range(Z * X)])]
    ppermute x2 -> x6, waiting for transfers between devices: 11.1 us -> 20.3 us  [across_x(): return lax.ppermute(value, 'tp', [(i, i ^ 1) for i in range(Z * X)])]
    ppermute x12, starting transfers between devices: 1.63 us -> 10.8 us  [across_core(): return lax.ppermute(value, 'seq', [(i, i ^ 1) for i in range(Y * C)])]
    ppermute x9 -> x33, waiting for transfers between devices: 31.3 us -> 38.4 us  [along_z(): return lax.ppermute(value, 'tp', pairs)]
    all_to_all x1 -> x0, starting transfers between devices: 3.91 us -> none  [exchanged(): return lax.all_to_all(value, 'tp', 0, 0, tiled=True)]
  transfers between devices with their start and end apart: 36 -> 63, of which waited for: 24 -> 41; matrix products, arithmetic and copies ran while one was open for 1% -> 1% of each run, Pallas kernels for 1% -> 2%
where the time goes in v2:
time: 237 us; the launch traced here: 233 us
  starting transfers between devices  96.4 us (41%)
  waiting for transfers between devices  89.5 us (38%)
  Pallas kernels  33.2 us (14%)
  local copies, waits for them, and re-layouts  11 us (5%)
    ppermute x33, starting transfers between devices, along_z(): return lax.ppermute(value, 'tp', pairs)  45.6 us
    ppermute x33, waiting for transfers between devices, along_z(): return lax.ppermute(value, 'tp', pairs)  38.4 us
    ppermute x6, waiting for transfers between devices, across_x(): return lax.ppermute(value, 'tp', [(i, i ^ 1) for i in range(Z * X)])  20.3 us
    ppermute x9, waiting for transfers between devices, along_y(): return lax.ppermute(value, 'seq', pairs)  17.4 us
    ppermute x9, starting transfers between devices, along_y(): return lax.ppermute(value, 'seq', pairs)  14.1 us
    pallas_call x2, Pallas kernels, rest_of_layer(): call(attend, 'attend', [SMEM] * 2 + [VMEM] * 21, [row_bf16] * 8, [pltpu.V...  13.9 us
    ppermute x6, starting transfers between devices, across_x(): return lax.ppermute(value, 'tp', [(i, i ^ 1) for i in range(Z * X)])  13.4 us
    ppermute x12, starting transfers between devices, across_core(): return lax.ppermute(value, 'seq', [(i, i ^ 1) for i in range(Y * C)])  10.8 us
  transfers between devices with their start and end apart: 63, of which 41 were waited for; matrix products, arithmetic and copies ran while one was open for 1% of the time, Pallas kernels for 2%

profile of v2, /device:TPU:0, one launch (start us, length us, event | category | flops | bytes accessed | tf_op | source)
XLA Modules:
  0.0 232.9 jit_solution(8628789899201829028)
XLA Ops:
  2.5 3.4 %collective-permute-start.12 = (bf16[2,480,128]{2,1,0:T(8,128)(2,1)S(1)}, bf16[2,480,128]{2,1,0:T(8,128)(2,1)}, u32[]{:S(2)}, u32[]{:S(2)}) collective-permute-start(bf16[2,480,128]{2,1,0:T(8,128)(2,1)S(1)} %pack_stale.1.refs_8_), channel_id=1, source_target_pairs={{0,32},{8,40},{16,48},{24,56},{32,0},{40,8},{48,16},{56,24},{1,33}... | collective-permute-start | bytes 737288 | tf_op jit(solution)/shard_map/ppermute | solution.py:53
  8.6 4.9 %project_first.1 = (bf16[256,192]{1,0:T(8,128)(2,1)}, f32[64,192]{1,0:T(8,128)}, bf16[2,480,128]{2,1,0:T(8,128)(2,1)}, bf16[64,384]{1,0:T(8,128)(2,1)}, bf16[40,1536]{1,0:T(8,128)(2,1)}) custom-call(s32[4]{0:T(128)} %pad_add_fusion.place, bf16[8,32,1536]{2,1,0:T(8,128)(2,1)} %bitcast.108, bf16[8,8,1536]{2,1,0:T(8,128)(2,1)} %bitcast.109, ...), custom_call_target="tpu_custom_call" | custom-call | tf_op jit(solution)/shard_map/project_first/pallas_call | solution.py:450
  19.4 4.7 %collective-permute-done.5.refs_6_ = bf16[2,480,128]{2,1,0:T(8,128)(2,1)} collective-permute-done((bf16[2,480,128]{2,1,0:T(8,128)(2,1)}, bf16[2,480,128]{2,1,0:T(8,128)(2,1)}, u32[]{:S(2)}, u32[]{:S(2)}) %collective-permute-start.5) | collective-permute-done | bytes 245792 | tf_op jit(solution)/shard_map/ppermute | solution.py:53
  24.1 4.5 %collective-permute-done.3.refs_4_ = bf16[2,480,128]{2,1,0:T(8,128)(2,1)} collective-permute-done((bf16[2,480,128]{2,1,0:T(8,128)(2,1)}, bf16[2,480,128]{2,1,0:T(8,128)(2,1)}, u32[]{:S(2)}, u32[]{:S(2)}) %collective-permute-start.3) | collective-permute-done | bytes 245792 | tf_op jit(solution)/shard_map/ppermute | solution.py:53
  35.3 7.3 %attend.2 = (bf16[40,1536]{1,0:T(8,128)(2,1)S(1)}, bf16[40,1536]{1,0:T(8,128)(2,1)S(1)}, bf16[40,1536]{1,0:T(8,128)(2,1)S(1)}, bf16[40,1536]{1,0:T(8,128)(2,1)S(...) custom-call(s32[4]{0:T(128)S(1)} %copy-done.21, ...), custom_call_target="tpu_custom_call" | custom-call | tf_op jit(solution)/shard_map/attend/pallas_call | solution.py:419
  42.6 4.0 %collective-permute-start.17 = (bf16[40,1536]{1,0:T(8,128)(2,1)S(1)}, bf16[40,1536]{1,0:T(8,128)(2,1)S(1)}, u32[]{:S(2)}, u32[]{:S(2)}) collective-permute-start(bf16[40,1536]{1,0:T(8,128)(2,1)S(1)} %get-tuple-element.60), channel_id=1, source_target_pairs={{0,4},{1,5},{2,6},{3,7},{4,0},{5,1},{6,2},{7,3},{8,12},{9,13},{10,... | collective-permute-start | bytes 368648 | tf_op jit(solution)/shard_map/ppermute | solution.py:44
  50.9 3.4 %collective-permute-start.16 = (bf16[40,1536]{1,0:T(8,128)(2,1)S(1)}, bf16[40,1536]{1,0:T(8,128)(2,1)S(1)}, u32[]{:S(2)}, u32[]{:S(2)}) collective-permute-start(bf16[40,1536]{1,0:T(8,128)(2,1)S(1)} %get-tuple-element.58), channel_id=1, source_target_pairs={{0,6},{1,7},{2,0},{3,1},{4,2},{5,3},{6,4},{7,5},{8,14},{9,15},{10,... | collective-permute-start | bytes 368648 | tf_op jit(solution)/shard_map/ppermute | solution.py:44
  64.8 3.7 %collective-permute-done.21 = bf16[40,1536]{1,0:T(8,128)(2,1)S(1)} collective-permute-done((bf16[40,1536]{1,0:T(8,128)(2,1)S(1)}, bf16[40,1536]{1,0:T(8,128)(2,1)S(1)}, u32[]{:S(2)}, u32[]{:S(2)}) %collective-permute-start.21) | collective-permute-done | bytes 122912 | tf_op jit(solution)/shard_map/ppermute | solution.py:48
  68.6 4.3 %collective-permute-start.24 = (bf16[2,40,1536]{2,1,0:T(8,128)(2,1)S(1)}, bf16[2,40,1536]{2,1,0:T(8,128)(2,1)S(1)}, u32[]{:S(2)}, u32[]{:S(2)}) collective-permute-start(bf16[2,40,1536]{2,1,0:T(8,128)(2,1)S(1)} %pad_maximum_fusion.p0), channel_id=1, source_target_pairs={{0,6},{1,7},{2,0},{3,1},{4,2},{5,3},{6,4},{7,5},{8,14},{9,15},{10,... | collective-permute-start | bytes 737288 | tf_op jit(solution)/shard_map/ppermute | solution.py:44
  73.8 5.4 %collective-permute-done.24.p3 = bf16[2,40,1536]{2,1,0:T(8,128)(2,1)S(1)} collective-permute-done((bf16[2,40,1536]{2,1,0:T(8,128)(2,1)S(1)}, bf16[2,40,1536]{2,1,0:T(8,128)(2,1)S(1)}, u32[]{:S(2)}, u32[]{:S(2)}) %collective-permute-start.24) | collective-permute-done | bytes 245792 | tf_op jit(solution)/shard_map/ppermute | solution.py:44
  82.9 3.1 %feed_forward.2 = (bf16[40,1536]{1,0:T(8,128)(2,1)S(1)}, bf16[40,1536]{1,0:T(8,128)(2,1)S(1)}, bf16[40,1536]{1,0:T(8,128)(2,1)S(1)}, bf16[40,1536]{1,0:T(8,128)(...) custom-call(s32[4]{0:T(128)S(1)} %copy-done.21, ...), custom_call_target="tpu_custom_call" | custom-call | tf_op jit(solution)/shard_map/feed_forward/pallas_call | solution.py:445
  95.0 3.0 %collective-permute-start.31 = (bf16[40,1536]{1,0:T(8,128)(2,1)S(1)}, bf16[40,1536]{1,0:T(8,128)(2,1)S(1)}, u32[]{:S(2)}, u32[]{:S(2)}) collective-permute-start(bf16[40,1536]{1,0:T(8,128)(2,1)S(1)} %add_far.5), channel_id=1, source_target_pairs={{0,1},{1,0},{2,3},{3,2},{4,5},{5,4},{6,7},{7,6},{8,9},{9,8},{10,11... | collective-permute-start | bytes 368648 | tf_op jit(solution)/shard_map/ppermute | solution.py:48
  98.1 3.7 %collective-permute-done.31.p4 = bf16[40,1536]{1,0:T(8,128)(2,1)S(1)} collective-permute-done((bf16[40,1536]{1,0:T(8,128)(2,1)S(1)}, bf16[40,1536]{1,0:T(8,128)(2,1)S(1)}, u32[]{:S(2)}, u32[]{:S(2)}) %collective-permute-start.31) | collective-permute-done | bytes 122912 | tf_op jit(solution)/shard_map/ppermute | solution.py:48
  102.5 4.4 %collective-permute-start.33 = (bf16[40,1536]{1,0:T(8,128)(2,1)S(1)}, bf16[40,1536]{1,0:T(8,128)(2,1)S(1)}, u32[]{:S(2)}, u32[]{:S(2)}) collective-permute-start(bf16[40,1536]{1,0:T(8,128)(2,1)S(1)} %after_mlp.1.refs_1_), channel_id=1, source_target_pairs={{0,65},{1,64},{2,67},{3,66},{4,69},{5,68},{6,71},{7,70},{8,73},{9,... | collective-permute-start | bytes 368648 | tf_op jit(solution)/shard_map/ppermute | solution.py:62
  113.9 5.4 %collective-permute-done.36.p3 = bf16[2,40,1536]{2,1,0:T(8,128)(2,1)S(1)} collective-permute-done((bf16[2,40,1536]{2,1,0:T(8,128)(2,1)S(1)}, bf16[2,40,1536]{2,1,0:T(8,128)(2,1)S(1)}, u32[]{:S(2)}, u32[]{:S(2)}) %collective-permute-start.36) | collective-permute-done | bytes 245792 | tf_op jit(solution)/shard_map/ppermute | solution.py:44
  129.6 3.6 %collective-permute-done.42.refs_6_ = bf16[2,480,128]{2,1,0:T(8,128)(2,1)S(1)} collective-permute-done((bf16[2,480,128]{2,1,0:T(8,128)(2,1)S(1)}, bf16[2,480,128]{2,1,0:T(8,128)(2,1)S(1)}, u32[]{:S(2)}, u32[]{:S(2)}) %collective-permute-start.42) | collective-permute-done | bytes 245792 | tf_op jit(solution)/shard_map/ppermute | solution.py:53
  136.6 9.6 %collective-permute-start.39 = (bf16[2,480,128]{2,1,0:T(8,128)(2,1)S(1)}, bf16[2,480,128]{2,1,0:T(8,128)(2,1)S(1)}, u32[]{:S(2)}, u32[]{:S(2)}) collective-permute-start(bf16[2,480,128]{2,1,0:T(8,128)(2,1)S(1)} %collective-permute-done.38.refs_2_), channel_id=1, source_target_pairs={{0,8},{8,0},{16,24},{24,16},{32,40},{40,32},{48,56},{56,48},{1,9},... | collective-permute-start | bytes 737288 | tf_op jit(solution)/shard_map/ppermute | solution.py:57
  147.8 6.7 %attend.3 = (bf16[40,1536]{1,0:T(8,128)(2,1)S(1)}, bf16[40,1536]{1,0:T(8,128)(2,1)S(1)}, bf16[40,1536]{1,0:T(8,128)(2,1)S(1)}, bf16[40,1536]{1,0:T(8,128)(2,1)S(...) custom-call(s32[4]{0:T(128)S(1)} %copy-done.21, ...), custom_call_target="tpu_custom_call" | custom-call | tf_op jit(solution)/shard_map/attend/pallas_call | solution.py:419
  174.3 4.9 %collective-permute-done.51 = bf16[40,1536]{1,0:T(8,128)(2,1)S(1)} collective-permute-done((bf16[40,1536]{1,0:T(8,128)(2,1)S(1)}, bf16[40,1536]{1,0:T(8,128)(2,1)S(1)}, u32[]{:S(2)}, u32[]{:S(2)}) %collective-permute-start.51) | collective-permute-done | bytes 122912 | tf_op jit(solution)/shard_map/ppermute | solution.py:48
  182.2 3.8 %collective-permute-done.54.p3 = bf16[2,40,1536]{2,1,0:T(8,128)(2,1)S(1)} collective-permute-done((bf16[2,40,1536]{2,1,0:T(8,128)(2,1)S(1)}, bf16[2,40,1536]{2,1,0:T(8,128)(2,1)S(1)}, u32[]{:S(2)}, u32[]{:S(2)}) %collective-permute-start.54) | collective-permute-done | bytes 245792 | tf_op jit(solution)/shard_map/ppermute | solution.py:44
  190.5 3.8 %feed_forward.3 = (bf16[40,1536]{1,0:T(8,128)(2,1)S(1)}, bf16[40,1536]{1,0:T(8,128)(2,1)S(1)}, bf16[40,1536]{1,0:T(8,128)(2,1)S(1)}, bf16[40,1536]{1,0:T(8,128)(...) custom-call(s32[4]{0:T(128)S(1)} %copy-done.21, ...), custom_call_target="tpu_custom_call" | custom-call | tf_op jit(solution)/shard_map/feed_forward/pallas_call | solution.py:445
  198.7 3.0 %collective-permute-start.60 = (bf16[40,1536]{1,0:T(8,128)(2,1)}, bf16[40,1536]{1,0:T(8,128)(2,1)S(1)}, u32[]{:S(2)}, u32[]{:S(2)}) collective-permute-start(bf16[40,1536]{1,0:T(8,128)(2,1)} %get-tuple-element.93), channel_id=1, source_target_pairs={{0,6},{1,7},{2,0},{3,1},{4,2},{5,3},{6,4},{7,5},{8,14},{9,15},{10,... | collective-permute-start | bytes 368648 | tf_op jit(solution)/shard_map/ppermute | solution.py:44
  215.2 6.8 %all-to-all-start = ((bf16[16,8,1792]{2,1,0:T(8,128)(2,1)}), bf16[16,8,1792]{2,1,0:T(8,128)(2,1)S(1)}, u32[]{:S(2)}, u32[]{:S(2)}) async-start(bf16[16,8,1792]{2,1,0:T(8,128)(2,1)} %broadcast_in_dim.28), calls=%async_computation | async-start | bytes 917504 | tf_op jit(solution)/shard_map/all_to_all | solution.py:478
  223.4 7.9 %all-to-all-done.received = bf16[16,8,1792]{2,1,0:T(8,128)(2,1)S(1)} async-done(((bf16[16,8,1792]{2,1,0:T(8,128)(2,1)}), bf16[16,8,1792]{2,1,0:T(8,128)(2,1)S(1)}, u32[]{:S(2)}, u32[]{:S(2)}) %all-to-all-start) | async-done | bytes 458784 | tf_op jit(solution)/shard_map/all_to_all | solution.py:478
  (199 shorter events, 116.2 us)
Async XLA Ops:
  2.5 11.7 %collective-permute-start.12 = (bf16[2,480,128]{2,1,0:T(8,128)(2,1)S(1)}, bf16[2,480,128]{2,1,0:T(8,128)(2,1)}, u32[]{:S(2)}, u32[]{:S(2)}) collective-permute-start(bf16[2,480,128]{2,1,0:T(8,128)(2,1)S(1)} %pack_stale.1.refs_8_), channel_id=1, source_target_pairs={{0,32},{8,40},{16,48},{24,56},{32,0},{40,8},{48,16},{56,24},{1,33}... | collective-permute-start | bytes 737288 | tf_op jit(solution)/shard_map/ppermute | solution.py:53
  5.9 11.8 %collective-permute-start.10 = (bf16[2,480,128]{2,1,0:T(8,128)(2,1)S(1)}, bf16[2,480,128]{2,1,0:T(8,128)(2,1)}, u32[]{:S(2)}, u32[]{:S(2)}) collective-permute-start(bf16[2,480,128]{2,1,0:T(8,128)(2,1)S(1)} %pack_stale.1.refs_8_), channel_id=1, source_target_pairs={{0,48},{8,56},{16,0},{24,8},{32,16},{40,24},{48,32},{56,40},{1,49}... | collective-permute-start | bytes 737288 | tf_op jit(solution)/shard_map/ppermute | solution.py:53
  6.9 11.9 %collective-permute-start.8 = (bf16[2,480,128]{2,1,0:T(8,128)(2,1)S(1)}, bf16[2,480,128]{2,1,0:T(8,128)(2,1)}, u32[]{:S(2)}, u32[]{:S(2)}) collective-permute-start(bf16[2,480,128]{2,1,0:T(8,128)(2,1)S(1)} %pack_stale.1.refs_8_), channel_id=1, source_target_pairs={{0,16},{8,24},{16,32},{24,40},{32,48},{40,56},{48,0},{56,8},{1,17}... | collective-permute-start | bytes 737288 | tf_op jit(solution)/shard_map/ppermute | solution.py:53
  7.9 10.9 %collective-permute-start.7 = (bf16[2,480,128]{2,1,0:T(8,128)(2,1)S(1)}, bf16[2,480,128]{2,1,0:T(8,128)(2,1)}, u32[]{:S(2)}, u32[]{:S(2)}) collective-permute-start(bf16[2,480,128]{2,1,0:T(8,128)(2,1)S(1)} %pack_stale.1.refs_8_), channel_id=1, source_target_pairs={{0,8},{8,0},{16,24},{24,16},{32,40},{40,32},{48,56},{56,48},{1,9},... | collective-permute-start | bytes 737288 | tf_op jit(solution)/shard_map/ppermute | solution.py:57
  13.5 10.6 %collective-permute-start.5 = (bf16[2,480,128]{2,1,0:T(8,128)(2,1)}, bf16[2,480,128]{2,1,0:T(8,128)(2,1)}, u32[]{:S(2)}, u32[]{:S(2)}) collective-permute-start(bf16[2,480,128]{2,1,0:T(8,128)(2,1)} %get-tuple-element.54.refs_0_), channel_id=1, source_target_pairs={{0,32},{8,40},{16,48},{24,56},{32,0},{40,8},{48,16},{56,24},{1,33}... | collective-permute-start | bytes 737288 | tf_op jit(solution)/shard_map/ppermute | solution.py:53
  14.2 14.4 %collective-permute-start.3 = (bf16[2,480,128]{2,1,0:T(8,128)(2,1)}, bf16[2,480,128]{2,1,0:T(8,128)(2,1)}, u32[]{:S(2)}, u32[]{:S(2)}) collective-permute-start(bf16[2,480,128]{2,1,0:T(8,128)(2,1)} %get-tuple-element.54.refs_0_), channel_id=1, source_target_pairs={{0,48},{8,56},{16,0},{24,8},{32,16},{40,24},{48,32},{56,40},{1,49}... | collective-permute-start | bytes 737288 | tf_op jit(solution)/shard_map/ppermute | solution.py:53
  17.7 11.3 %collective-permute-start.1 = (bf16[2,480,128]{2,1,0:T(8,128)(2,1)}, bf16[2,480,128]{2,1,0:T(8,128)(2,1)}, u32[]{:S(2)}, u32[]{:S(2)}) collective-permute-start(bf16[2,480,128]{2,1,0:T(8,128)(2,1)} %get-tuple-element.54.refs_0_), channel_id=1, source_target_pairs={{0,16},{8,24},{16,32},{24,40},{32,48},{40,56},{48,0},{56,8},{1,17}... | collective-permute-start | bytes 737288 | tf_op jit(solution)/shard_map/ppermute | solution.py:53
  18.8 10.2 %collective-permute-start = (bf16[2,480,128]{2,1,0:T(8,128)(2,1)}, bf16[2,480,128]{2,1,0:T(8,128)(2,1)}, u32[]{:S(2)}, u32[]{:S(2)}) collective-permute-start(bf16[2,480,128]{2,1,0:T(8,128)(2,1)} %get-tuple-element.54.refs_0_), channel_id=1, source_target_pairs={{0,8},{8,0},{16,24},{24,16},{32,40},{40,32},{48,56},{56,48},{1,9},... | collective-permute-start | bytes 737288 | tf_op jit(solution)/shard_map/ppermute | solution.py:57
  18.9 10.6 %collective-permute-start.13 = (bf16[2,480,128]{2,1,0:T(8,128)(2,1)}, bf16[2,480,128]{2,1,0:T(8,128)(2,1)}, u32[]{:S(2)}, u32[]{:S(2)}) collective-permute-start(bf16[2,480,128]{2,1,0:T(8,128)(2,1)} %collective-permute-done.12.refs_14_), channel_id=1, source_target_pairs={{0,8},{8,0},{16,24},{24,16},{32,40},{40,32},{48,56},{56,48},{1,9},... | collective-permute-start | bytes 737288 | tf_op jit(solution)/shard_map/ppermute | solution.py:57
  68.6 10.6 %collective-permute-start.24 = (bf16[2,40,1536]{2,1,0:T(8,128)(2,1)S(1)}, bf16[2,40,1536]{2,1,0:T(8,128)(2,1)S(1)}, u32[]{:S(2)}, u32[]{:S(2)}) collective-permute-start(bf16[2,40,1536]{2,1,0:T(8,128)(2,1)S(1)} %pad_maximum_fusion.p0), channel_id=1, source_target_pairs={{0,6},{1,7},{2,0},{3,1},{4,2},{5,3},{6,4},{7,5},{8,14},{9,15},{10,... | collective-permute-start | bytes 737288 | tf_op jit(solution)/shard_map/ppermute | solution.py:44
  72.9 10.0 %collective-permute-start.22 = (bf16[2,40,1536]{2,1,0:T(8,128)(2,1)S(1)}, bf16[2,40,1536]{2,1,0:T(8,128)(2,1)S(1)}, u32[]{:S(2)}, u32[]{:S(2)}) collective-permute-start(bf16[2,40,1536]{2,1,0:T(8,128)(2,1)S(1)} %pad_maximum_fusion.p0), channel_id=1, source_target_pairs={{0,2},{1,3},{2,4},{3,5},{4,6},{5,7},{6,0},{7,1},{8,10},{9,11},{10,... | collective-permute-start | bytes 737288 | tf_op jit(solution)/shard_map/ppermute | solution.py:44
  86.5 8.5 %collective-permute-start.29 = (bf16[40,1536]{1,0:T(8,128)(2,1)S(1)}, bf16[40,1536]{1,0:T(8,128)(2,1)S(1)}, u32[]{:S(2)}, u32[]{:S(2)}) collective-permute-start(bf16[40,1536]{1,0:T(8,128)(2,1)S(1)} %get-tuple-element.71), channel_id=1, source_target_pairs={{0,2},{1,3},{2,4},{3,5},{4,6},{5,7},{6,0},{7,1},{8,10},{9,11},{10,... | collective-permute-start | bytes 368648 | tf_op jit(solution)/shard_map/ppermute | solution.py:44
  110.7 8.6 %collective-permute-start.36 = (bf16[2,40,1536]{2,1,0:T(8,128)(2,1)S(1)}, bf16[2,40,1536]{2,1,0:T(8,128)(2,1)S(1)}, u32[]{:S(2)}, u32[]{:S(2)}) collective-permute-start(bf16[2,40,1536]{2,1,0:T(8,128)(2,1)S(1)} %pad_maximum_fusion.1.p0), channel_id=1, source_target_pairs={{0,6},{1,7},{2,0},{3,1},{4,2},{5,3},{6,4},{7,5},{8,14},{9,15},{10,... | collective-permute-start | bytes 737288 | tf_op jit(solution)/shard_map/ppermute | solution.py:44
  112.9 10.0 %collective-permute-start.34 = (bf16[2,40,1536]{2,1,0:T(8,128)(2,1)S(1)}, bf16[2,40,1536]{2,1,0:T(8,128)(2,1)S(1)}, u32[]{:S(2)}, u32[]{:S(2)}) collective-permute-start(bf16[2,40,1536]{2,1,0:T(8,128)(2,1)S(1)} %pad_maximum_fusion.1.p0), channel_id=1, source_target_pairs={{0,2},{1,3},{2,4},{3,5},{4,6},{5,7},{6,0},{7,1},{8,10},{9,11},{10,... | collective-permute-start | bytes 737288 | tf_op jit(solution)/shard_map/ppermute | solution.py:44
  129.6 16.7 %collective-permute-start.37 = (bf16[2,480,128]{2,1,0:T(8,128)(2,1)S(1)}, bf16[2,480,128]{2,1,0:T(8,128)(2,1)S(1)}, u32[]{:S(2)}, u32[]{:S(2)}) collective-permute-start(bf16[2,480,128]{2,1,0:T(8,128)(2,1)S(1)} %get-tuple-element.75.refs_0_), channel_id=1, source_target_pairs={{0,8},{8,0},{16,24},{24,16},{32,40},{40,32},{48,56},{56,48},{1,9},... | collective-permute-start | bytes 737288 | tf_op jit(solution)/shard_map/ppermute | solution.py:57
  133.2 13.1 %collective-permute-start.43 = (bf16[2,480,128]{2,1,0:T(8,128)(2,1)S(1)}, bf16[2,480,128]{2,1,0:T(8,128)(2,1)S(1)}, u32[]{:S(2)}, u32[]{:S(2)}) collective-permute-start(bf16[2,480,128]{2,1,0:T(8,128)(2,1)S(1)} %collective-permute-done.42.refs_6_), channel_id=1, source_target_pairs={{0,8},{8,0},{16,24},{24,16},{32,40},{40,32},{48,56},{56,48},{1,9},... | collective-permute-start | bytes 737288 | tf_op jit(solution)/shard_map/ppermute | solution.py:57
  135.8 10.5 %collective-permute-start.41 = (bf16[2,480,128]{2,1,0:T(8,128)(2,1)S(1)}, bf16[2,480,128]{2,1,0:T(8,128)(2,1)S(1)}, u32[]{:S(2)}, u32[]{:S(2)}) collective-permute-start(bf16[2,480,128]{2,1,0:T(8,128)(2,1)S(1)} %collective-permute-done.40.refs_4_), channel_id=1, source_target_pairs={{0,8},{8,0},{16,24},{24,16},{32,40},{40,32},{48,56},{56,48},{1,9},... | collective-permute-start | bytes 737288 | tf_op jit(solution)/shard_map/ppermute | solution.py:57
  136.6 11.2 %collective-permute-start.39 = (bf16[2,480,128]{2,1,0:T(8,128)(2,1)S(1)}, bf16[2,480,128]{2,1,0:T(8,128)(2,1)S(1)}, u32[]{:S(2)}, u32[]{:S(2)}) collective-permute-start(bf16[2,480,128]{2,1,0:T(8,128)(2,1)S(1)} %collective-permute-done.38.refs_2_), channel_id=1, source_target_pairs={{0,8},{8,0},{16,24},{24,16},{32,40},{40,32},{48,56},{56,48},{1,9},... | collective-permute-start | bytes 737288 | tf_op jit(solution)/shard_map/ppermute | solution.py:57
  154.9 10.5 %collective-permute-start.48 = (bf16[40,1536]{1,0:T(8,128)(2,1)S(1)}, bf16[40,1536]{1,0:T(8,128)(2,1)S(1)}, u32[]{:S(2)}, u32[]{:S(2)}) collective-permute-start(bf16[40,1536]{1,0:T(8,128)(2,1)S(1)} %get-tuple-element.82), channel_id=1, source_target_pairs={{0,2},{1,3},{2,4},{3,5},{4,6},{5,7},{6,0},{7,1},{8,10},{9,11},{10,... | collective-permute-start | bytes 368648 | tf_op jit(solution)/shard_map/ppermute | solution.py:44
  156.3 9.0 %collective-permute-start.49 = (bf16[40,1536]{1,0:T(8,128)(2,1)S(1)}, bf16[40,1536]{1,0:T(8,128)(2,1)S(1)}, u32[]{:S(2)}, u32[]{:S(2)}) collective-permute-start(bf16[40,1536]{1,0:T(8,128)(2,1)S(1)} %get-tuple-element.83), channel_id=1, source_target_pairs={{0,6},{1,7},{2,0},{3,1},{4,2},{5,3},{6,4},{7,5},{8,14},{9,15},{10,... | collective-permute-start | bytes 368648 | tf_op jit(solution)/shard_map/ppermute | solution.py:44
  158.1 9.4 %collective-permute-start.44 = (bf16[40,1536]{1,0:T(8,128)(2,1)S(1)}, bf16[40,1536]{1,0:T(8,128)(2,1)S(1)}, u32[]{:S(2)}, u32[]{:S(2)}) collective-permute-start(bf16[40,1536]{1,0:T(8,128)(2,1)S(1)} %get-tuple-element.77), channel_id=1, source_target_pairs={{0,4},{1,5},{2,6},{3,7},{4,0},{5,1},{6,2},{7,3},{8,12},{9,13},{10,... | collective-permute-start | bytes 368648 | tf_op jit(solution)/shard_map/ppermute | solution.py:44
  160.1 9.0 %collective-permute-start.45 = (bf16[40,1536]{1,0:T(8,128)(2,1)S(1)}, bf16[40,1536]{1,0:T(8,128)(2,1)S(1)}, u32[]{:S(2)}, u32[]{:S(2)}) collective-permute-start(bf16[40,1536]{1,0:T(8,128)(2,1)S(1)} %get-tuple-element.78), channel_id=1, source_target_pairs={{0,2},{1,3},{2,4},{3,5},{4,6},{5,7},{6,0},{7,1},{8,10},{9,11},{10,... | collective-permute-start | bytes 368648 | tf_op jit(solution)/shard_map/ppermute | solution.py:44
  181.6 8.9 %collective-permute-start.52 = (bf16[2,40,1536]{2,1,0:T(8,128)(2,1)S(1)}, bf16[2,40,1536]{2,1,0:T(8,128)(2,1)S(1)}, u32[]{:S(2)}, u32[]{:S(2)}) collective-permute-start(bf16[2,40,1536]{2,1,0:T(8,128)(2,1)S(1)} %pad_maximum_fusion.2.p0), channel_id=1, source_target_pairs={{0,2},{1,3},{2,4},{3,5},{4,6},{5,7},{6,0},{7,1},{8,10},{9,11},{10,... | collective-permute-start | bytes 737288 | tf_op jit(solution)/shard_map/ppermute | solution.py:44
  215.2 16.2 %all-to-all-start = ((bf16[16,8,1792]{2,1,0:T(8,128)(2,1)}), bf16[16,8,1792]{2,1,0:T(8,128)(2,1)S(1)}, u32[]{:S(2)}, u32[]{:S(2)}) async-start(bf16[16,8,1792]{2,1,0:T(8,128)(2,1)} %broadcast_in_dim.28), calls=%async_computation | async-start | bytes 917504 | tf_op jit(solution)/shard_map/all_to_all | solution.py:478
  (72 other events, 1044.4 us)

commit v3 on v2

--- a/solution.py
+++ b/solution.py
@@ -274,24 +274,39 @@
 
 
 def feed_forward(place, p0, p1, p2, p3, up_image, down_image, up_text, down_text, *refs):
-    outs, (image_rows, text_rows) = refs[:8], refs[8:]
+    outs, (image_rows, text_rows, image_hidden, text_hidden) = refs[:8], refs[8:]
     for d, piece in enumerate((p0, p1, p2, p3)):
         for flip in range(X):
             at = d * X + flip
             image_rows[at * PT : (at + 1) * PT, :] = piece[flip, 0:PT, :]
             text_rows[at * TQ : (at + 1) * TQ, :] = piece[flip, PT:ROWS, :].astype(F32)
-    hidden = jax.nn.gelu(mm(image_rows[...], up_image[...]), approximate=True).astype(BF16)
-    image = mm(hidden, down_image[...])
-    hidden = jax.nn.gelu(
-        mm(text_rows[...].astype(BF16), up_text[...]), approximate=True
-    ).astype(BF16)
-    text = mm(hidden, down_text[...])
-    for d in range(Z):
-        for flip in range(X):
-            at = d * X + flip
-            out = outs[(Z - d) % Z * X + flip]
-            out[0:PT, :] = image[at * PT : (at + 1) * PT].astype(BF16)
-            out[PT:ROWS, :] = text[at * TQ : (at + 1) * TQ].astype(BF16)
+    hidden_width, d_model = down_image.shape
+    block = hidden_width // 3
+
+    @pl.loop(0, hidden_width // block)
+    def _(j):
+        lanes = pl.ds(pl.multiple_of(j * block, block), block)
+        for rows, up, hidden in (
+            (image_rows, up_image, image_hidden),
+            (text_rows, up_text, text_hidden),
+        ):
+            hidden[:, lanes] = jax.nn.gelu(
+                mm(rows[...].astype(BF16), up[:, lanes]), approximate=True
+            ).astype(BF16)
+
+    wide = d_model // 3
+
+    @pl.loop(0, d_model // wide)
+    def _(j):
+        lanes = pl.ds(pl.multiple_of(j * wide, wide), wide)
+        image = mm(image_hidden[...], down_image[:, lanes])
+        text = mm(text_hidden[...], down_text[:, lanes])
+        for d in range(Z):
+            for flip in range(X):
+                at = d * X + flip
+                out = outs[(Z - d) % Z * X + flip]
+                out[0:PT, lanes] = image[at * PT : (at + 1) * PT].astype(BF16)
+                out[PT:ROWS, lanes] = text[at * TQ : (at + 1) * TQ].astype(BF16)
 
 
 def layer_rows(place, h1, parts, mod_image, mod_text):
@@ -443,7 +458,15 @@
         )(place, rows, *exchanged(partial), *mods)
         pieces = spread_z(jnp.stack([b, across_x(b)]))
         partial = call(
-            feed_forward, "feed_forward", [SMEM] + [VMEM] * 8, [row_bf16] * 8, rows_scratch
+            feed_forward,
+            "feed_forward",
+            [SMEM] + [VMEM] * 8,
+            [row_bf16] * 8,
+            rows_scratch
+            + [
+                pltpu.VMEM((CHUNKS * PT, up_image.shape[2]), BF16),
+                pltpu.VMEM((CHUNKS * TQ, up_image.shape[2]), BF16),
+            ],
         )(place, *pieces, up_image[0], down_image[0], up_text[0], down_text[0])
         return h1, exchanged(partial)
 

time: 237 us -> 225 us (0.949); the launches traced: 233 us -> 224 us
  starting transfers between devices: 96.4 us -> 88.1 us
    ppermute x12, starting transfers between devices: 10.8 us -> 1.19 us  [across_core(): return lax.ppermute(value, 'seq', [(i, i ^ 1) for i in range(Y * C)])]
where the time goes in v3:
time: 225 us; the launch traced here: 224 us
  waiting for transfers between devices  88.3 us (39%)
  starting transfers between devices  88.1 us (39%)
  Pallas kernels  34.4 us (15%)
  local copies, waits for them, and re-layouts  11 us (5%)
    ppermute x33, starting transfers between devices, along_z(): return lax.ppermute(value, 'tp', pairs)  45.9 us
    ppermute x33, waiting for transfers between devices, along_z(): return lax.ppermute(value, 'tp', pairs)  38 us
    ppermute x6, waiting for transfers between devices, across_x(): return lax.ppermute(value, 'tp', [(i, i ^ 1) for i in range(Z * X)])  19.4 us
    ppermute x9, waiting for transfers between devices, along_y(): return lax.ppermute(value, 'seq', pairs)  17.4 us
    ppermute x6, starting transfers between devices, across_x(): return lax.ppermute(value, 'tp', [(i, i ^ 1) for i in range(Z * X)])  14.3 us
    ppermute x9, starting transfers between devices, along_y(): return lax.ppermute(value, 'seq', pairs)  14.2 us
    pallas_call x2, Pallas kernels, rest_of_layer(): call(attend, 'attend', [SMEM] * 2 + [VMEM] * 21, [row_bf16] * 8, [pltpu.V...  13.9 us
    unnamed x66, local copies, waits for them, and re-layouts  8.26 us
  transfers between devices with their start and end apart: 63, of which 41 were waited for; matrix products, arithmetic and copies ran while one was open for 1% of the time, Pallas kernels for 2%

profile of v3, /device:TPU:0, one launch (start us, length us, event | category | flops | bytes accessed | tf_op | source)
XLA Modules:
  0.0 224.2 jit_solution(8708379822233116499)
XLA Ops:
  2.5 3.4 %collective-permute-start.12 = (bf16[2,480,128]{2,1,0:T(8,128)(2,1)S(1)}, bf16[2,480,128]{2,1,0:T(8,128)(2,1)}, u32[]{:S(2)}, u32[]{:S(2)}) collective-permute-start(bf16[2,480,128]{2,1,0:T(8,128)(2,1)S(1)} %pack_stale.1.refs_8_), channel_id=1, source_target_pairs={{0,32},{8,40},{16,48},{24,56},{32,0},{40,8},{48,16},{56,24},{1,33}... | collective-permute-start | bytes 737288 | tf_op jit(solution)/shard_map/ppermute | solution.py:53
  8.6 4.9 %project_first.1 = (bf16[256,192]{1,0:T(8,128)(2,1)}, f32[64,192]{1,0:T(8,128)}, bf16[2,480,128]{2,1,0:T(8,128)(2,1)}, bf16[64,384]{1,0:T(8,128)(2,1)}, bf16[40,1536]{1,0:T(8,128)(2,1)}) custom-call(s32[4]{0:T(128)} %pad_add_fusion.place, bf16[8,32,1536]{2,1,0:T(8,128)(2,1)} %bitcast.108, bf16[8,8,1536]{2,1,0:T(8,128)(2,1)} %bitcast.109, ...), custom_call_target="tpu_custom_call" | custom-call | tf_op jit(solution)/shard_map/project_first/pallas_call | solution.py:473
  19.4 4.7 %collective-permute-done.5.refs_6_ = bf16[2,480,128]{2,1,0:T(8,128)(2,1)} collective-permute-done((bf16[2,480,128]{2,1,0:T(8,128)(2,1)}, bf16[2,480,128]{2,1,0:T(8,128)(2,1)}, u32[]{:S(2)}, u32[]{:S(2)}) %collective-permute-start.5) | collective-permute-done | bytes 245792 | tf_op jit(solution)/shard_map/ppermute | solution.py:53
  24.1 4.5 %collective-permute-done.3.refs_4_ = bf16[2,480,128]{2,1,0:T(8,128)(2,1)} collective-permute-done((bf16[2,480,128]{2,1,0:T(8,128)(2,1)}, bf16[2,480,128]{2,1,0:T(8,128)(2,1)}, u32[]{:S(2)}, u32[]{:S(2)}) %collective-permute-start.3) | collective-permute-done | bytes 245792 | tf_op jit(solution)/shard_map/ppermute | solution.py:53
  35.3 7.3 %attend.2 = (bf16[40,1536]{1,0:T(8,128)(2,1)S(1)}, bf16[40,1536]{1,0:T(8,128)(2,1)S(1)}, bf16[40,1536]{1,0:T(8,128)(2,1)S(1)}, bf16[40,1536]{1,0:T(8,128)(2,1)S(...) custom-call(s32[4]{0:T(128)S(1)} %copy-done.21, ...), custom_call_target="tpu_custom_call" | custom-call | tf_op jit(solution)/shard_map/attend/pallas_call | solution.py:434
  42.6 4.0 %collective-permute-start.17 = (bf16[40,1536]{1,0:T(8,128)(2,1)S(1)}, bf16[40,1536]{1,0:T(8,128)(2,1)S(1)}, u32[]{:S(2)}, u32[]{:S(2)}) collective-permute-start(bf16[40,1536]{1,0:T(8,128)(2,1)S(1)} %get-tuple-element.60), channel_id=1, source_target_pairs={{0,4},{1,5},{2,6},{3,7},{4,0},{5,1},{6,2},{7,3},{8,12},{9,13},{10,... | collective-permute-start | bytes 368648 | tf_op jit(solution)/shard_map/ppermute | solution.py:44
  50.6 3.7 %collective-permute-start.16 = (bf16[40,1536]{1,0:T(8,128)(2,1)S(1)}, bf16[40,1536]{1,0:T(8,128)(2,1)S(1)}, u32[]{:S(2)}, u32[]{:S(2)}) collective-permute-start(bf16[40,1536]{1,0:T(8,128)(2,1)S(1)} %get-tuple-element.58), channel_id=1, source_target_pairs={{0,6},{1,7},{2,0},{3,1},{4,2},{5,3},{6,4},{7,5},{8,14},{9,15},{10,... | collective-permute-start | bytes 368648 | tf_op jit(solution)/shard_map/ppermute | solution.py:44
  54.4 3.1 %collective-permute-start.20 = (bf16[40,1536]{1,0:T(8,128)(2,1)S(1)}, bf16[40,1536]{1,0:T(8,128)(2,1)S(1)}, u32[]{:S(2)}, u32[]{:S(2)}) collective-permute-start(bf16[40,1536]{1,0:T(8,128)(2,1)S(1)} %add_far.4), channel_id=1, source_target_pairs={{0,1},{1,0},{2,3},{3,2},{4,5},{5,4},{6,7},{7,6},{8,9},{9,8},{10,11... | collective-permute-start | bytes 368648 | tf_op jit(solution)/shard_map/ppermute | solution.py:48
  61.7 3.1 %collective-permute-start.21 = (bf16[40,1536]{1,0:T(8,128)(2,1)S(1)}, bf16[40,1536]{1,0:T(8,128)(2,1)S(1)}, u32[]{:S(2)}, u32[]{:S(2)}) collective-permute-start(bf16[40,1536]{1,0:T(8,128)(2,1)S(1)} %get-tuple-element.64), channel_id=1, source_target_pairs={{0,1},{1,0},{2,3},{3,2},{4,5},{5,4},{6,7},{7,6},{8,9},{9,8},{10,11... | collective-permute-start | bytes 368648 | tf_op jit(solution)/shard_map/ppermute | solution.py:48
  64.9 3.3 %collective-permute-done.21 = bf16[40,1536]{1,0:T(8,128)(2,1)S(1)} collective-permute-done((bf16[40,1536]{1,0:T(8,128)(2,1)S(1)}, bf16[40,1536]{1,0:T(8,128)(2,1)S(1)}, u32[]{:S(2)}, u32[]{:S(2)}) %collective-permute-start.21) | collective-permute-done | bytes 122912 | tf_op jit(solution)/shard_map/ppermute | solution.py:48
  68.2 4.6 %collective-permute-start.24 = (bf16[2,40,1536]{2,1,0:T(8,128)(2,1)S(1)}, bf16[2,40,1536]{2,1,0:T(8,128)(2,1)S(1)}, u32[]{:S(2)}, u32[]{:S(2)}) collective-permute-start(bf16[2,40,1536]{2,1,0:T(8,128)(2,1)S(1)} %pad_maximum_fusion.p0), channel_id=1, source_target_pairs={{0,6},{1,7},{2,0},{3,1},{4,2},{5,3},{6,4},{7,5},{8,14},{9,15},{10,... | collective-permute-start | bytes 737288 | tf_op jit(solution)/shard_map/ppermute | solution.py:44
  73.7 5.4 %collective-permute-done.24.p3 = bf16[2,40,1536]{2,1,0:T(8,128)(2,1)S(1)} collective-permute-done((bf16[2,40,1536]{2,1,0:T(8,128)(2,1)S(1)}, bf16[2,40,1536]{2,1,0:T(8,128)(2,1)S(1)}, u32[]{:S(2)}, u32[]{:S(2)}) %collective-permute-start.24) | collective-permute-done | bytes 245792 | tf_op jit(solution)/shard_map/ppermute | solution.py:44
  82.9 3.7 %feed_forward.2 = (bf16[40,1536]{1,0:T(8,128)(2,1)S(1)}, bf16[40,1536]{1,0:T(8,128)(2,1)S(1)}, bf16[40,1536]{1,0:T(8,128)(2,1)S(1)}, bf16[40,1536]{1,0:T(8,128)(...) custom-call(s32[4]{0:T(128)S(1)} %copy-done.21, ...), custom_call_target="tpu_custom_call" | custom-call | tf_op jit(solution)/shard_map/feed_forward/pallas_call | solution.py:460
  95.5 3.2 %collective-permute-start.31 = (bf16[40,1536]{1,0:T(8,128)(2,1)S(1)}, bf16[40,1536]{1,0:T(8,128)(2,1)S(1)}, u32[]{:S(2)}, u32[]{:S(2)}) collective-permute-start(bf16[40,1536]{1,0:T(8,128)(2,1)S(1)} %add_far.5), channel_id=1, source_target_pairs={{0,1},{1,0},{2,3},{3,2},{4,5},{5,4},{6,7},{7,6},{8,9},{9,8},{10,11... | collective-permute-start | bytes 368648 | tf_op jit(solution)/shard_map/ppermute | solution.py:48
  98.7 3.6 %collective-permute-done.31.p4 = bf16[40,1536]{1,0:T(8,128)(2,1)S(1)} collective-permute-done((bf16[40,1536]{1,0:T(8,128)(2,1)S(1)}, bf16[40,1536]{1,0:T(8,128)(2,1)S(1)}, u32[]{:S(2)}, u32[]{:S(2)}) %collective-permute-start.31) | collective-permute-done | bytes 122912 | tf_op jit(solution)/shard_map/ppermute | solution.py:48
  103.0 4.4 %collective-permute-start.33 = (bf16[40,1536]{1,0:T(8,128)(2,1)S(1)}, bf16[40,1536]{1,0:T(8,128)(2,1)S(1)}, u32[]{:S(2)}, u32[]{:S(2)}) collective-permute-start(bf16[40,1536]{1,0:T(8,128)(2,1)S(1)} %after_mlp.1.refs_1_), channel_id=1, source_target_pairs={{0,65},{1,64},{2,67},{3,66},{4,69},{5,68},{6,71},{7,70},{8,73},{9,... | collective-permute-start | bytes 368648 | tf_op jit(solution)/shard_map/ppermute | solution.py:62
  114.3 5.4 %collective-permute-done.36.p3 = bf16[2,40,1536]{2,1,0:T(8,128)(2,1)S(1)} collective-permute-done((bf16[2,40,1536]{2,1,0:T(8,128)(2,1)S(1)}, bf16[2,40,1536]{2,1,0:T(8,128)(2,1)S(1)}, u32[]{:S(2)}, u32[]{:S(2)}) %collective-permute-start.36) | collective-permute-done | bytes 245792 | tf_op jit(solution)/shard_map/ppermute | solution.py:44
  130.2 3.5 %collective-permute-done.42.refs_6_ = bf16[2,480,128]{2,1,0:T(8,128)(2,1)S(1)} collective-permute-done((bf16[2,480,128]{2,1,0:T(8,128)(2,1)S(1)}, bf16[2,480,128]{2,1,0:T(8,128)(2,1)S(1)}, u32[]{:S(2)}, u32[]{:S(2)}) %collective-permute-start.42) | collective-permute-done | bytes 245792 | tf_op jit(solution)/shard_map/ppermute | solution.py:53
  138.7 6.7 %attend.3 = (bf16[40,1536]{1,0:T(8,128)(2,1)S(1)}, bf16[40,1536]{1,0:T(8,128)(2,1)S(1)}, bf16[40,1536]{1,0:T(8,128)(2,1)S(1)}, bf16[40,1536]{1,0:T(8,128)(2,1)S(...) custom-call(s32[4]{0:T(128)S(1)} %copy-done.21, ...), custom_call_target="tpu_custom_call" | custom-call | tf_op jit(solution)/shard_map/attend/pallas_call | solution.py:434
  165.2 4.9 %collective-permute-done.51 = bf16[40,1536]{1,0:T(8,128)(2,1)S(1)} collective-permute-done((bf16[40,1536]{1,0:T(8,128)(2,1)S(1)}, bf16[40,1536]{1,0:T(8,128)(2,1)S(1)}, u32[]{:S(2)}, u32[]{:S(2)}) %collective-permute-start.51) | collective-permute-done | bytes 122912 | tf_op jit(solution)/shard_map/ppermute | solution.py:48
  173.1 3.8 %collective-permute-done.54.p3 = bf16[2,40,1536]{2,1,0:T(8,128)(2,1)S(1)} collective-permute-done((bf16[2,40,1536]{2,1,0:T(8,128)(2,1)S(1)}, bf16[2,40,1536]{2,1,0:T(8,128)(2,1)S(1)}, u32[]{:S(2)}, u32[]{:S(2)}) %collective-permute-start.54) | collective-permute-done | bytes 245792 | tf_op jit(solution)/shard_map/ppermute | solution.py:44
  181.4 4.4 %feed_forward.3 = (bf16[40,1536]{1,0:T(8,128)(2,1)S(1)}, bf16[40,1536]{1,0:T(8,128)(2,1)S(1)}, bf16[40,1536]{1,0:T(8,128)(2,1)S(1)}, bf16[40,1536]{1,0:T(8,128)(...) custom-call(s32[4]{0:T(128)S(1)} %copy-done.21, ...), custom_call_target="tpu_custom_call" | custom-call | tf_op jit(solution)/shard_map/feed_forward/pallas_call | solution.py:460
  206.7 6.8 %all-to-all-start = ((bf16[16,8,1792]{2,1,0:T(8,128)(2,1)}), bf16[16,8,1792]{2,1,0:T(8,128)(2,1)S(1)}, u32[]{:S(2)}, u32[]{:S(2)}) async-start(bf16[16,8,1792]{2,1,0:T(8,128)(2,1)} %broadcast_in_dim.28), calls=%async_computation | async-start | bytes 917504 | tf_op jit(solution)/shard_map/all_to_all | solution.py:501
  215.0 7.9 %all-to-all-done.received = bf16[16,8,1792]{2,1,0:T(8,128)(2,1)S(1)} async-done(((bf16[16,8,1792]{2,1,0:T(8,128)(2,1)}), bf16[16,8,1792]{2,1,0:T(8,128)(2,1)S(1)}, u32[]{:S(2)}, u32[]{:S(2)}) %all-to-all-start) | async-done | bytes 458784 | tf_op jit(solution)/shard_map/all_to_all | solution.py:501
  (199 shorter events, 112.9 us)
Async XLA Ops:
  2.5 11.7 %collective-permute-start.12 = (bf16[2,480,128]{2,1,0:T(8,128)(2,1)S(1)}, bf16[2,480,128]{2,1,0:T(8,128)(2,1)}, u32[]{:S(2)}, u32[]{:S(2)}) collective-permute-start(bf16[2,480,128]{2,1,0:T(8,128)(2,1)S(1)} %pack_stale.1.refs_8_), channel_id=1, source_target_pairs={{0,32},{8,40},{16,48},{24,56},{32,0},{40,8},{48,16},{56,24},{1,33}... | collective-permute-start | bytes 737288 | tf_op jit(solution)/shard_map/ppermute | solution.py:53
  5.9 11.8 %collective-permute-start.10 = (bf16[2,480,128]{2,1,0:T(8,128)(2,1)S(1)}, bf16[2,480,128]{2,1,0:T(8,128)(2,1)}, u32[]{:S(2)}, u32[]{:S(2)}) collective-permute-start(bf16[2,480,128]{2,1,0:T(8,128)(2,1)S(1)} %pack_stale.1.refs_8_), channel_id=1, source_target_pairs={{0,48},{8,56},{16,0},{24,8},{32,16},{40,24},{48,32},{56,40},{1,49}... | collective-permute-start | bytes 737288 | tf_op jit(solution)/shard_map/ppermute | solution.py:53
  6.9 11.9 %collective-permute-start.8 = (bf16[2,480,128]{2,1,0:T(8,128)(2,1)S(1)}, bf16[2,480,128]{2,1,0:T(8,128)(2,1)}, u32[]{:S(2)}, u32[]{:S(2)}) collective-permute-start(bf16[2,480,128]{2,1,0:T(8,128)(2,1)S(1)} %pack_stale.1.refs_8_), channel_id=1, source_target_pairs={{0,16},{8,24},{16,32},{24,40},{32,48},{40,56},{48,0},{56,8},{1,17}... | collective-permute-start | bytes 737288 | tf_op jit(solution)/shard_map/ppermute | solution.py:53
  7.9 10.9 %collective-permute-start.7 = (bf16[2,480,128]{2,1,0:T(8,128)(2,1)S(1)}, bf16[2,480,128]{2,1,0:T(8,128)(2,1)}, u32[]{:S(2)}, u32[]{:S(2)}) collective-permute-start(bf16[2,480,128]{2,1,0:T(8,128)(2,1)S(1)} %pack_stale.1.refs_8_), channel_id=1, source_target_pairs={{0,8},{8,0},{16,24},{24,16},{32,40},{40,32},{48,56},{56,48},{1,9},... | collective-permute-start | bytes 737288 | tf_op jit(solution)/shard_map/ppermute | solution.py:57
  13.5 10.6 %collective-permute-start.5 = (bf16[2,480,128]{2,1,0:T(8,128)(2,1)}, bf16[2,480,128]{2,1,0:T(8,128)(2,1)}, u32[]{:S(2)}, u32[]{:S(2)}) collective-permute-start(bf16[2,480,128]{2,1,0:T(8,128)(2,1)} %get-tuple-element.54.refs_0_), channel_id=1, source_target_pairs={{0,32},{8,40},{16,48},{24,56},{32,0},{40,8},{48,16},{56,24},{1,33}... | collective-permute-start | bytes 737288 | tf_op jit(solution)/shard_map/ppermute | solution.py:53
  14.2 14.4 %collective-permute-start.3 = (bf16[2,480,128]{2,1,0:T(8,128)(2,1)}, bf16[2,480,128]{2,1,0:T(8,128)(2,1)}, u32[]{:S(2)}, u32[]{:S(2)}) collective-permute-start(bf16[2,480,128]{2,1,0:T(8,128)(2,1)} %get-tuple-element.54.refs_0_), channel_id=1, source_target_pairs={{0,48},{8,56},{16,0},{24,8},{32,16},{40,24},{48,32},{56,40},{1,49}... | collective-permute-start | bytes 737288 | tf_op jit(solution)/shard_map/ppermute | solution.py:53
  17.7 11.3 %collective-permute-start.1 = (bf16[2,480,128]{2,1,0:T(8,128)(2,1)}, bf16[2,480,128]{2,1,0:T(8,128)(2,1)}, u32[]{:S(2)}, u32[]{:S(2)}) collective-permute-start(bf16[2,480,128]{2,1,0:T(8,128)(2,1)} %get-tuple-element.54.refs_0_), channel_id=1, source_target_pairs={{0,16},{8,24},{16,32},{24,40},{32,48},{40,56},{48,0},{56,8},{1,17}... | collective-permute-start | bytes 737288 | tf_op jit(solution)/shard_map/ppermute | solution.py:53
  18.8 10.2 %collective-permute-start = (bf16[2,480,128]{2,1,0:T(8,128)(2,1)}, bf16[2,480,128]{2,1,0:T(8,128)(2,1)}, u32[]{:S(2)}, u32[]{:S(2)}) collective-permute-start(bf16[2,480,128]{2,1,0:T(8,128)(2,1)} %get-tuple-element.54.refs_0_), channel_id=1, source_target_pairs={{0,8},{8,0},{16,24},{24,16},{32,40},{40,32},{48,56},{56,48},{1,9},... | collective-permute-start | bytes 737288 | tf_op jit(solution)/shard_map/ppermute | solution.py:57
  18.9 10.6 %collective-permute-start.13 = (bf16[2,480,128]{2,1,0:T(8,128)(2,1)}, bf16[2,480,128]{2,1,0:T(8,128)(2,1)}, u32[]{:S(2)}, u32[]{:S(2)}) collective-permute-start(bf16[2,480,128]{2,1,0:T(8,128)(2,1)} %collective-permute-done.12.refs_14_), channel_id=1, source_target_pairs={{0,8},{8,0},{16,24},{24,16},{32,40},{40,32},{48,56},{56,48},{1,9},... | collective-permute-start | bytes 737288 | tf_op jit(solution)/shard_map/ppermute | solution.py:57
  49.8 8.6 %collective-permute-start.15 = (bf16[40,1536]{1,0:T(8,128)(2,1)S(1)}, bf16[40,1536]{1,0:T(8,128)(2,1)S(1)}, u32[]{:S(2)}, u32[]{:S(2)}) collective-permute-start(bf16[40,1536]{1,0:T(8,128)(2,1)S(1)} %get-tuple-element.57), channel_id=1, source_target_pairs={{0,2},{1,3},{2,4},{3,5},{4,6},{5,7},{6,0},{7,1},{8,10},{9,11},{10,... | collective-permute-start | bytes 368648 | tf_op jit(solution)/shard_map/ppermute | solution.py:44
  50.6 8.2 %collective-permute-start.16 = (bf16[40,1536]{1,0:T(8,128)(2,1)S(1)}, bf16[40,1536]{1,0:T(8,128)(2,1)S(1)}, u32[]{:S(2)}, u32[]{:S(2)}) collective-permute-start(bf16[40,1536]{1,0:T(8,128)(2,1)S(1)} %get-tuple-element.58), channel_id=1, source_target_pairs={{0,6},{1,7},{2,0},{3,1},{4,2},{5,3},{6,4},{7,5},{8,14},{9,15},{10,... | collective-permute-start | bytes 368648 | tf_op jit(solution)/shard_map/ppermute | solution.py:44
  68.2 10.9 %collective-permute-start.24 = (bf16[2,40,1536]{2,1,0:T(8,128)(2,1)S(1)}, bf16[2,40,1536]{2,1,0:T(8,128)(2,1)S(1)}, u32[]{:S(2)}, u32[]{:S(2)}) collective-permute-start(bf16[2,40,1536]{2,1,0:T(8,128)(2,1)S(1)} %pad_maximum_fusion.p0), channel_id=1, source_target_pairs={{0,6},{1,7},{2,0},{3,1},{4,2},{5,3},{6,4},{7,5},{8,14},{9,15},{10,... | collective-permute-start | bytes 737288 | tf_op jit(solution)/shard_map/ppermute | solution.py:44
  72.8 10.0 %collective-permute-start.22 = (bf16[2,40,1536]{2,1,0:T(8,128)(2,1)S(1)}, bf16[2,40,1536]{2,1,0:T(8,128)(2,1)S(1)}, u32[]{:S(2)}, u32[]{:S(2)}) collective-permute-start(bf16[2,40,1536]{2,1,0:T(8,128)(2,1)S(1)} %pad_maximum_fusion.p0), channel_id=1, source_target_pairs={{0,2},{1,3},{2,4},{3,5},{4,6},{5,7},{6,0},{7,1},{8,10},{9,11},{10,... | collective-permute-start | bytes 737288 | tf_op jit(solution)/shard_map/ppermute | solution.py:44
  87.0 8.5 %collective-permute-start.29 = (bf16[40,1536]{1,0:T(8,128)(2,1)S(1)}, bf16[40,1536]{1,0:T(8,128)(2,1)S(1)}, u32[]{:S(2)}, u32[]{:S(2)}) collective-permute-start(bf16[40,1536]{1,0:T(8,128)(2,1)S(1)} %get-tuple-element.71), channel_id=1, source_target_pairs={{0,2},{1,3},{2,4},{3,5},{4,6},{5,7},{6,0},{7,1},{8,10},{9,11},{10,... | collective-permute-start | bytes 368648 | tf_op jit(solution)/shard_map/ppermute | solution.py:44
  90.2 8.5 %collective-permute-start.25 = (bf16[40,1536]{1,0:T(8,128)(2,1)S(1)}, bf16[40,1536]{1,0:T(8,128)(2,1)S(1)}, u32[]{:S(2)}, u32[]{:S(2)}) collective-permute-start(bf16[40,1536]{1,0:T(8,128)(2,1)S(1)} %get-tuple-element.66), channel_id=1, source_target_pairs={{0,4},{1,5},{2,6},{3,7},{4,0},{5,1},{6,2},{7,3},{8,12},{9,13},{10,... | collective-permute-start | bytes 368648 | tf_op jit(solution)/shard_map/ppermute | solution.py:44
  111.2 8.6 %collective-permute-start.36 = (bf16[2,40,1536]{2,1,0:T(8,128)(2,1)S(1)}, bf16[2,40,1536]{2,1,0:T(8,128)(2,1)S(1)}, u32[]{:S(2)}, u32[]{:S(2)}) collective-permute-start(bf16[2,40,1536]{2,1,0:T(8,128)(2,1)S(1)} %pad_maximum_fusion.1.p0), channel_id=1, source_target_pairs={{0,6},{1,7},{2,0},{3,1},{4,2},{5,3},{6,4},{7,5},{8,14},{9,15},{10,... | collective-permute-start | bytes 737288 | tf_op jit(solution)/shard_map/ppermute | solution.py:44
  113.4 10.0 %collective-permute-start.34 = (bf16[2,40,1536]{2,1,0:T(8,128)(2,1)S(1)}, bf16[2,40,1536]{2,1,0:T(8,128)(2,1)S(1)}, u32[]{:S(2)}, u32[]{:S(2)}) collective-permute-start(bf16[2,40,1536]{2,1,0:T(8,128)(2,1)S(1)} %pad_maximum_fusion.1.p0), channel_id=1, source_target_pairs={{0,2},{1,3},{2,4},{3,5},{4,6},{5,7},{6,0},{7,1},{8,10},{9,11},{10,... | collective-permute-start | bytes 737288 | tf_op jit(solution)/shard_map/ppermute | solution.py:44
  145.7 10.6 %collective-permute-start.48 = (bf16[40,1536]{1,0:T(8,128)(2,1)S(1)}, bf16[40,1536]{1,0:T(8,128)(2,1)S(1)}, u32[]{:S(2)}, u32[]{:S(2)}) collective-permute-start(bf16[40,1536]{1,0:T(8,128)(2,1)S(1)} %get-tuple-element.82), channel_id=1, source_target_pairs={{0,2},{1,3},{2,4},{3,5},{4,6},{5,7},{6,0},{7,1},{8,10},{9,11},{10,... | collective-permute-start | bytes 368648 | tf_op jit(solution)/shard_map/ppermute | solution.py:44
  147.2 9.1 %collective-permute-start.49 = (bf16[40,1536]{1,0:T(8,128)(2,1)S(1)}, bf16[40,1536]{1,0:T(8,128)(2,1)S(1)}, u32[]{:S(2)}, u32[]{:S(2)}) collective-permute-start(bf16[40,1536]{1,0:T(8,128)(2,1)S(1)} %get-tuple-element.83), channel_id=1, source_target_pairs={{0,6},{1,7},{2,0},{3,1},{4,2},{5,3},{6,4},{7,5},{8,14},{9,15},{10,... | collective-permute-start | bytes 368648 | tf_op jit(solution)/shard_map/ppermute | solution.py:44
  149.0 9.5 %collective-permute-start.44 = (bf16[40,1536]{1,0:T(8,128)(2,1)S(1)}, bf16[40,1536]{1,0:T(8,128)(2,1)S(1)}, u32[]{:S(2)}, u32[]{:S(2)}) collective-permute-start(bf16[40,1536]{1,0:T(8,128)(2,1)S(1)} %get-tuple-element.77), channel_id=1, source_target_pairs={{0,4},{1,5},{2,6},{3,7},{4,0},{5,1},{6,2},{7,3},{8,12},{9,13},{10,... | collective-permute-start | bytes 368648 | tf_op jit(solution)/shard_map/ppermute | solution.py:44
  151.0 9.0 %collective-permute-start.45 = (bf16[40,1536]{1,0:T(8,128)(2,1)S(1)}, bf16[40,1536]{1,0:T(8,128)(2,1)S(1)}, u32[]{:S(2)}, u32[]{:S(2)}) collective-permute-start(bf16[40,1536]{1,0:T(8,128)(2,1)S(1)} %get-tuple-element.78), channel_id=1, source_target_pairs={{0,2},{1,3},{2,4},{3,5},{4,6},{5,7},{6,0},{7,1},{8,10},{9,11},{10,... | collective-permute-start | bytes 368648 | tf_op jit(solution)/shard_map/ppermute | solution.py:44
  170.6 8.3 %collective-permute-start.53 = (bf16[2,40,1536]{2,1,0:T(8,128)(2,1)S(1)}, bf16[2,40,1536]{2,1,0:T(8,128)(2,1)S(1)}, u32[]{:S(2)}, u32[]{:S(2)}) collective-permute-start(bf16[2,40,1536]{2,1,0:T(8,128)(2,1)S(1)} %pad_maximum_fusion.2.p0), channel_id=1, source_target_pairs={{0,4},{1,5},{2,6},{3,7},{4,0},{5,1},{6,2},{7,3},{8,12},{9,13},{10,... | collective-permute-start | bytes 737288 | tf_op jit(solution)/shard_map/ppermute | solution.py:44
  172.6 8.8 %collective-permute-start.52 = (bf16[2,40,1536]{2,1,0:T(8,128)(2,1)S(1)}, bf16[2,40,1536]{2,1,0:T(8,128)(2,1)S(1)}, u32[]{:S(2)}, u32[]{:S(2)}) collective-permute-start(bf16[2,40,1536]{2,1,0:T(8,128)(2,1)S(1)} %pad_maximum_fusion.2.p0), channel_id=1, source_target_pairs={{0,2},{1,3},{2,4},{3,5},{4,6},{5,7},{6,0},{7,1},{8,10},{9,11},{10,... | collective-permute-start | bytes 737288 | tf_op jit(solution)/shard_map/ppermute | solution.py:44
  206.7 16.2 %all-to-all-start = ((bf16[16,8,1792]{2,1,0:T(8,128)(2,1)}), bf16[16,8,1792]{2,1,0:T(8,128)(2,1)S(1)}, u32[]{:S(2)}, u32[]{:S(2)}) async-start(bf16[16,8,1792]{2,1,0:T(8,128)(2,1)} %broadcast_in_dim.28), calls=%async_computation | async-start | bytes 917504 | tf_op jit(solution)/shard_map/all_to_all | solution.py:501
  (72 other events, 1006.2 us)

commit v4 on v3

--- a/solution.py
+++ b/solution.py
@@ -189,15 +189,10 @@
             axis=0,
         )
 
-    def scores_of(queries, pieces, text, r):
-        keys = jnp.concatenate([piece[r, 0:width, :] for piece in pieces], axis=1)
-        return jnp.concatenate([mm(queries, keys), mm_t(queries, text[:, 0:width])], axis=1)
-
-    def summed_of(weights, pieces, text, r):
-        values = jnp.concatenate([piece[r, width : 2 * width, :] for piece in pieces], axis=1)
-        return mm_t(weights[:, 0:image_keys], values) + mm(
-            weights[:, image_keys:], text[:, width:]
-        )
+    fresh_share = jnp.where(is_fresh, 1.0, 0.0).astype(BF16)
+
+    def all_of(pieces, r, at):
+        return jnp.concatenate([piece[r, at : at + width, :] for piece in pieces], axis=1)
 
     for r in range(REQ):
         q = jnp.concatenate(
@@ -207,22 +202,42 @@
             ],
             axis=0,
         )
+        q = q * HD ** (-0.5)
         queries = jnp.concatenate(
             [jnp.where(lane_head == h, q, 0.0) for h in range(heads)], axis=0
         ).astype(BF16)
         fresh_text, stale_text = text_of(fresh, r), text_of(stale, r)
-        scores = jnp.where(
-            is_fresh,
-            scores_of(queries, fresh, fresh_text, r),
-            scores_of(queries, stale, stale_text, r),
-        ) * HD ** (-0.5)
-        scores = scores + bias[r : r + 1, :]
-        top = jnp.max(scores, axis=-1, keepdims=True)
-        weights = jnp.exp(scores - top)
-        total = jnp.sum(weights, axis=-1, keepdims=True)
-        summed = summed_of(
-            jnp.where(is_fresh, weights, 0.0).astype(BF16), fresh, fresh_text, r
-        ) + summed_of(jnp.where(is_fresh, 0.0, weights).astype(BF16), stale, stale_text, r)
+        image_scores = jnp.where(
+            is_fresh[:, 0:image_keys],
+            mm(queries, all_of(fresh, r, 0)),
+            mm(queries, all_of(stale, r, 0)),
+        )
+        text_scores = jnp.where(
+            is_fresh[:, image_keys:],
+            mm_t(queries, fresh_text[:, 0:width]),
+            mm_t(queries, stale_text[:, 0:width]),
+        ) + bias[r : r + 1, image_keys:]
+        top = jnp.maximum(
+            jnp.max(image_scores, axis=-1, keepdims=True),
+            jnp.max(text_scores, axis=-1, keepdims=True),
+        )
+        image_weights = jnp.exp(image_scores - top)
+        text_weights = jnp.exp(text_scores - top)
+        total = jnp.sum(image_weights, axis=-1, keepdims=True) + jnp.sum(
+            text_weights, axis=-1, keepdims=True
+        )
+        whole = image_weights.astype(BF16)
+        part = whole * fresh_share[:, 0:image_keys]
+        summed = mm_t(part, all_of(fresh, r, width)) + mm_t(
+            whole - part, all_of(stale, r, width)
+        )
+        whole = text_weights.astype(BF16)
+        part = whole * fresh_share[:, image_keys:]
+        summed = (
+            summed
+            + mm(part, fresh_text[:, width:])
+            + mm(whole - part, stale_text[:, width:])
+        )
         summed = summed / total
         merged = summed[0:rows]
         for h in range(1, heads):

time: 225 us -> 224 us (level)
  no operation moved by 1% of the time
where the time goes in v4:
time: 224 us
  waiting for transfers between devices  88.4 us (39%)
  starting transfers between devices  88 us (39%)
  Pallas kernels  33.8 us (15%)
  local copies, waits for them, and re-layouts  11 us (5%)
    ppermute x33, starting transfers between devices, along_z(): return lax.ppermute(value, 'tp', pairs)  45.8 us
    ppermute x33, waiting for transfers between devices, along_z(): return lax.ppermute(value, 'tp', pairs)  38.1 us
    ppermute x6, waiting for transfers between devices, across_x(): return lax.ppermute(value, 'tp', [(i, i ^ 1) for i in range(Z * X)])  19.5 us
    ppermute x9, waiting for transfers between devices, along_y(): return lax.ppermute(value, 'seq', pairs)  17.3 us
    ppermute x6, starting transfers between devices, across_x(): return lax.ppermute(value, 'tp', [(i, i ^ 1) for i in range(Z * X)])  14.3 us
    ppermute x9, starting transfers between devices, along_y(): return lax.ppermute(value, 'seq', pairs)  14.2 us
    pallas_call x2, Pallas kernels, rest_of_layer(): call(attend, 'attend', [SMEM] * 2 + [VMEM] * 21, [row_bf16] * 8, [pltpu.V...  13.4 us
    unnamed x66, local copies, waits for them, and re-layouts  8.26 us
  transfers between devices with their start and end apart: 63, of which 41 were waited for; matrix products, arithmetic and copies ran while one was open for 1% of the time, Pallas kernels for 2%

profile of v4, /device:TPU:0, one launch (start us, length us, event | category | flops | bytes accessed | tf_op | source)
XLA Modules:
  0.0 223.6 jit_solution(9224951657349195095)
XLA Ops:
  2.5 3.4 %collective-permute-start.12 = (bf16[2,480,128]{2,1,0:T(8,128)(2,1)S(1)}, bf16[2,480,128]{2,1,0:T(8,128)(2,1)}, u32[]{:S(2)}, u32[]{:S(2)}) collective-permute-start(bf16[2,480,128]{2,1,0:T(8,128)(2,1)S(1)} %pack_stale.1.refs_8_), channel_id=1, source_target_pairs={{0,32},{8,40},{16,48},{24,56},{32,0},{40,8},{48,16},{56,24},{1,33}... | collective-permute-start | bytes 737288 | tf_op jit(solution)/shard_map/ppermute | solution.py:53
  8.6 4.9 %project_first.1 = (bf16[256,192]{1,0:T(8,128)(2,1)}, f32[64,192]{1,0:T(8,128)}, bf16[2,480,128]{2,1,0:T(8,128)(2,1)}, bf16[64,384]{1,0:T(8,128)(2,1)}, bf16[40,1536]{1,0:T(8,128)(2,1)}) custom-call(s32[4]{0:T(128)} %pad_add_fusion.place, bf16[8,32,1536]{2,1,0:T(8,128)(2,1)} %bitcast.108, bf16[8,8,1536]{2,1,0:T(8,128)(2,1)} %bitcast.109, ...), custom_call_target="tpu_custom_call" | custom-call | tf_op jit(solution)/shard_map/project_first/pallas_call | solution.py:488
  19.4 4.7 %collective-permute-done.5.refs_6_ = bf16[2,480,128]{2,1,0:T(8,128)(2,1)} collective-permute-done((bf16[2,480,128]{2,1,0:T(8,128)(2,1)}, bf16[2,480,128]{2,1,0:T(8,128)(2,1)}, u32[]{:S(2)}, u32[]{:S(2)}) %collective-permute-start.5) | collective-permute-done | bytes 245792 | tf_op jit(solution)/shard_map/ppermute | solution.py:53
  24.1 4.5 %collective-permute-done.3.refs_4_ = bf16[2,480,128]{2,1,0:T(8,128)(2,1)} collective-permute-done((bf16[2,480,128]{2,1,0:T(8,128)(2,1)}, bf16[2,480,128]{2,1,0:T(8,128)(2,1)}, u32[]{:S(2)}, u32[]{:S(2)}) %collective-permute-start.3) | collective-permute-done | bytes 245792 | tf_op jit(solution)/shard_map/ppermute | solution.py:53
  35.3 7.0 %attend.2 = (bf16[40,1536]{1,0:T(8,128)(2,1)S(1)}, bf16[40,1536]{1,0:T(8,128)(2,1)S(1)}, bf16[40,1536]{1,0:T(8,128)(2,1)S(1)}, bf16[40,1536]{1,0:T(8,128)(2,1)S(...) custom-call(s32[4]{0:T(128)S(1)} %copy-done.21, ...), custom_call_target="tpu_custom_call" | custom-call | tf_op jit(solution)/shard_map/attend/pallas_call | solution.py:449
  42.3 4.0 %collective-permute-start.17 = (bf16[40,1536]{1,0:T(8,128)(2,1)S(1)}, bf16[40,1536]{1,0:T(8,128)(2,1)S(1)}, u32[]{:S(2)}, u32[]{:S(2)}) collective-permute-start(bf16[40,1536]{1,0:T(8,128)(2,1)S(1)} %get-tuple-element.60), channel_id=1, source_target_pairs={{0,4},{1,5},{2,6},{3,7},{4,0},{5,1},{6,2},{7,3},{8,12},{9,13},{10,... | collective-permute-start | bytes 368648 | tf_op jit(solution)/shard_map/ppermute | solution.py:44
  50.4 3.7 %collective-permute-start.16 = (bf16[40,1536]{1,0:T(8,128)(2,1)S(1)}, bf16[40,1536]{1,0:T(8,128)(2,1)S(1)}, u32[]{:S(2)}, u32[]{:S(2)}) collective-permute-start(bf16[40,1536]{1,0:T(8,128)(2,1)S(1)} %get-tuple-element.58), channel_id=1, source_target_pairs={{0,6},{1,7},{2,0},{3,1},{4,2},{5,3},{6,4},{7,5},{8,14},{9,15},{10,... | collective-permute-start | bytes 368648 | tf_op jit(solution)/shard_map/ppermute | solution.py:44
  54.2 3.1 %collective-permute-start.20 = (bf16[40,1536]{1,0:T(8,128)(2,1)S(1)}, bf16[40,1536]{1,0:T(8,128)(2,1)S(1)}, u32[]{:S(2)}, u32[]{:S(2)}) collective-permute-start(bf16[40,1536]{1,0:T(8,128)(2,1)S(1)} %add_far.4), channel_id=1, source_target_pairs={{0,1},{1,0},{2,3},{3,2},{4,5},{5,4},{6,7},{7,6},{8,9},{9,8},{10,11... | collective-permute-start | bytes 368648 | tf_op jit(solution)/shard_map/ppermute | solution.py:48
  61.5 3.1 %collective-permute-start.21 = (bf16[40,1536]{1,0:T(8,128)(2,1)S(1)}, bf16[40,1536]{1,0:T(8,128)(2,1)S(1)}, u32[]{:S(2)}, u32[]{:S(2)}) collective-permute-start(bf16[40,1536]{1,0:T(8,128)(2,1)S(1)} %get-tuple-element.64), channel_id=1, source_target_pairs={{0,1},{1,0},{2,3},{3,2},{4,5},{5,4},{6,7},{7,6},{8,9},{9,8},{10,11... | collective-permute-start | bytes 368648 | tf_op jit(solution)/shard_map/ppermute | solution.py:48
  64.6 3.3 %collective-permute-done.21 = bf16[40,1536]{1,0:T(8,128)(2,1)S(1)} collective-permute-done((bf16[40,1536]{1,0:T(8,128)(2,1)S(1)}, bf16[40,1536]{1,0:T(8,128)(2,1)S(1)}, u32[]{:S(2)}, u32[]{:S(2)}) %collective-permute-start.21) | collective-permute-done | bytes 122912 | tf_op jit(solution)/shard_map/ppermute | solution.py:48
  68.0 4.6 %collective-permute-start.24 = (bf16[2,40,1536]{2,1,0:T(8,128)(2,1)S(1)}, bf16[2,40,1536]{2,1,0:T(8,128)(2,1)S(1)}, u32[]{:S(2)}, u32[]{:S(2)}) collective-permute-start(bf16[2,40,1536]{2,1,0:T(8,128)(2,1)S(1)} %pad_maximum_fusion.p0), channel_id=1, source_target_pairs={{0,6},{1,7},{2,0},{3,1},{4,2},{5,3},{6,4},{7,5},{8,14},{9,15},{10,... | collective-permute-start | bytes 737288 | tf_op jit(solution)/shard_map/ppermute | solution.py:44
  73.5 5.4 %collective-permute-done.24.p3 = bf16[2,40,1536]{2,1,0:T(8,128)(2,1)S(1)} collective-permute-done((bf16[2,40,1536]{2,1,0:T(8,128)(2,1)S(1)}, bf16[2,40,1536]{2,1,0:T(8,128)(2,1)S(1)}, u32[]{:S(2)}, u32[]{:S(2)}) %collective-permute-start.24) | collective-permute-done | bytes 245792 | tf_op jit(solution)/shard_map/ppermute | solution.py:44
  82.6 3.7 %feed_forward.2 = (bf16[40,1536]{1,0:T(8,128)(2,1)S(1)}, bf16[40,1536]{1,0:T(8,128)(2,1)S(1)}, bf16[40,1536]{1,0:T(8,128)(2,1)S(1)}, bf16[40,1536]{1,0:T(8,128)(...) custom-call(s32[4]{0:T(128)S(1)} %copy-done.21, ...), custom_call_target="tpu_custom_call" | custom-call | tf_op jit(solution)/shard_map/feed_forward/pallas_call | solution.py:475
  95.3 3.2 %collective-permute-start.31 = (bf16[40,1536]{1,0:T(8,128)(2,1)S(1)}, bf16[40,1536]{1,0:T(8,128)(2,1)S(1)}, u32[]{:S(2)}, u32[]{:S(2)}) collective-permute-start(bf16[40,1536]{1,0:T(8,128)(2,1)S(1)} %add_far.5), channel_id=1, source_target_pairs={{0,1},{1,0},{2,3},{3,2},{4,5},{5,4},{6,7},{7,6},{8,9},{9,8},{10,11... | collective-permute-start | bytes 368648 | tf_op jit(solution)/shard_map/ppermute | solution.py:48
  98.4 3.6 %collective-permute-done.31.p4 = bf16[40,1536]{1,0:T(8,128)(2,1)S(1)} collective-permute-done((bf16[40,1536]{1,0:T(8,128)(2,1)S(1)}, bf16[40,1536]{1,0:T(8,128)(2,1)S(1)}, u32[]{:S(2)}, u32[]{:S(2)}) %collective-permute-start.31) | collective-permute-done | bytes 122912 | tf_op jit(solution)/shard_map/ppermute | solution.py:48
  102.7 4.4 %collective-permute-start.33 = (bf16[40,1536]{1,0:T(8,128)(2,1)S(1)}, bf16[40,1536]{1,0:T(8,128)(2,1)S(1)}, u32[]{:S(2)}, u32[]{:S(2)}) collective-permute-start(bf16[40,1536]{1,0:T(8,128)(2,1)S(1)} %after_mlp.1.refs_1_), channel_id=1, source_target_pairs={{0,65},{1,64},{2,67},{3,66},{4,69},{5,68},{6,71},{7,70},{8,73},{9,... | collective-permute-start | bytes 368648 | tf_op jit(solution)/shard_map/ppermute | solution.py:62
  114.1 5.4 %collective-permute-done.36.p3 = bf16[2,40,1536]{2,1,0:T(8,128)(2,1)S(1)} collective-permute-done((bf16[2,40,1536]{2,1,0:T(8,128)(2,1)S(1)}, bf16[2,40,1536]{2,1,0:T(8,128)(2,1)S(1)}, u32[]{:S(2)}, u32[]{:S(2)}) %collective-permute-start.36) | collective-permute-done | bytes 245792 | tf_op jit(solution)/shard_map/ppermute | solution.py:44
  130.0 3.5 %collective-permute-done.42.refs_6_ = bf16[2,480,128]{2,1,0:T(8,128)(2,1)S(1)} collective-permute-done((bf16[2,480,128]{2,1,0:T(8,128)(2,1)S(1)}, bf16[2,480,128]{2,1,0:T(8,128)(2,1)S(1)}, u32[]{:S(2)}, u32[]{:S(2)}) %collective-permute-start.42) | collective-permute-done | bytes 245792 | tf_op jit(solution)/shard_map/ppermute | solution.py:53
  138.4 6.4 %attend.3 = (bf16[40,1536]{1,0:T(8,128)(2,1)S(1)}, bf16[40,1536]{1,0:T(8,128)(2,1)S(1)}, bf16[40,1536]{1,0:T(8,128)(2,1)S(1)}, bf16[40,1536]{1,0:T(8,128)(2,1)S(...) custom-call(s32[4]{0:T(128)S(1)} %copy-done.21, ...), custom_call_target="tpu_custom_call" | custom-call | tf_op jit(solution)/shard_map/attend/pallas_call | solution.py:449
  164.7 4.9 %collective-permute-done.51 = bf16[40,1536]{1,0:T(8,128)(2,1)S(1)} collective-permute-done((bf16[40,1536]{1,0:T(8,128)(2,1)S(1)}, bf16[40,1536]{1,0:T(8,128)(2,1)S(1)}, u32[]{:S(2)}, u32[]{:S(2)}) %collective-permute-start.51) | collective-permute-done | bytes 122912 | tf_op jit(solution)/shard_map/ppermute | solution.py:48
  172.6 3.8 %collective-permute-done.54.p3 = bf16[2,40,1536]{2,1,0:T(8,128)(2,1)S(1)} collective-permute-done((bf16[2,40,1536]{2,1,0:T(8,128)(2,1)S(1)}, bf16[2,40,1536]{2,1,0:T(8,128)(2,1)S(1)}, u32[]{:S(2)}, u32[]{:S(2)}) %collective-permute-start.54) | collective-permute-done | bytes 245792 | tf_op jit(solution)/shard_map/ppermute | solution.py:44
  180.9 4.4 %feed_forward.3 = (bf16[40,1536]{1,0:T(8,128)(2,1)S(1)}, bf16[40,1536]{1,0:T(8,128)(2,1)S(1)}, bf16[40,1536]{1,0:T(8,128)(2,1)S(1)}, bf16[40,1536]{1,0:T(8,128)(...) custom-call(s32[4]{0:T(128)S(1)} %copy-done.21, ...), custom_call_target="tpu_custom_call" | custom-call | tf_op jit(solution)/shard_map/feed_forward/pallas_call | solution.py:475
  206.2 6.8 %all-to-all-start = ((bf16[16,8,1792]{2,1,0:T(8,128)(2,1)}), bf16[16,8,1792]{2,1,0:T(8,128)(2,1)S(1)}, u32[]{:S(2)}, u32[]{:S(2)}) async-start(bf16[16,8,1792]{2,1,0:T(8,128)(2,1)} %broadcast_in_dim.28), calls=%async_computation | async-start | bytes 917504 | tf_op jit(solution)/shard_map/all_to_all | solution.py:516
  214.4 7.9 %all-to-all-done.received = bf16[16,8,1792]{2,1,0:T(8,128)(2,1)S(1)} async-done(((bf16[16,8,1792]{2,1,0:T(8,128)(2,1)}), bf16[16,8,1792]{2,1,0:T(8,128)(2,1)S(1)}, u32[]{:S(2)}, u32[]{:S(2)}) %all-to-all-start) | async-done | bytes 458784 | tf_op jit(solution)/shard_map/all_to_all | solution.py:516
  (199 shorter events, 112.9 us)
Async XLA Ops:
  2.5 11.7 %collective-permute-start.12 = (bf16[2,480,128]{2,1,0:T(8,128)(2,1)S(1)}, bf16[2,480,128]{2,1,0:T(8,128)(2,1)}, u32[]{:S(2)}, u32[]{:S(2)}) collective-permute-start(bf16[2,480,128]{2,1,0:T(8,128)(2,1)S(1)} %pack_stale.1.refs_8_), channel_id=1, source_target_pairs={{0,32},{8,40},{16,48},{24,56},{32,0},{40,8},{48,16},{56,24},{1,33}... | collective-permute-start | bytes 737288 | tf_op jit(solution)/shard_map/ppermute | solution.py:53
  5.9 11.8 %collective-permute-start.10 = (bf16[2,480,128]{2,1,0:T(8,128)(2,1)S(1)}, bf16[2,480,128]{2,1,0:T(8,128)(2,1)}, u32[]{:S(2)}, u32[]{:S(2)}) collective-permute-start(bf16[2,480,128]{2,1,0:T(8,128)(2,1)S(1)} %pack_stale.1.refs_8_), channel_id=1, source_target_pairs={{0,48},{8,56},{16,0},{24,8},{32,16},{40,24},{48,32},{56,40},{1,49}... | collective-permute-start | bytes 737288 | tf_op jit(solution)/shard_map/ppermute | solution.py:53
  6.9 11.9 %collective-permute-start.8 = (bf16[2,480,128]{2,1,0:T(8,128)(2,1)S(1)}, bf16[2,480,128]{2,1,0:T(8,128)(2,1)}, u32[]{:S(2)}, u32[]{:S(2)}) collective-permute-start(bf16[2,480,128]{2,1,0:T(8,128)(2,1)S(1)} %pack_stale.1.refs_8_), channel_id=1, source_target_pairs={{0,16},{8,24},{16,32},{24,40},{32,48},{40,56},{48,0},{56,8},{1,17}... | collective-permute-start | bytes 737288 | tf_op jit(solution)/shard_map/ppermute | solution.py:53
  7.9 10.9 %collective-permute-start.7 = (bf16[2,480,128]{2,1,0:T(8,128)(2,1)S(1)}, bf16[2,480,128]{2,1,0:T(8,128)(2,1)}, u32[]{:S(2)}, u32[]{:S(2)}) collective-permute-start(bf16[2,480,128]{2,1,0:T(8,128)(2,1)S(1)} %pack_stale.1.refs_8_), channel_id=1, source_target_pairs={{0,8},{8,0},{16,24},{24,16},{32,40},{40,32},{48,56},{56,48},{1,9},... | collective-permute-start | bytes 737288 | tf_op jit(solution)/shard_map/ppermute | solution.py:57
  13.5 10.6 %collective-permute-start.5 = (bf16[2,480,128]{2,1,0:T(8,128)(2,1)}, bf16[2,480,128]{2,1,0:T(8,128)(2,1)}, u32[]{:S(2)}, u32[]{:S(2)}) collective-permute-start(bf16[2,480,128]{2,1,0:T(8,128)(2,1)} %get-tuple-element.54.refs_0_), channel_id=1, source_target_pairs={{0,32},{8,40},{16,48},{24,56},{32,0},{40,8},{48,16},{56,24},{1,33}... | collective-permute-start | bytes 737288 | tf_op jit(solution)/shard_map/ppermute | solution.py:53
  14.2 14.4 %collective-permute-start.3 = (bf16[2,480,128]{2,1,0:T(8,128)(2,1)}, bf16[2,480,128]{2,1,0:T(8,128)(2,1)}, u32[]{:S(2)}, u32[]{:S(2)}) collective-permute-start(bf16[2,480,128]{2,1,0:T(8,128)(2,1)} %get-tuple-element.54.refs_0_), channel_id=1, source_target_pairs={{0,48},{8,56},{16,0},{24,8},{32,16},{40,24},{48,32},{56,40},{1,49}... | collective-permute-start | bytes 737288 | tf_op jit(solution)/shard_map/ppermute | solution.py:53
  17.7 11.3 %collective-permute-start.1 = (bf16[2,480,128]{2,1,0:T(8,128)(2,1)}, bf16[2,480,128]{2,1,0:T(8,128)(2,1)}, u32[]{:S(2)}, u32[]{:S(2)}) collective-permute-start(bf16[2,480,128]{2,1,0:T(8,128)(2,1)} %get-tuple-element.54.refs_0_), channel_id=1, source_target_pairs={{0,16},{8,24},{16,32},{24,40},{32,48},{40,56},{48,0},{56,8},{1,17}... | collective-permute-start | bytes 737288 | tf_op jit(solution)/shard_map/ppermute | solution.py:53
  18.8 10.2 %collective-permute-start = (bf16[2,480,128]{2,1,0:T(8,128)(2,1)}, bf16[2,480,128]{2,1,0:T(8,128)(2,1)}, u32[]{:S(2)}, u32[]{:S(2)}) collective-permute-start(bf16[2,480,128]{2,1,0:T(8,128)(2,1)} %get-tuple-element.54.refs_0_), channel_id=1, source_target_pairs={{0,8},{8,0},{16,24},{24,16},{32,40},{40,32},{48,56},{56,48},{1,9},... | collective-permute-start | bytes 737288 | tf_op jit(solution)/shard_map/ppermute | solution.py:57
  18.9 10.6 %collective-permute-start.13 = (bf16[2,480,128]{2,1,0:T(8,128)(2,1)}, bf16[2,480,128]{2,1,0:T(8,128)(2,1)}, u32[]{:S(2)}, u32[]{:S(2)}) collective-permute-start(bf16[2,480,128]{2,1,0:T(8,128)(2,1)} %collective-permute-done.12.refs_14_), channel_id=1, source_target_pairs={{0,8},{8,0},{16,24},{24,16},{32,40},{40,32},{48,56},{56,48},{1,9},... | collective-permute-start | bytes 737288 | tf_op jit(solution)/shard_map/ppermute | solution.py:57
  49.5 8.6 %collective-permute-start.15 = (bf16[40,1536]{1,0:T(8,128)(2,1)S(1)}, bf16[40,1536]{1,0:T(8,128)(2,1)S(1)}, u32[]{:S(2)}, u32[]{:S(2)}) collective-permute-start(bf16[40,1536]{1,0:T(8,128)(2,1)S(1)} %get-tuple-element.57), channel_id=1, source_target_pairs={{0,2},{1,3},{2,4},{3,5},{4,6},{5,7},{6,0},{7,1},{8,10},{9,11},{10,... | collective-permute-start | bytes 368648 | tf_op jit(solution)/shard_map/ppermute | solution.py:44
  50.4 8.2 %collective-permute-start.16 = (bf16[40,1536]{1,0:T(8,128)(2,1)S(1)}, bf16[40,1536]{1,0:T(8,128)(2,1)S(1)}, u32[]{:S(2)}, u32[]{:S(2)}) collective-permute-start(bf16[40,1536]{1,0:T(8,128)(2,1)S(1)} %get-tuple-element.58), channel_id=1, source_target_pairs={{0,6},{1,7},{2,0},{3,1},{4,2},{5,3},{6,4},{7,5},{8,14},{9,15},{10,... | collective-permute-start | bytes 368648 | tf_op jit(solution)/shard_map/ppermute | solution.py:44
  68.0 10.9 %collective-permute-start.24 = (bf16[2,40,1536]{2,1,0:T(8,128)(2,1)S(1)}, bf16[2,40,1536]{2,1,0:T(8,128)(2,1)S(1)}, u32[]{:S(2)}, u32[]{:S(2)}) collective-permute-start(bf16[2,40,1536]{2,1,0:T(8,128)(2,1)S(1)} %pad_maximum_fusion.p0), channel_id=1, source_target_pairs={{0,6},{1,7},{2,0},{3,1},{4,2},{5,3},{6,4},{7,5},{8,14},{9,15},{10,... | collective-permute-start | bytes 737288 | tf_op jit(solution)/shard_map/ppermute | solution.py:44
  72.5 10.0 %collective-permute-start.22 = (bf16[2,40,1536]{2,1,0:T(8,128)(2,1)S(1)}, bf16[2,40,1536]{2,1,0:T(8,128)(2,1)S(1)}, u32[]{:S(2)}, u32[]{:S(2)}) collective-permute-start(bf16[2,40,1536]{2,1,0:T(8,128)(2,1)S(1)} %pad_maximum_fusion.p0), channel_id=1, source_target_pairs={{0,2},{1,3},{2,4},{3,5},{4,6},{5,7},{6,0},{7,1},{8,10},{9,11},{10,... | collective-permute-start | bytes 737288 | tf_op jit(solution)/shard_map/ppermute | solution.py:44
  86.7 8.5 %collective-permute-start.29 = (bf16[40,1536]{1,0:T(8,128)(2,1)S(1)}, bf16[40,1536]{1,0:T(8,128)(2,1)S(1)}, u32[]{:S(2)}, u32[]{:S(2)}) collective-permute-start(bf16[40,1536]{1,0:T(8,128)(2,1)S(1)} %get-tuple-element.71), channel_id=1, source_target_pairs={{0,2},{1,3},{2,4},{3,5},{4,6},{5,7},{6,0},{7,1},{8,10},{9,11},{10,... | collective-permute-start | bytes 368648 | tf_op jit(solution)/shard_map/ppermute | solution.py:44
  89.9 8.5 %collective-permute-start.25 = (bf16[40,1536]{1,0:T(8,128)(2,1)S(1)}, bf16[40,1536]{1,0:T(8,128)(2,1)S(1)}, u32[]{:S(2)}, u32[]{:S(2)}) collective-permute-start(bf16[40,1536]{1,0:T(8,128)(2,1)S(1)} %get-tuple-element.66), channel_id=1, source_target_pairs={{0,4},{1,5},{2,6},{3,7},{4,0},{5,1},{6,2},{7,3},{8,12},{9,13},{10,... | collective-permute-start | bytes 368648 | tf_op jit(solution)/shard_map/ppermute | solution.py:44
  110.9 8.6 %collective-permute-start.36 = (bf16[2,40,1536]{2,1,0:T(8,128)(2,1)S(1)}, bf16[2,40,1536]{2,1,0:T(8,128)(2,1)S(1)}, u32[]{:S(2)}, u32[]{:S(2)}) collective-permute-start(bf16[2,40,1536]{2,1,0:T(8,128)(2,1)S(1)} %pad_maximum_fusion.1.p0), channel_id=1, source_target_pairs={{0,6},{1,7},{2,0},{3,1},{4,2},{5,3},{6,4},{7,5},{8,14},{9,15},{10,... | collective-permute-start | bytes 737288 | tf_op jit(solution)/shard_map/ppermute | solution.py:44
  113.1 10.0 %collective-permute-start.34 = (bf16[2,40,1536]{2,1,0:T(8,128)(2,1)S(1)}, bf16[2,40,1536]{2,1,0:T(8,128)(2,1)S(1)}, u32[]{:S(2)}, u32[]{:S(2)}) collective-permute-start(bf16[2,40,1536]{2,1,0:T(8,128)(2,1)S(1)} %pad_maximum_fusion.1.p0), channel_id=1, source_target_pairs={{0,2},{1,3},{2,4},{3,5},{4,6},{5,7},{6,0},{7,1},{8,10},{9,11},{10,... | collective-permute-start | bytes 737288 | tf_op jit(solution)/shard_map/ppermute | solution.py:44
  145.2 10.6 %collective-permute-start.48 = (bf16[40,1536]{1,0:T(8,128)(2,1)S(1)}, bf16[40,1536]{1,0:T(8,128)(2,1)S(1)}, u32[]{:S(2)}, u32[]{:S(2)}) collective-permute-start(bf16[40,1536]{1,0:T(8,128)(2,1)S(1)} %get-tuple-element.82), channel_id=1, source_target_pairs={{0,2},{1,3},{2,4},{3,5},{4,6},{5,7},{6,0},{7,1},{8,10},{9,11},{10,... | collective-permute-start | bytes 368648 | tf_op jit(solution)/shard_map/ppermute | solution.py:44
  146.7 9.1 %collective-permute-start.49 = (bf16[40,1536]{1,0:T(8,128)(2,1)S(1)}, bf16[40,1536]{1,0:T(8,128)(2,1)S(1)}, u32[]{:S(2)}, u32[]{:S(2)}) collective-permute-start(bf16[40,1536]{1,0:T(8,128)(2,1)S(1)} %get-tuple-element.83), channel_id=1, source_target_pairs={{0,6},{1,7},{2,0},{3,1},{4,2},{5,3},{6,4},{7,5},{8,14},{9,15},{10,... | collective-permute-start | bytes 368648 | tf_op jit(solution)/shard_map/ppermute | solution.py:44
  148.5 9.5 %collective-permute-start.44 = (bf16[40,1536]{1,0:T(8,128)(2,1)S(1)}, bf16[40,1536]{1,0:T(8,128)(2,1)S(1)}, u32[]{:S(2)}, u32[]{:S(2)}) collective-permute-start(bf16[40,1536]{1,0:T(8,128)(2,1)S(1)} %get-tuple-element.77), channel_id=1, source_target_pairs={{0,4},{1,5},{2,6},{3,7},{4,0},{5,1},{6,2},{7,3},{8,12},{9,13},{10,... | collective-permute-start | bytes 368648 | tf_op jit(solution)/shard_map/ppermute | solution.py:44
  150.5 9.0 %collective-permute-start.45 = (bf16[40,1536]{1,0:T(8,128)(2,1)S(1)}, bf16[40,1536]{1,0:T(8,128)(2,1)S(1)}, u32[]{:S(2)}, u32[]{:S(2)}) collective-permute-start(bf16[40,1536]{1,0:T(8,128)(2,1)S(1)} %get-tuple-element.78), channel_id=1, source_target_pairs={{0,2},{1,3},{2,4},{3,5},{4,6},{5,7},{6,0},{7,1},{8,10},{9,11},{10,... | collective-permute-start | bytes 368648 | tf_op jit(solution)/shard_map/ppermute | solution.py:44
  170.1 8.3 %collective-permute-start.53 = (bf16[2,40,1536]{2,1,0:T(8,128)(2,1)S(1)}, bf16[2,40,1536]{2,1,0:T(8,128)(2,1)S(1)}, u32[]{:S(2)}, u32[]{:S(2)}) collective-permute-start(bf16[2,40,1536]{2,1,0:T(8,128)(2,1)S(1)} %pad_maximum_fusion.2.p0), channel_id=1, source_target_pairs={{0,4},{1,5},{2,6},{3,7},{4,0},{5,1},{6,2},{7,3},{8,12},{9,13},{10,... | collective-permute-start | bytes 737288 | tf_op jit(solution)/shard_map/ppermute | solution.py:44
  172.1 8.9 %collective-permute-start.52 = (bf16[2,40,1536]{2,1,0:T(8,128)(2,1)S(1)}, bf16[2,40,1536]{2,1,0:T(8,128)(2,1)S(1)}, u32[]{:S(2)}, u32[]{:S(2)}) collective-permute-start(bf16[2,40,1536]{2,1,0:T(8,128)(2,1)S(1)} %pad_maximum_fusion.2.p0), channel_id=1, source_target_pairs={{0,2},{1,3},{2,4},{3,5},{4,6},{5,7},{6,0},{7,1},{8,10},{9,11},{10,... | collective-permute-start | bytes 737288 | tf_op jit(solution)/shard_map/ppermute | solution.py:44
  206.2 16.2 %all-to-all-start = ((bf16[16,8,1792]{2,1,0:T(8,128)(2,1)}), bf16[16,8,1792]{2,1,0:T(8,128)(2,1)S(1)}, u32[]{:S(2)}, u32[]{:S(2)}) async-start(bf16[16,8,1792]{2,1,0:T(8,128)(2,1)} %broadcast_in_dim.28), calls=%async_computation | async-start | bytes 917504 | tf_op jit(solution)/shard_map/all_to_all | solution.py:516
  (72 other events, 1004.0 us)

commit v5 on v4

--- a/solution.py
+++ b/solution.py
@@ -510,7 +510,7 @@
     )(place, *pieces, *mods, *weights)
     h1, received = rest_of_layer(q_image, q_text, kv_next, arrived)
     tail = ((TQ, d_model + PT * channels // TQ), BF16)
-    (tail_rows,) = call(last_rows, "last_rows", [SMEM] + [VMEM] * 11, [tail])(
+    (tail_rows,) = call(last_rows, "last_rows", [SMEM] + [VMEM] * 11, [tail], mib=60)(
         place, h1, *received, *mods, mod_final, jnp.transpose(final_weight), y_first
     )
     shared = lax.all_to_all(

time: 224 us -> 223 us (level)
    unnamed x66 -> x68, local copies, waits for them, and re-layouts: 8.26 us -> 6.07 us
where the time goes in v5:
time: 223 us
  starting transfers between devices  88.2 us (40%)
  waiting for transfers between devices  88 us (39%)
  Pallas kernels  34.6 us (16%)
  local copies, waits for them, and re-layouts  9.51 us (4%)
    ppermute x33, starting transfers between devices, along_z(): return lax.ppermute(value, 'tp', pairs)  46.1 us
    ppermute x33, waiting for transfers between devices, along_z(): return lax.ppermute(value, 'tp', pairs)  37.5 us
    ppermute x6, waiting for transfers between devices, across_x(): return lax.ppermute(value, 'tp', [(i, i ^ 1) for i in range(Z * X)])  19.6 us
    ppermute x9, waiting for transfers between devices, along_y(): return lax.ppermute(value, 'seq', pairs)  17.3 us
    ppermute x6, starting transfers between devices, across_x(): return lax.ppermute(value, 'tp', [(i, i ^ 1) for i in range(Z * X)])  14.3 us
    ppermute x9, starting transfers between devices, along_y(): return lax.ppermute(value, 'seq', pairs)  14.2 us
    pallas_call x2, Pallas kernels, rest_of_layer(): call(attend, 'attend', [SMEM] * 2 + [VMEM] * 21, [row_bf16] * 8, [pltpu.V...  13.4 us
    all_to_all x1, waiting for transfers between devices, on_device(): lax.all_to_all(jnp.broadcast_to(tail_rows[None], (2 * CHUNKS,) + tail_row...  7.95 us
  transfers between devices with their start and end apart: 63, of which 41 were waited for; matrix products, arithmetic and copies ran while one was open for 1% of the time, Pallas kernels for 2%

profile of v5, /device:TPU:0, one launch (start us, length us, event | category | flops | bytes accessed | tf_op | source)
XLA Modules:
  0.0 222.7 jit_solution(3871607568660362671)
XLA Ops:
  2.5 3.4 %collective-permute-start.12 = (bf16[2,480,128]{2,1,0:T(8,128)(2,1)S(1)}, bf16[2,480,128]{2,1,0:T(8,128)(2,1)}, u32[]{:S(2)}, u32[]{:S(2)}) collective-permute-start(bf16[2,480,128]{2,1,0:T(8,128)(2,1)S(1)} %pack_stale.1.refs_8_), channel_id=1, source_target_pairs={{0,32},{8,40},{16,48},{24,56},{32,0},{40,8},{48,16},{56,24},{1,33}... | collective-permute-start | bytes 737288 | tf_op jit(solution)/shard_map/ppermute | solution.py:53
  8.6 4.9 %project_first.1 = (bf16[256,192]{1,0:T(8,128)(2,1)}, f32[64,192]{1,0:T(8,128)}, bf16[2,480,128]{2,1,0:T(8,128)(2,1)}, bf16[64,384]{1,0:T(8,128)(2,1)}, bf16[40,1536]{1,0:T(8,128)(2,1)}) custom-call(s32[4]{0:T(128)} %pad_add_fusion.place, bf16[8,32,1536]{2,1,0:T(8,128)(2,1)} %bitcast.107, bf16[8,8,1536]{2,1,0:T(8,128)(2,1)} %bitcast.108, ...), custom_call_target="tpu_custom_call" | custom-call | tf_op jit(solution)/shard_map/project_first/pallas_call | solution.py:488
  19.4 4.7 %collective-permute-done.5.refs_6_ = bf16[2,480,128]{2,1,0:T(8,128)(2,1)} collective-permute-done((bf16[2,480,128]{2,1,0:T(8,128)(2,1)}, bf16[2,480,128]{2,1,0:T(8,128)(2,1)}, u32[]{:S(2)}, u32[]{:S(2)}) %collective-permute-start.5) | collective-permute-done | bytes 245792 | tf_op jit(solution)/shard_map/ppermute | solution.py:53
  24.1 4.5 %collective-permute-done.3.refs_4_ = bf16[2,480,128]{2,1,0:T(8,128)(2,1)} collective-permute-done((bf16[2,480,128]{2,1,0:T(8,128)(2,1)}, bf16[2,480,128]{2,1,0:T(8,128)(2,1)}, u32[]{:S(2)}, u32[]{:S(2)}) %collective-permute-start.3) | collective-permute-done | bytes 245792 | tf_op jit(solution)/shard_map/ppermute | solution.py:53
  35.2 7.0 %attend.2 = (bf16[40,1536]{1,0:T(8,128)(2,1)S(1)}, bf16[40,1536]{1,0:T(8,128)(2,1)S(1)}, bf16[40,1536]{1,0:T(8,128)(2,1)S(1)}, bf16[40,1536]{1,0:T(8,128)(2,1)S(...) custom-call(s32[4]{0:T(128)S(1)} %copy-done.21, ...), custom_call_target="tpu_custom_call" | custom-call | tf_op jit(solution)/shard_map/attend/pallas_call | solution.py:449
  42.3 4.0 %collective-permute-start.17 = (bf16[40,1536]{1,0:T(8,128)(2,1)S(1)}, bf16[40,1536]{1,0:T(8,128)(2,1)S(1)}, u32[]{:S(2)}, u32[]{:S(2)}) collective-permute-start(bf16[40,1536]{1,0:T(8,128)(2,1)S(1)} %get-tuple-element.60), channel_id=1, source_target_pairs={{0,4},{1,5},{2,6},{3,7},{4,0},{5,1},{6,2},{7,3},{8,12},{9,13},{10,... | collective-permute-start | bytes 368648 | tf_op jit(solution)/shard_map/ppermute | solution.py:44
  50.3 3.7 %collective-permute-start.16 = (bf16[40,1536]{1,0:T(8,128)(2,1)S(1)}, bf16[40,1536]{1,0:T(8,128)(2,1)S(1)}, u32[]{:S(2)}, u32[]{:S(2)}) collective-permute-start(bf16[40,1536]{1,0:T(8,128)(2,1)S(1)} %get-tuple-element.58), channel_id=1, source_target_pairs={{0,6},{1,7},{2,0},{3,1},{4,2},{5,3},{6,4},{7,5},{8,14},{9,15},{10,... | collective-permute-start | bytes 368648 | tf_op jit(solution)/shard_map/ppermute | solution.py:44
  54.1 3.1 %collective-permute-start.20 = (bf16[40,1536]{1,0:T(8,128)(2,1)S(1)}, bf16[40,1536]{1,0:T(8,128)(2,1)S(1)}, u32[]{:S(2)}, u32[]{:S(2)}) collective-permute-start(bf16[40,1536]{1,0:T(8,128)(2,1)S(1)} %add_far.4), channel_id=1, source_target_pairs={{0,1},{1,0},{2,3},{3,2},{4,5},{5,4},{6,7},{7,6},{8,9},{9,8},{10,11... | collective-permute-start | bytes 368648 | tf_op jit(solution)/shard_map/ppermute | solution.py:48
  61.4 3.1 %collective-permute-start.21 = (bf16[40,1536]{1,0:T(8,128)(2,1)S(1)}, bf16[40,1536]{1,0:T(8,128)(2,1)S(1)}, u32[]{:S(2)}, u32[]{:S(2)}) collective-permute-start(bf16[40,1536]{1,0:T(8,128)(2,1)S(1)} %get-tuple-element.64), channel_id=1, source_target_pairs={{0,1},{1,0},{2,3},{3,2},{4,5},{5,4},{6,7},{7,6},{8,9},{9,8},{10,11... | collective-permute-start | bytes 368648 | tf_op jit(solution)/shard_map/ppermute | solution.py:48
  64.5 3.4 %collective-permute-done.21 = bf16[40,1536]{1,0:T(8,128)(2,1)S(1)} collective-permute-done((bf16[40,1536]{1,0:T(8,128)(2,1)S(1)}, bf16[40,1536]{1,0:T(8,128)(2,1)S(1)}, u32[]{:S(2)}, u32[]{:S(2)}) %collective-permute-start.21) | collective-permute-done | bytes 122912 | tf_op jit(solution)/shard_map/ppermute | solution.py:48
  67.9 4.6 %collective-permute-start.24 = (bf16[2,40,1536]{2,1,0:T(8,128)(2,1)S(1)}, bf16[2,40,1536]{2,1,0:T(8,128)(2,1)S(1)}, u32[]{:S(2)}, u32[]{:S(2)}) collective-permute-start(bf16[2,40,1536]{2,1,0:T(8,128)(2,1)S(1)} %pad_maximum_fusion.p0), channel_id=1, source_target_pairs={{0,6},{1,7},{2,0},{3,1},{4,2},{5,3},{6,4},{7,5},{8,14},{9,15},{10,... | collective-permute-start | bytes 737288 | tf_op jit(solution)/shard_map/ppermute | solution.py:44
  73.4 5.4 %collective-permute-done.24.p3 = bf16[2,40,1536]{2,1,0:T(8,128)(2,1)S(1)} collective-permute-done((bf16[2,40,1536]{2,1,0:T(8,128)(2,1)S(1)}, bf16[2,40,1536]{2,1,0:T(8,128)(2,1)S(1)}, u32[]{:S(2)}, u32[]{:S(2)}) %collective-permute-start.24) | collective-permute-done | bytes 245792 | tf_op jit(solution)/shard_map/ppermute | solution.py:44
  82.6 3.7 %feed_forward.2 = (bf16[40,1536]{1,0:T(8,128)(2,1)S(1)}, bf16[40,1536]{1,0:T(8,128)(2,1)S(1)}, bf16[40,1536]{1,0:T(8,128)(2,1)S(1)}, bf16[40,1536]{1,0:T(8,128)(...) custom-call(s32[4]{0:T(128)S(1)} %copy-done.21, ...), custom_call_target="tpu_custom_call" | custom-call | tf_op jit(solution)/shard_map/feed_forward/pallas_call | solution.py:475
  95.2 3.2 %collective-permute-start.31 = (bf16[40,1536]{1,0:T(8,128)(2,1)S(1)}, bf16[40,1536]{1,0:T(8,128)(2,1)S(1)}, u32[]{:S(2)}, u32[]{:S(2)}) collective-permute-start(bf16[40,1536]{1,0:T(8,128)(2,1)S(1)} %add_far.5), channel_id=1, source_target_pairs={{0,1},{1,0},{2,3},{3,2},{4,5},{5,4},{6,7},{7,6},{8,9},{9,8},{10,11... | collective-permute-start | bytes 368648 | tf_op jit(solution)/shard_map/ppermute | solution.py:48
  98.4 3.6 %collective-permute-done.31.p4 = bf16[40,1536]{1,0:T(8,128)(2,1)S(1)} collective-permute-done((bf16[40,1536]{1,0:T(8,128)(2,1)S(1)}, bf16[40,1536]{1,0:T(8,128)(2,1)S(1)}, u32[]{:S(2)}, u32[]{:S(2)}) %collective-permute-start.31) | collective-permute-done | bytes 122912 | tf_op jit(solution)/shard_map/ppermute | solution.py:48
  102.7 4.5 %collective-permute-start.33 = (bf16[40,1536]{1,0:T(8,128)(2,1)S(1)}, bf16[40,1536]{1,0:T(8,128)(2,1)S(1)}, u32[]{:S(2)}, u32[]{:S(2)}) collective-permute-start(bf16[40,1536]{1,0:T(8,128)(2,1)S(1)} %after_mlp.1.refs_1_), channel_id=1, source_target_pairs={{0,65},{1,64},{2,67},{3,66},{4,69},{5,68},{6,71},{7,70},{8,73},{9,... | collective-permute-start | bytes 368648 | tf_op jit(solution)/shard_map/ppermute | solution.py:62
  114.1 5.4 %collective-permute-done.36.p3 = bf16[2,40,1536]{2,1,0:T(8,128)(2,1)S(1)} collective-permute-done((bf16[2,40,1536]{2,1,0:T(8,128)(2,1)S(1)}, bf16[2,40,1536]{2,1,0:T(8,128)(2,1)S(1)}, u32[]{:S(2)}, u32[]{:S(2)}) %collective-permute-start.36) | collective-permute-done | bytes 245792 | tf_op jit(solution)/shard_map/ppermute | solution.py:44
  130.0 3.5 %collective-permute-done.42.refs_6_ = bf16[2,480,128]{2,1,0:T(8,128)(2,1)S(1)} collective-permute-done((bf16[2,480,128]{2,1,0:T(8,128)(2,1)S(1)}, bf16[2,480,128]{2,1,0:T(8,128)(2,1)S(1)}, u32[]{:S(2)}, u32[]{:S(2)}) %collective-permute-start.42) | collective-permute-done | bytes 245792 | tf_op jit(solution)/shard_map/ppermute | solution.py:53
  138.4 6.4 %attend.3 = (bf16[40,1536]{1,0:T(8,128)(2,1)S(1)}, bf16[40,1536]{1,0:T(8,128)(2,1)S(1)}, bf16[40,1536]{1,0:T(8,128)(2,1)S(1)}, bf16[40,1536]{1,0:T(8,128)(2,1)S(...) custom-call(s32[4]{0:T(128)S(1)} %copy-done.21, ...), custom_call_target="tpu_custom_call" | custom-call | tf_op jit(solution)/shard_map/attend/pallas_call | solution.py:449
  164.7 4.9 %collective-permute-done.51 = bf16[40,1536]{1,0:T(8,128)(2,1)S(1)} collective-permute-done((bf16[40,1536]{1,0:T(8,128)(2,1)S(1)}, bf16[40,1536]{1,0:T(8,128)(2,1)S(1)}, u32[]{:S(2)}, u32[]{:S(2)}) %collective-permute-start.51) | collective-permute-done | bytes 122912 | tf_op jit(solution)/shard_map/ppermute | solution.py:48
  172.6 3.8 %collective-permute-done.54.p3 = bf16[2,40,1536]{2,1,0:T(8,128)(2,1)S(1)} collective-permute-done((bf16[2,40,1536]{2,1,0:T(8,128)(2,1)S(1)}, bf16[2,40,1536]{2,1,0:T(8,128)(2,1)S(1)}, u32[]{:S(2)}, u32[]{:S(2)}) %collective-permute-start.54) | collective-permute-done | bytes 245792 | tf_op jit(solution)/shard_map/ppermute | solution.py:44
  180.9 3.7 %feed_forward.3 = (bf16[40,1536]{1,0:T(8,128)(2,1)S(1)}, bf16[40,1536]{1,0:T(8,128)(2,1)S(1)}, bf16[40,1536]{1,0:T(8,128)(2,1)S(1)}, bf16[40,1536]{1,0:T(8,128)(...) custom-call(s32[4]{0:T(128)S(1)} %copy-done.21, ...), custom_call_target="tpu_custom_call" | custom-call | tf_op jit(solution)/shard_map/feed_forward/pallas_call | solution.py:475
  205.4 6.6 %all-to-all-start = ((bf16[16,8,1792]{2,1,0:T(8,128)(2,1)}), bf16[16,8,1792]{2,1,0:T(8,128)(2,1)S(1)}, u32[]{:S(2)}, u32[]{:S(2)}) async-start(bf16[16,8,1792]{2,1,0:T(8,128)(2,1)} %broadcast_in_dim.28), calls=%async_computation | async-start | bytes 917504 | tf_op jit(solution)/shard_map/all_to_all | solution.py:516
  213.5 7.9 %all-to-all-done.received = bf16[16,8,1792]{2,1,0:T(8,128)(2,1)S(1)} async-done(((bf16[16,8,1792]{2,1,0:T(8,128)(2,1)}), bf16[16,8,1792]{2,1,0:T(8,128)(2,1)S(1)}, u32[]{:S(2)}, u32[]{:S(2)}) %all-to-all-start) | async-done | bytes 458784 | tf_op jit(solution)/shard_map/all_to_all | solution.py:516
  (201 shorter events, 112.8 us)
Async XLA Ops:
  2.5 11.6 %collective-permute-start.12 = (bf16[2,480,128]{2,1,0:T(8,128)(2,1)S(1)}, bf16[2,480,128]{2,1,0:T(8,128)(2,1)}, u32[]{:S(2)}, u32[]{:S(2)}) collective-permute-start(bf16[2,480,128]{2,1,0:T(8,128)(2,1)S(1)} %pack_stale.1.refs_8_), channel_id=1, source_target_pairs={{0,32},{8,40},{16,48},{24,56},{32,0},{40,8},{48,16},{56,24},{1,33}... | collective-permute-start | bytes 737288 | tf_op jit(solution)/shard_map/ppermute | solution.py:53
  5.9 11.8 %collective-permute-start.10 = (bf16[2,480,128]{2,1,0:T(8,128)(2,1)S(1)}, bf16[2,480,128]{2,1,0:T(8,128)(2,1)}, u32[]{:S(2)}, u32[]{:S(2)}) collective-permute-start(bf16[2,480,128]{2,1,0:T(8,128)(2,1)S(1)} %pack_stale.1.refs_8_), channel_id=1, source_target_pairs={{0,48},{8,56},{16,0},{24,8},{32,16},{40,24},{48,32},{56,40},{1,49}... | collective-permute-start | bytes 737288 | tf_op jit(solution)/shard_map/ppermute | solution.py:53
  6.9 11.9 %collective-permute-start.8 = (bf16[2,480,128]{2,1,0:T(8,128)(2,1)S(1)}, bf16[2,480,128]{2,1,0:T(8,128)(2,1)}, u32[]{:S(2)}, u32[]{:S(2)}) collective-permute-start(bf16[2,480,128]{2,1,0:T(8,128)(2,1)S(1)} %pack_stale.1.refs_8_), channel_id=1, source_target_pairs={{0,16},{8,24},{16,32},{24,40},{32,48},{40,56},{48,0},{56,8},{1,17}... | collective-permute-start | bytes 737288 | tf_op jit(solution)/shard_map/ppermute | solution.py:53
  7.9 10.9 %collective-permute-start.7 = (bf16[2,480,128]{2,1,0:T(8,128)(2,1)S(1)}, bf16[2,480,128]{2,1,0:T(8,128)(2,1)}, u32[]{:S(2)}, u32[]{:S(2)}) collective-permute-start(bf16[2,480,128]{2,1,0:T(8,128)(2,1)S(1)} %pack_stale.1.refs_8_), channel_id=1, source_target_pairs={{0,8},{8,0},{16,24},{24,16},{32,40},{40,32},{48,56},{56,48},{1,9},... | collective-permute-start | bytes 737288 | tf_op jit(solution)/shard_map/ppermute | solution.py:57
  13.4 10.6 %collective-permute-start.5 = (bf16[2,480,128]{2,1,0:T(8,128)(2,1)}, bf16[2,480,128]{2,1,0:T(8,128)(2,1)}, u32[]{:S(2)}, u32[]{:S(2)}) collective-permute-start(bf16[2,480,128]{2,1,0:T(8,128)(2,1)} %get-tuple-element.54.refs_0_), channel_id=1, source_target_pairs={{0,32},{8,40},{16,48},{24,56},{32,0},{40,8},{48,16},{56,24},{1,33}... | collective-permute-start | bytes 737288 | tf_op jit(solution)/shard_map/ppermute | solution.py:53
  14.2 14.4 %collective-permute-start.3 = (bf16[2,480,128]{2,1,0:T(8,128)(2,1)}, bf16[2,480,128]{2,1,0:T(8,128)(2,1)}, u32[]{:S(2)}, u32[]{:S(2)}) collective-permute-start(bf16[2,480,128]{2,1,0:T(8,128)(2,1)} %get-tuple-element.54.refs_0_), channel_id=1, source_target_pairs={{0,48},{8,56},{16,0},{24,8},{32,16},{40,24},{48,32},{56,40},{1,49}... | collective-permute-start | bytes 737288 | tf_op jit(solution)/shard_map/ppermute | solution.py:53
  17.7 11.3 %collective-permute-start.1 = (bf16[2,480,128]{2,1,0:T(8,128)(2,1)}, bf16[2,480,128]{2,1,0:T(8,128)(2,1)}, u32[]{:S(2)}, u32[]{:S(2)}) collective-permute-start(bf16[2,480,128]{2,1,0:T(8,128)(2,1)} %get-tuple-element.54.refs_0_), channel_id=1, source_target_pairs={{0,16},{8,24},{16,32},{24,40},{32,48},{40,56},{48,0},{56,8},{1,17}... | collective-permute-start | bytes 737288 | tf_op jit(solution)/shard_map/ppermute | solution.py:53
  18.8 10.2 %collective-permute-start = (bf16[2,480,128]{2,1,0:T(8,128)(2,1)}, bf16[2,480,128]{2,1,0:T(8,128)(2,1)}, u32[]{:S(2)}, u32[]{:S(2)}) collective-permute-start(bf16[2,480,128]{2,1,0:T(8,128)(2,1)} %get-tuple-element.54.refs_0_), channel_id=1, source_target_pairs={{0,8},{8,0},{16,24},{24,16},{32,40},{40,32},{48,56},{56,48},{1,9},... | collective-permute-start | bytes 737288 | tf_op jit(solution)/shard_map/ppermute | solution.py:57
  18.9 10.6 %collective-permute-start.13 = (bf16[2,480,128]{2,1,0:T(8,128)(2,1)}, bf16[2,480,128]{2,1,0:T(8,128)(2,1)}, u32[]{:S(2)}, u32[]{:S(2)}) collective-permute-start(bf16[2,480,128]{2,1,0:T(8,128)(2,1)} %collective-permute-done.12.refs_14_), channel_id=1, source_target_pairs={{0,8},{8,0},{16,24},{24,16},{32,40},{40,32},{48,56},{56,48},{1,9},... | collective-permute-start | bytes 737288 | tf_op jit(solution)/shard_map/ppermute | solution.py:57
  49.5 8.6 %collective-permute-start.15 = (bf16[40,1536]{1,0:T(8,128)(2,1)S(1)}, bf16[40,1536]{1,0:T(8,128)(2,1)S(1)}, u32[]{:S(2)}, u32[]{:S(2)}) collective-permute-start(bf16[40,1536]{1,0:T(8,128)(2,1)S(1)} %get-tuple-element.57), channel_id=1, source_target_pairs={{0,2},{1,3},{2,4},{3,5},{4,6},{5,7},{6,0},{7,1},{8,10},{9,11},{10,... | collective-permute-start | bytes 368648 | tf_op jit(solution)/shard_map/ppermute | solution.py:44
  50.3 8.2 %collective-permute-start.16 = (bf16[40,1536]{1,0:T(8,128)(2,1)S(1)}, bf16[40,1536]{1,0:T(8,128)(2,1)S(1)}, u32[]{:S(2)}, u32[]{:S(2)}) collective-permute-start(bf16[40,1536]{1,0:T(8,128)(2,1)S(1)} %get-tuple-element.58), channel_id=1, source_target_pairs={{0,6},{1,7},{2,0},{3,1},{4,2},{5,3},{6,4},{7,5},{8,14},{9,15},{10,... | collective-permute-start | bytes 368648 | tf_op jit(solution)/shard_map/ppermute | solution.py:44
  67.9 10.9 %collective-permute-start.24 = (bf16[2,40,1536]{2,1,0:T(8,128)(2,1)S(1)}, bf16[2,40,1536]{2,1,0:T(8,128)(2,1)S(1)}, u32[]{:S(2)}, u32[]{:S(2)}) collective-permute-start(bf16[2,40,1536]{2,1,0:T(8,128)(2,1)S(1)} %pad_maximum_fusion.p0), channel_id=1, source_target_pairs={{0,6},{1,7},{2,0},{3,1},{4,2},{5,3},{6,4},{7,5},{8,14},{9,15},{10,... | collective-permute-start | bytes 737288 | tf_op jit(solution)/shard_map/ppermute | solution.py:44
  72.5 10.0 %collective-permute-start.22 = (bf16[2,40,1536]{2,1,0:T(8,128)(2,1)S(1)}, bf16[2,40,1536]{2,1,0:T(8,128)(2,1)S(1)}, u32[]{:S(2)}, u32[]{:S(2)}) collective-permute-start(bf16[2,40,1536]{2,1,0:T(8,128)(2,1)S(1)} %pad_maximum_fusion.p0), channel_id=1, source_target_pairs={{0,2},{1,3},{2,4},{3,5},{4,6},{5,7},{6,0},{7,1},{8,10},{9,11},{10,... | collective-permute-start | bytes 737288 | tf_op jit(solution)/shard_map/ppermute | solution.py:44
  86.7 8.5 %collective-permute-start.29 = (bf16[40,1536]{1,0:T(8,128)(2,1)S(1)}, bf16[40,1536]{1,0:T(8,128)(2,1)S(1)}, u32[]{:S(2)}, u32[]{:S(2)}) collective-permute-start(bf16[40,1536]{1,0:T(8,128)(2,1)S(1)} %get-tuple-element.71), channel_id=1, source_target_pairs={{0,2},{1,3},{2,4},{3,5},{4,6},{5,7},{6,0},{7,1},{8,10},{9,11},{10,... | collective-permute-start | bytes 368648 | tf_op jit(solution)/shard_map/ppermute | solution.py:44
  89.9 8.5 %collective-permute-start.25 = (bf16[40,1536]{1,0:T(8,128)(2,1)S(1)}, bf16[40,1536]{1,0:T(8,128)(2,1)S(1)}, u32[]{:S(2)}, u32[]{:S(2)}) collective-permute-start(bf16[40,1536]{1,0:T(8,128)(2,1)S(1)} %get-tuple-element.66), channel_id=1, source_target_pairs={{0,4},{1,5},{2,6},{3,7},{4,0},{5,1},{6,2},{7,3},{8,12},{9,13},{10,... | collective-permute-start | bytes 368648 | tf_op jit(solution)/shard_map/ppermute | solution.py:44
  110.9 8.6 %collective-permute-start.36 = (bf16[2,40,1536]{2,1,0:T(8,128)(2,1)S(1)}, bf16[2,40,1536]{2,1,0:T(8,128)(2,1)S(1)}, u32[]{:S(2)}, u32[]{:S(2)}) collective-permute-start(bf16[2,40,1536]{2,1,0:T(8,128)(2,1)S(1)} %pad_maximum_fusion.1.p0), channel_id=1, source_target_pairs={{0,6},{1,7},{2,0},{3,1},{4,2},{5,3},{6,4},{7,5},{8,14},{9,15},{10,... | collective-permute-start | bytes 737288 | tf_op jit(solution)/shard_map/ppermute | solution.py:44
  113.2 10.0 %collective-permute-start.34 = (bf16[2,40,1536]{2,1,0:T(8,128)(2,1)S(1)}, bf16[2,40,1536]{2,1,0:T(8,128)(2,1)S(1)}, u32[]{:S(2)}, u32[]{:S(2)}) collective-permute-start(bf16[2,40,1536]{2,1,0:T(8,128)(2,1)S(1)} %pad_maximum_fusion.1.p0), channel_id=1, source_target_pairs={{0,2},{1,3},{2,4},{3,5},{4,6},{5,7},{6,0},{7,1},{8,10},{9,11},{10,... | collective-permute-start | bytes 737288 | tf_op jit(solution)/shard_map/ppermute | solution.py:44
  145.2 10.6 %collective-permute-start.48 = (bf16[40,1536]{1,0:T(8,128)(2,1)S(1)}, bf16[40,1536]{1,0:T(8,128)(2,1)S(1)}, u32[]{:S(2)}, u32[]{:S(2)}) collective-permute-start(bf16[40,1536]{1,0:T(8,128)(2,1)S(1)} %get-tuple-element.82), channel_id=1, source_target_pairs={{0,2},{1,3},{2,4},{3,5},{4,6},{5,7},{6,0},{7,1},{8,10},{9,11},{10,... | collective-permute-start | bytes 368648 | tf_op jit(solution)/shard_map/ppermute | solution.py:44
  146.7 9.1 %collective-permute-start.49 = (bf16[40,1536]{1,0:T(8,128)(2,1)S(1)}, bf16[40,1536]{1,0:T(8,128)(2,1)S(1)}, u32[]{:S(2)}, u32[]{:S(2)}) collective-permute-start(bf16[40,1536]{1,0:T(8,128)(2,1)S(1)} %get-tuple-element.83), channel_id=1, source_target_pairs={{0,6},{1,7},{2,0},{3,1},{4,2},{5,3},{6,4},{7,5},{8,14},{9,15},{10,... | collective-permute-start | bytes 368648 | tf_op jit(solution)/shard_map/ppermute | solution.py:44
  148.4 9.5 %collective-permute-start.44 = (bf16[40,1536]{1,0:T(8,128)(2,1)S(1)}, bf16[40,1536]{1,0:T(8,128)(2,1)S(1)}, u32[]{:S(2)}, u32[]{:S(2)}) collective-permute-start(bf16[40,1536]{1,0:T(8,128)(2,1)S(1)} %get-tuple-element.77), channel_id=1, source_target_pairs={{0,4},{1,5},{2,6},{3,7},{4,0},{5,1},{6,2},{7,3},{8,12},{9,13},{10,... | collective-permute-start | bytes 368648 | tf_op jit(solution)/shard_map/ppermute | solution.py:44
  150.5 9.0 %collective-permute-start.45 = (bf16[40,1536]{1,0:T(8,128)(2,1)S(1)}, bf16[40,1536]{1,0:T(8,128)(2,1)S(1)}, u32[]{:S(2)}, u32[]{:S(2)}) collective-permute-start(bf16[40,1536]{1,0:T(8,128)(2,1)S(1)} %get-tuple-element.78), channel_id=1, source_target_pairs={{0,2},{1,3},{2,4},{3,5},{4,6},{5,7},{6,0},{7,1},{8,10},{9,11},{10,... | collective-permute-start | bytes 368648 | tf_op jit(solution)/shard_map/ppermute | solution.py:44
  170.1 8.3 %collective-permute-start.53 = (bf16[2,40,1536]{2,1,0:T(8,128)(2,1)S(1)}, bf16[2,40,1536]{2,1,0:T(8,128)(2,1)S(1)}, u32[]{:S(2)}, u32[]{:S(2)}) collective-permute-start(bf16[2,40,1536]{2,1,0:T(8,128)(2,1)S(1)} %pad_maximum_fusion.2.p0), channel_id=1, source_target_pairs={{0,4},{1,5},{2,6},{3,7},{4,0},{5,1},{6,2},{7,3},{8,12},{9,13},{10,... | collective-permute-start | bytes 737288 | tf_op jit(solution)/shard_map/ppermute | solution.py:44
  172.0 8.8 %collective-permute-start.52 = (bf16[2,40,1536]{2,1,0:T(8,128)(2,1)S(1)}, bf16[2,40,1536]{2,1,0:T(8,128)(2,1)S(1)}, u32[]{:S(2)}, u32[]{:S(2)}) collective-permute-start(bf16[2,40,1536]{2,1,0:T(8,128)(2,1)S(1)} %pad_maximum_fusion.2.p0), channel_id=1, source_target_pairs={{0,2},{1,3},{2,4},{3,5},{4,6},{5,7},{6,0},{7,1},{8,10},{9,11},{10,... | collective-permute-start | bytes 737288 | tf_op jit(solution)/shard_map/ppermute | solution.py:44
  205.4 16.0 %all-to-all-start = ((bf16[16,8,1792]{2,1,0:T(8,128)(2,1)}), bf16[16,8,1792]{2,1,0:T(8,128)(2,1)S(1)}, u32[]{:S(2)}, u32[]{:S(2)}) async-start(bf16[16,8,1792]{2,1,0:T(8,128)(2,1)} %broadcast_in_dim.28), calls=%async_computation | async-start | bytes 917504 | tf_op jit(solution)/shard_map/all_to_all | solution.py:516
  (73 other events, 1028.7 us)
